TPU v7x, 128 devices: a whole 4x4x4 slice. The times are simulated.
128 devices in a mesh: ifg: 32 (over y, x_lo, z), rows: 4 (over x_hi, core).
Axes of the slice: x: 4 (x_hi: 2, x_lo: 2; x = x_hi * 2 + x_lo), y: 4, z: 4, core: 2. Of those that a mesh axis runs over, the one named last changes fastest.
Arguments:
- phase: float32 [256, 128, 2048], P('ifg', 'rows'), may hold values from -3.1416 to 3.1416, as said below
- weights: int32 [256, 128, 2048], P('ifg', 'rows'), may hold values from 1 to 16
- network: int32 [256, 2], replicated, may hold values from 0 to 95, as said below
Outputs:
- series: float32 [95, 128, 2048], P(None, 'rows', 'ifg')
- filtered: bfloat16 [256, 128, 2048], P(None, 'rows', 'ifg')
Inputs may be any that keep to these rules, and one draw needn't show every extreme that they name: `phase`: values lie in the range of atan2. `network`: row e < 95 joins date e to date e + 1; every row names an earlier date in column 0 and a later date in column 1, at most 24 dates apart, and the span 24 occurs.
All inputs are finite; a program needn't handle non-finite values.
Results may differ from a plain program's by a relative error of at most 0.0018.
Values sent between devices are 32-bit elements; how exact they have to be, the bound alone decides.
A program may use at most 192 MiB of HBM per device.

v0:
```python
import functools

import numpy as np
import jax
import jax.numpy as jnp
from jax import lax
from jax.experimental import pallas as pl
from jax.experimental.pallas import tpu as pltpu
from jax.sharding import PartitionSpec as P

DATES = 96
SWEEPS = 4
HALO = SWEEPS
PI32 = float(np.float32(np.pi))
TWO_PI_HI = float(np.float32(2 * np.pi))
TWO_PI_LO = float(np.float32(2 * np.pi - np.float64(np.float32(2 * np.pi))))


def extended_2(block, sides, width):
    for axis, dim in sides:
        count = lax.axis_size(axis)
        forward = [(i, i + 1) for i in range(count - 1)]
        backward = [(target, source) for source, target in forward]
        low = lax.ppermute(
            lax.slice_in_dim(block, block.shape[dim] - width, None, axis=dim), axis, forward
        )
        high = lax.ppermute(lax.slice_in_dim(block, 0, width, axis=dim), axis, backward)
        block = jnp.concatenate([low, block, high], axis=dim)
    return block


def wrapped_diff(delta):
    above = (delta - TWO_PI_HI) - TWO_PI_LO
    below = (delta + TWO_PI_HI) + TWO_PI_LO
    return jnp.where(delta >= PI32, above, jnp.where(delta <= -PI32, below, delta))


def unwrap_kernel(rows_out, p_ref, q_ref, o_ref, cur_ref):
    p = p_ref[0]
    q = q_ref[0]
    nr, nc = p.shape
    row = lax.broadcasted_iota(jnp.int32, (nr, nc), 0)
    col = lax.broadcasted_iota(jnp.int32, (nr, nc), 1)
    zero = jnp.zeros((nr, nc), jnp.float32)
    p_dn = pltpu.roll(p, nr - 1, 0)
    q_dn = pltpu.roll(q, nr - 1, 0)
    g_dn = wrapped_diff(p_dn - p)
    w_dn = jnp.where(row < nr - 1, q_dn * q, zero)
    p_rt = pltpu.roll(p, nc - 1, 1)
    q_rt = pltpu.roll(q, nc - 1, 1)
    g_rt = wrapped_diff(p_rt - p)
    w_rt = jnp.where(col < nc - 1, q_rt * q, zero)
    g_up = pltpu.roll(g_dn, 1, 0)
    w_up = pltpu.roll(w_dn, 1, 0)
    g_lt = pltpu.roll(g_rt, 1, 1)
    w_lt = pltpu.roll(w_rt, 1, 1)
    den = ((w_up + w_dn) + w_lt) + w_rt
    den = jnp.where(den > 0.0, den, 1.0)
    cur = zero
    for _ in range(SWEEPS):
        c_up = pltpu.roll(cur, 1, 0)
        c_dn = pltpu.roll(cur, nr - 1, 0)
        c_lt = pltpu.roll(cur, 1, 1)
        c_rt = pltpu.roll(cur, nc - 1, 1)
        num = w_up * (c_up + g_up)
        num = num + w_dn * (c_dn - g_dn)
        num = num + w_lt * (c_lt + g_lt)
        num = num + w_rt * (c_rt - g_rt)
        cur = num / den
    cur_ref[...] = cur
    o_ref[0] = cur_ref[pl.ds(HALO, rows_out), :]


def unwrap(phase_ext, quality_ext, rows_out):
    n, nr, nc = phase_ext.shape
    return pl.pallas_call(
        functools.partial(unwrap_kernel, rows_out),
        grid=(n,),
        in_specs=[
            pl.BlockSpec((1, nr, nc), lambda i: (i, 0, 0)),
            pl.BlockSpec((1, nr, nc), lambda i: (i, 0, 0)),
        ],
        out_specs=pl.BlockSpec((1, rows_out, nc), lambda i: (i, 0, 0)),
        out_shape=jax.ShapeDtypeStruct((n, rows_out, nc), jnp.float32),
        scratch_shapes=[pltpu.VMEM((nr, nc), jnp.float32)],
        cost_estimate=pl.CostEstimate(
            flops=120 * n * nr * nc, bytes_accessed=4 * n * nc * (2 * nr + rows_out), transcendentals=0
        ),
    )(phase_ext, quality_ext)


def binomial(padded, axis):
    length = padded.shape[axis] - 4

    def shifted(offset):
        return lax.slice_in_dim(padded, offset, offset + length, axis=axis)

    return (
        shifted(0) + 4.0 * shifted(1) + 6.0 * shifted(2) + 4.0 * shifted(3) + shifted(4)
    ) * 0.0625


def network_maps(network):
    date_ids = jnp.arange(DATES, dtype=jnp.int32)[None, :]
    full = (network[:, 1:2] == date_ids).astype(jnp.float32) - (network[:, 0:1] == date_ids).astype(
        jnp.float32
    )
    design = full[:, 1:]
    normal_matrix = jnp.dot(design.T, design, precision=lax.Precision.HIGHEST)
    factor = jnp.linalg.cholesky(normal_matrix)
    pseudo = jax.scipy.linalg.cho_solve((factor, True), design.T)
    return (design, pseudo)


def on_device(phase, weights, network):
    design, pseudo = network_maps(network)
    stacked = jnp.stack([phase, weights.astype(jnp.float32)])
    extended = extended_2(stacked, (("rows", 2),), HALO)
    current = unwrap(extended[0], extended[1], phase.shape[1])
    block = lax.all_to_all(current, "ifg", split_axis=2, concat_axis=0, tiled=True)
    series_block = jnp.einsum("ei,irc->erc", pseudo, block, precision=lax.Precision.HIGHEST)
    residual = block - jnp.einsum(
        "ie,erc->irc", design, series_block, precision=lax.Precision.HIGHEST
    )
    padded = extended_2(residual, (("rows", 1), ("ifg", 2)), 2)
    filtered = binomial(binomial(padded, 1), 2)
    return (series_block, filtered.astype(jnp.bfloat16))


def solution(mesh):
    return jax.shard_map(
        on_device,
        mesh=mesh,
        in_specs=(P("ifg", "rows", None), P("ifg", "rows", None), P()),
        out_specs=(P(None, "rows", "ifg"), P(None, "rows", "ifg")),
        check_vma=False,
    )
```

profile of v0, /device:TPU:9, one launch (start us, length us, event | category | flops | bytes accessed | tf_op | source)
XLA Modules:
  0.0 132.4 jit_solution(17067851785536970901)
XLA Ops:
  0.6 1.9 %convert_bitcast_fusion = f32[1,8,32,2048]{3,2,1,0:T(8,128)S(1)} fusion(s32[8,32,2048]{2,1,0:T(8,128)} %param.4), kind=kLoop, calls=%fused_computation.21 | loop fusion | flops 524288 | bytes 4194304 | tf_op jit(solution)/shard_map/stack | solution.py:117
  3.1 5.2 %collective-permute-start = (f32[2,8,4,2048]{3,2,1,0:T(4,128)S(1)}, f32[2,8,4,2048]{3,2,1,0:T(4,128)S(1)}, u32[]{:S(2)}, u32[]{:S(2)}) collective-permute-start(f32[2,8,4,2048]{3,2,1,0:T(4,128)S(1)} %get-tuple-element.4), channel_id=1, source_target_pairs={{0,1},{1,2},{2,3},{4,5},{5,6},{6,7},{8,9},{9,10},{10,11},{12,13},{... | collective-permute-start | bytes 1572872 | tf_op jit(solution)/shard_map/ppermute | solution.py:24
  8.3 1.9 %collective-permute-start.1 = (f32[2,8,4,2048]{3,2,1,0:T(4,128)S(1)}, f32[2,8,4,2048]{3,2,1,0:T(4,128)S(1)}, u32[]{:S(2)}, u32[]{:S(2)}) collective-permute-start(f32[2,8,4,2048]{3,2,1,0:T(4,128)S(1)} %get-tuple-element.5), channel_id=1, source_target_pairs={{1,0},{2,1},{3,2},{5,4},{6,5},{7,6},{9,8},{10,9},{11,10},{13,12},{... | collective-permute-start | bytes 1572872 | tf_op jit(solution)/shard_map/ppermute | solution.py:27
  10.3 4.2 %collective-permute-done = f32[2,8,4,2048]{3,2,1,0:T(4,128)S(1)} collective-permute-done((f32[2,8,4,2048]{3,2,1,0:T(4,128)S(1)}, f32[2,8,4,2048]{3,2,1,0:T(4,128)S(1)}, u32[]{:S(2)}, u32[]{:S(2)}) %collective-permute-start) | collective-permute-done | bytes 524320 | tf_op jit(solution)/shard_map/ppermute | solution.py:24
  14.4 5.9 %collective-permute-done.1 = f32[2,8,4,2048]{3,2,1,0:T(4,128)S(1)} collective-permute-done((f32[2,8,4,2048]{3,2,1,0:T(4,128)S(1)}, f32[2,8,4,2048]{3,2,1,0:T(4,128)S(1)}, u32[]{:S(2)}, u32[]{:S(2)}) %collective-permute-start.1) | collective-permute-done | bytes 524320 | tf_op jit(solution)/shard_map/ppermute | solution.py:27
  20.3 1.1 pad_maximum_fusion
  21.5 2.6 %slice_bitcast_fusion = (f32[8,40,2048]{2,1,0:T(8,128)}, f32[8,40,2048]{2,1,0:T(8,128)}) fusion(f32[2,8,40,2048]{3,2,1,0:T(8,128)S(1)} %pad_maximum_fusion), kind=kLoop, calls=%fused_computation.2 | loop fusion | bytes 10485760 | tf_op jit(solution)/shard_map/squeeze | solution.py:119
  24.1 12.8 %shard_map.50 = f32[8,32,2048]{2,1,0:T(8,128)} custom-call(f32[8,40,2048]{2,1,0:T(8,128)} %get-tuple-element.3.p_ref, f32[8,40,2048]{2,1,0:T(8,128)} %get-tuple-element.2.q_ref), custom_call_target="tpu_custom_call" | custom-call | flops 78643200 | bytes 7340032 | tf_op jit(solution)/shard_map/pallas_call | solution.py:76
  36.9 6.3 %copy.12 = f32[8,32,2048]{1,0,2:T(8,128)} copy(f32[8,32,2048]{2,1,0:T(8,128)} %shard_map.50) | data formatting | bytes 4194304 | tf_op jit(solution)/shard_map/pallas_call | solution.py:76
  43.2 7.7 %reshape.21 = f32[32,1,16384]{2,1,0:T(1,128)} reshape(f32[2048,8,32]{2,1,0:T(8,128)} %bitcast.36) | data formatting | bytes 4194304
  51.0 8.2 %all-to-all-start = ((f32[32,1,16384]{2,1,0:T(1,128)}), f32[32,1,16384]{2,1,0:T(1,128)S(1)}, u32[]{:S(2)}, u32[]{:S(2)}) async-start(f32[32,1,16384]{2,1,0:T(1,128)} %reshape.21), calls=%async_computation | async-start | bytes 4194304 | tf_op jit(solution)/shard_map/all_to_all | solution.py:120
  59.6 8.7 %cholesky.16 = f32[95,95]{1,0:T(8,128)S(1)} custom-call(f32[95,95]{1,0:T(8,128)S(1)} %fusion.34), custom_call_target="Cholesky" | custom-call | tf_op jit(solution)/shard_map/jit(cholesky)/cholesky | solution.py:110
  68.3 0.6 compare_reduce_fusion
  68.9 0.7 fusion.21
  69.6 7.3 %custom-call.10 = f32[1,95,95]{1,2,0:T(8,128)S(1)} custom-call(f32[1,95,95]{2,1,0:T(8,128)S(1)} %fusion.21), custom_call_target="InvertDiagBlocksLowerTriangular" | custom-call | tf_op jit(solution)/shard_map/jit(_cho_solve)/triangular_solve | solution.py:111
  77.4 1.9 %all-to-all-done = f32[32,1,16384]{2,1,0:T(1,128)S(1)} async-done(((f32[32,1,16384]{2,1,0:T(1,128)}), f32[32,1,16384]{2,1,0:T(1,128)S(1)}, u32[]{:S(2)}, u32[]{:S(2)}) %all-to-all-start) | async-done | bytes 2097184 | tf_op jit(solution)/shard_map/all_to_all | solution.py:120
  79.3 1.3 %copy-done.1 = f32[32,1,16384]{2,1,0:T(1,128)} copy-done((f32[32,1,16384]{2,1,0:T(1,128)}, f32[32,1,16384]{2,1,0:T(1,128)S(1)}, u32[]{:S(2)}) %copy-start.1) | copy-done | bytes 2097176
  80.7 0.5 broadcast.95
  81.2 7.4 %reduce.6 = f32[32,16384]{1,0:T(8,128)S(1)} reduce(f32[32,1,16384]{2,1,0:T(1,128)} %copy-done.1, f32[]{:T(128)} %broadcast.95), dimensions={1}, to_apply=%all_to_all.13.reduce_sub_computation | reduce | bytes 4194308 | tf_op jit(solution)/shard_map/all_to_all | solution.py:120
  88.6 4.8 %reshape.22 = f32[2048,8,32]{2,1,0:T(8,128)} reshape(f32[32,16384]{1,0:T(8,128)S(1)} %reduce.6) | data formatting | bytes 4194304
  93.4 6.8 %copy.13 = f32[8,32,32,64]{3,1,0,2:T(8,128)} copy(f32[8,32,32,64]{1,0,3,2:T(8,128)} %bitcast.37) | data formatting | bytes 4194304 | tf_op jit(solution)/shard_map/all_to_all | solution.py:120
  100.2 3.8 %copy.14 = f32[256,32,64]{0,2,1:T(8,128)S(1)} copy(f32[256,32,64]{2,1,0:T(8,128)} %bitcast.39) | data formatting | bytes 4194304 | tf_op jit(solution)/shard_map/all_to_all | solution.py:120
  104.0 1.9 %fusion.40 = f32[95,2048]{0,1:S(1)} fusion(f32[95,256]{1,0:T(8,128)S(1)} %fusion.31, f32[256,2048]{0,1:T(8,128)S(1)} %bitcast.38), kind=kOutput, calls=%fused_computation.60 | convolution fusion | flops 597688320 | bytes 2972672
  105.8 1.8 %fusion.9 = f32[256,2048]{0,1:S(1)} fusion(f32[95,2048]{0,1:S(1)} %fusion.40, s32[256]{0:T(256)S(1)} %bitcast.49, s32[256]{0:T(256)S(1)} %bitcast.46), kind=kOutput, calls=%fused_computation.22 | convolution fusion | flops 597834240 | bytes 2877440
  108.1 3.8 %collective-permute-start.2 = (f32[256,2,64]{0,2,1:T(8,128)S(1)}, f32[256,2,64]{0,2,1:T(8,128)S(1)}, u32[]{:S(2)}, u32[]{:S(2)}) collective-permute-start(f32[256,2,64]{0,2,1:T(8,128)S(1)} %get-tuple-element.8), channel_id=1, source_target_pairs={{0,1},{1,2},{2,3},{4,5},{5,6},{6,7},{8,9},{9,10},{10,11},{12,13},{... | collective-permute-start | bytes 393224 | tf_op jit(solution)/shard_map/ppermute | solution.py:24
  111.9 1.9 %collective-permute-start.3 = (f32[256,2,64]{0,2,1:T(8,128)S(1)}, f32[256,2,64]{0,2,1:T(8,128)S(1)}, u32[]{:S(2)}, u32[]{:S(2)}) collective-permute-start(f32[256,2,64]{0,2,1:T(8,128)S(1)} %get-tuple-element.9), channel_id=1, source_target_pairs={{1,0},{2,1},{3,2},{5,4},{6,5},{7,6},{9,8},{10,9},{11,10},{13,12},{... | collective-permute-start | bytes 393224 | tf_op jit(solution)/shard_map/ppermute | solution.py:27
  113.8 5.9 %collective-permute-done.3 = f32[256,2,64]{0,2,1:T(8,128)S(1)} collective-permute-done((f32[256,2,64]{0,2,1:T(8,128)S(1)}, f32[256,2,64]{0,2,1:T(8,128)S(1)}, u32[]{:S(2)}, u32[]{:S(2)}) %collective-permute-start.3) | collective-permute-done | bytes 131104 | tf_op jit(solution)/shard_map/ppermute | solution.py:27
  119.7 2.4 %collective-permute-start.4 = (f32[256,36,2]{0,2,1:T(2,128)S(1)}, f32[256,36,2]{0,2,1:T(2,128)S(1)}, u32[]{:S(2)}, u32[]{:S(2)}) collective-permute-start(f32[256,36,2]{0,2,1:T(2,128)S(1)} %get-tuple-element.6), channel_id=1, source_target_pairs={{0,4},{4,8},{8,12},{12,16},{16,20},{20,24},{24,28},{28,32},{32,36}... | collective-permute-start | bytes 221192 | tf_op jit(solution)/shard_map/ppermute | solution.py:24
  122.1 5.9 %collective-permute-start.5 = (f32[256,36,2]{0,2,1:T(2,128)S(1)}, f32[256,36,2]{0,2,1:T(2,128)S(1)}, u32[]{:S(2)}, u32[]{:S(2)}) collective-permute-start(f32[256,36,2]{0,2,1:T(2,128)S(1)} %get-tuple-element.7), channel_id=1, source_target_pairs={{4,0},{8,4},{12,8},{16,12},{20,16},{24,20},{28,24},{32,28},{36,32}... | collective-permute-start | bytes 221192 | tf_op jit(solution)/shard_map/ppermute | solution.py:27
  128.1 1.4 %collective-permute-done.5 = f32[256,36,2]{0,2,1:T(2,128)S(1)} collective-permute-done((f32[256,36,2]{0,2,1:T(2,128)S(1)}, f32[256,36,2]{0,2,1:T(2,128)S(1)}, u32[]{:S(2)}, u32[]{:S(2)}) %collective-permute-start.5) | collective-permute-done | bytes 73760 | tf_op jit(solution)/shard_map/ppermute | solution.py:27
  129.7 0.5 fusion
  130.3 2.1 %fusion.5 = bf16[256,32,64]{0,2,1:T(8,128)(2,1)} fusion(f32[256,32,68]{0,2,1:T(8,128)S(1)} %fusion), kind=kLoop, calls=%fused_computation.14 | loop fusion | flops 4718592 | bytes 11534336 | tf_op jit(solution)/shard_map/convert_element_type | solution.py:127
  (21 shorter events, 2.2 us)
Async XLA Ops:
  0.6 2.2 %copy-start = (f32[8,32,2048]{2,1,0:T(8,128)S(1)}, f32[8,32,2048]{2,1,0:T(8,128)}, u32[]{:S(2)}) copy-start(f32[8,32,2048]{2,1,0:T(8,128)} %param.3) | copy-start | bytes 6291460
  3.1 11.3 %collective-permute-start = (f32[2,8,4,2048]{3,2,1,0:T(4,128)S(1)}, f32[2,8,4,2048]{3,2,1,0:T(4,128)S(1)}, u32[]{:S(2)}, u32[]{:S(2)}) collective-permute-start(f32[2,8,4,2048]{3,2,1,0:T(4,128)S(1)} %get-tuple-element.4), channel_id=1, source_target_pairs={{0,1},{1,2},{2,3},{4,5},{5,6},{6,7},{8,9},{9,10},{10,11},{12,13},{... | collective-permute-start | bytes 1572872 | tf_op jit(solution)/shard_map/ppermute | solution.py:24
  8.3 12.0 %collective-permute-start.1 = (f32[2,8,4,2048]{3,2,1,0:T(4,128)S(1)}, f32[2,8,4,2048]{3,2,1,0:T(4,128)S(1)}, u32[]{:S(2)}, u32[]{:S(2)}) collective-permute-start(f32[2,8,4,2048]{3,2,1,0:T(4,128)S(1)} %get-tuple-element.5), channel_id=1, source_target_pairs={{1,0},{2,1},{3,2},{5,4},{6,5},{7,6},{9,8},{10,9},{11,10},{13,12},{... | collective-permute-start | bytes 1572872 | tf_op jit(solution)/shard_map/ppermute | solution.py:27
  51.0 8.2 %copy-start.3 = (s32[256,2]{0,1:T(2,128)S(1)}, s32[256,2]{0,1:T(2,128)}, u32[]{:S(2)}) copy-start(s32[256,2]{0,1:T(2,128)} %param.5) | copy-start | bytes 6148
  51.0 28.3 %all-to-all-start = ((f32[32,1,16384]{2,1,0:T(1,128)}), f32[32,1,16384]{2,1,0:T(1,128)S(1)}, u32[]{:S(2)}, u32[]{:S(2)}) async-start(f32[32,1,16384]{2,1,0:T(1,128)} %reshape.21), calls=%async_computation | async-start | bytes 4194304 | tf_op jit(solution)/shard_map/all_to_all | solution.py:120
  79.3 1.3 %copy-start.1 = (f32[32,1,16384]{2,1,0:T(1,128)}, f32[32,1,16384]{2,1,0:T(1,128)S(1)}, u32[]{:S(2)}) copy-start(f32[32,1,16384]{2,1,0:T(1,128)S(1)} %all-to-all-done) | copy-start | bytes 6291460
  105.8 2.2 %copy-start.2 = (f32[95,2048]{0,1}, f32[95,2048]{0,1:S(1)}, u32[]{:S(2)}) copy-start(f32[95,2048]{0,1:S(1)} %fusion.40) | copy-start | bytes 2334724
  108.1 5.7 %collective-permute-start.2 = (f32[256,2,64]{0,2,1:T(8,128)S(1)}, f32[256,2,64]{0,2,1:T(8,128)S(1)}, u32[]{:S(2)}, u32[]{:S(2)}) collective-permute-start(f32[256,2,64]{0,2,1:T(8,128)S(1)} %get-tuple-element.8), channel_id=1, source_target_pairs={{0,1},{1,2},{2,3},{4,5},{5,6},{6,7},{8,9},{9,10},{10,11},{12,13},{... | collective-permute-start | bytes 393224 | tf_op jit(solution)/shard_map/ppermute | solution.py:24
  111.9 7.8 %collective-permute-start.3 = (f32[256,2,64]{0,2,1:T(8,128)S(1)}, f32[256,2,64]{0,2,1:T(8,128)S(1)}, u32[]{:S(2)}, u32[]{:S(2)}) collective-permute-start(f32[256,2,64]{0,2,1:T(8,128)S(1)} %get-tuple-element.9), channel_id=1, source_target_pairs={{1,0},{2,1},{3,2},{5,4},{6,5},{7,6},{9,8},{10,9},{11,10},{13,12},{... | collective-permute-start | bytes 393224 | tf_op jit(solution)/shard_map/ppermute | solution.py:27
  119.7 8.3 %collective-permute-start.4 = (f32[256,36,2]{0,2,1:T(2,128)S(1)}, f32[256,36,2]{0,2,1:T(2,128)S(1)}, u32[]{:S(2)}, u32[]{:S(2)}) collective-permute-start(f32[256,36,2]{0,2,1:T(2,128)S(1)} %get-tuple-element.6), channel_id=1, source_target_pairs={{0,4},{4,8},{8,12},{12,16},{16,20},{20,24},{24,28},{28,32},{32,36}... | collective-permute-start | bytes 221192 | tf_op jit(solution)/shard_map/ppermute | solution.py:24
  122.1 7.3 %collective-permute-start.5 = (f32[256,36,2]{0,2,1:T(2,128)S(1)}, f32[256,36,2]{0,2,1:T(2,128)S(1)}, u32[]{:S(2)}, u32[]{:S(2)}) collective-permute-start(f32[256,36,2]{0,2,1:T(2,128)S(1)} %get-tuple-element.7), channel_id=1, source_target_pairs={{4,0},{8,4},{12,8},{16,12},{20,16},{24,20},{28,24},{32,28},{36,32}... | collective-permute-start | bytes 221192 | tf_op jit(solution)/shard_map/ppermute | solution.py:27
where the time goes:
time: 133 us; the launch traced here: 132 us
  local copies, waits for them, and re-layouts  34.4 us (26%)
  other arithmetic  31.3 us (24%)
  starting transfers between devices  29.3 us (22%)
  waiting for transfers between devices  19.2 us (14%)
  Pallas kernels  12.8 us (10%)
  matrix products  4.47 us (3%)
    unnamed x10, local copies, waits for them, and re-layouts  14.2 us
    ppermute x3, waiting for transfers between devices, extended_2(): lax.ppermute(lax.slice_in_dim(block, 0, width, axis=dim), axis, backward)  13.1 us
    pallas_call x1, Pallas kernels, unwrap(): pl.pallas_call(functools.partial(unwrap_kernel, rows_out), grid=(n,), in_...  12.8 us
    ppermute x3, starting transfers between devices, extended_2(): lax.ppermute(lax.slice_in_dim(block, block.shape[dim] - width, None, axis...  11.4 us
    all_to_all x3, local copies, waits for them, and re-layouts, on_device(): lax.all_to_all(current, 'ifg', split_axis=2, concat_axis=0, tiled=True)  11.1 us
    ppermute x3, starting transfers between devices, extended_2(): lax.ppermute(lax.slice_in_dim(block, 0, width, axis=dim), axis, backward)  9.73 us
    another operation x3, other arithmetic, network_maps(): factor = jnp.linalg.cholesky(normal_matrix)  9.36 us
    all_to_all x1, starting transfers between devices, on_device(): lax.all_to_all(current, 'ifg', split_axis=2, concat_axis=0, tiled=True)  8.16 us
  transfers between devices with their start and end apart: 7, of which 5 were waited for; matrix products, arithmetic and copies ran while one was open for 14% of the time, Pallas kernels for 0%

commit v1 on v0

--- a/solution.py
+++ b/solution.py
@@ -68,7 +68,16 @@
         num = num + w_rt * (c_rt - g_rt)
         cur = num / den
     cur_ref[...] = cur
-    o_ref[0] = cur_ref[pl.ds(HALO, rows_out), :]
+    half = rows_out // 2
+    upper = cur_ref[pl.ds(HALO, half), :]
+    lower = cur_ref[pl.ds(HALO + half, half), :]
+    lane = lax.broadcasted_iota(jnp.int32, (half, nc), 1) % 128
+    first = lane < 64
+    even = jnp.where(first, upper, pltpu.roll(lower, 64, 1))
+    odd = jnp.where(first, pltpu.roll(upper, nc - 64, 1), lower)
+    for m in range(nc // 128):
+        o_ref[2 * m, 0] = even[:, 128 * m : 128 * (m + 1)]
+        o_ref[2 * m + 1, 0] = odd[:, 128 * m : 128 * (m + 1)]
 
 
 def unwrap(phase_ext, quality_ext, rows_out):
@@ -80,8 +89,8 @@
             pl.BlockSpec((1, nr, nc), lambda i: (i, 0, 0)),
             pl.BlockSpec((1, nr, nc), lambda i: (i, 0, 0)),
         ],
-        out_specs=pl.BlockSpec((1, rows_out, nc), lambda i: (i, 0, 0)),
-        out_shape=jax.ShapeDtypeStruct((n, rows_out, nc), jnp.float32),
+        out_specs=pl.BlockSpec((nc // 64, 1, rows_out // 2, 128), lambda i: (0, i, 0, 0)),
+        out_shape=jax.ShapeDtypeStruct((nc // 64, n, rows_out // 2, 128), jnp.float32),
         scratch_shapes=[pltpu.VMEM((nr, nc), jnp.float32)],
         cost_estimate=pl.CostEstimate(
             flops=120 * n * nr * nc, bytes_accessed=4 * n * nc * (2 * nr + rows_out), transcendentals=0
@@ -116,8 +125,11 @@
     design, pseudo = network_maps(network)
     stacked = jnp.stack([phase, weights.astype(jnp.float32)])
     extended = extended_2(stacked, (("rows", 2),), HALO)
-    current = unwrap(extended[0], extended[1], phase.shape[1])
-    block = lax.all_to_all(current, "ifg", split_axis=2, concat_axis=0, tiled=True)
+    rows = phase.shape[1]
+    current = unwrap(extended[0], extended[1], rows)
+    received = lax.all_to_all(current, "ifg", split_axis=0, concat_axis=0, tiled=True)
+    ifg = received.shape[0] * received.shape[1]
+    block = received.reshape(ifg, rows // 2, 2, 64).transpose(0, 2, 1, 3).reshape(ifg, rows, 64)
     series_block = jnp.einsum("ei,irc->erc", pseudo, block, precision=lax.Precision.HIGHEST)
     residual = block - jnp.einsum(
         "ie,erc->irc", design, series_block, precision=lax.Precision.HIGHEST

time: 133 us -> 105 us (0.79)
  local copies, waits for them, and re-layouts: 34.4 us -> 12.1 us
  other arithmetic: 31.3 us -> 24 us
    unnamed x10 -> x6, local copies, waits for them, and re-layouts: 14.2 us -> 0.33 us
    all_to_all x3 -> x0, local copies, waits for them, and re-layouts: 11.1 us -> none  [on_device(): lax.all_to_all(current, 'ifg', split_axis=2, concat_axis=0, tiled=True)]
    all_to_all x1 -> x0, other arithmetic: 7.39 us -> none  [on_device(): lax.all_to_all(current, 'ifg', split_axis=2, concat_axis=0, tiled=True)]
    pallas_call x1 -> x0, local copies, waits for them, and re-layouts: 6.33 us -> none  [unwrap(): pl.pallas_call(functools.partial(unwrap_kernel, rows_out), grid=(n,), in_...]
    transpose x0 -> x1, local copies, waits for them, and re-layouts: none -> 5.38 us  [on_device(): received.reshape(ifg, rows // 2, 2, 64).transpose(0, 2, 1, 3)]
    reshape x0 -> x1, local copies, waits for them, and re-layouts: none -> 3.67 us  [on_device(): received.reshape(ifg, rows // 2, 2, 64).transpose(0, 2, 1, 3)]
  transfers between devices with their start and end apart: 7 -> 7, of which waited for: 5 -> 5; matrix products, arithmetic and copies ran while one was open for 14% -> 18% of each run, Pallas kernels for 0% -> 0%
where the time goes in v1:
time: 105 us; the launch traced here: 104 us
  starting transfers between devices  29.3 us (28%)
  other arithmetic  24 us (23%)
  waiting for transfers between devices  19.2 us (18%)
  Pallas kernels  13.6 us (13%)
  local copies, waits for them, and re-layouts  12.1 us (12%)
  matrix products  4.46 us (4%)
    pallas_call x1, Pallas kernels, unwrap(): pl.pallas_call(functools.partial(unwrap_kernel, rows_out), grid=(n,), in_...  13.6 us
    ppermute x3, waiting for transfers between devices, extended_2(): lax.ppermute(lax.slice_in_dim(block, 0, width, axis=dim), axis, backward)  13.1 us
    ppermute x3, starting transfers between devices, extended_2(): lax.ppermute(lax.slice_in_dim(block, block.shape[dim] - width, None, axis...  11.4 us
    ppermute x3, starting transfers between devices, extended_2(): lax.ppermute(lax.slice_in_dim(block, 0, width, axis=dim), axis, backward)  9.73 us
    another operation x3, other arithmetic, network_maps(): factor = jnp.linalg.cholesky(normal_matrix)  9.36 us
    all_to_all x1, starting transfers between devices, on_device(): lax.all_to_all(current, 'ifg', split_axis=0, concat_axis=0, tiled=True)  8.16 us
    another operation x2, other arithmetic, network_maps(): pseudo = jax.scipy.linalg.cho_solve((factor, True), design.T)  7.94 us
    transpose x1, local copies, waits for them, and re-layouts, on_device(): received.reshape(ifg, rows // 2, 2, 64).transpose(0, 2, 1, 3)  5.38 us
  transfers between devices with their start and end apart: 7, of which 5 were waited for; matrix products, arithmetic and copies ran while one was open for 18% of the time, Pallas kernels for 0%

profile of v1, /device:TPU:9, one launch (start us, length us, event | category | flops | bytes accessed | tf_op | source)
XLA Modules:
  0.0 103.7 jit_solution(10649313937523637371)
XLA Ops:
  0.6 1.9 %convert_bitcast_fusion = f32[1,8,32,2048]{3,2,1,0:T(8,128)S(1)} fusion(s32[8,32,2048]{2,1,0:T(8,128)} %param.4), kind=kLoop, calls=%fused_computation.22 | loop fusion | flops 524288 | bytes 4194304 | tf_op jit(solution)/shard_map/stack | solution.py:126
  2.5 0.3 copy-done
  2.9 0.2 pad_maximum_fusion.3
  3.1 5.2 %collective-permute-start = (f32[2,8,4,2048]{3,2,1,0:T(4,128)S(1)}, f32[2,8,4,2048]{3,2,1,0:T(4,128)S(1)}, u32[]{:S(2)}, u32[]{:S(2)}) collective-permute-start(f32[2,8,4,2048]{3,2,1,0:T(4,128)S(1)} %get-tuple-element.4), channel_id=1, source_target_pairs={{0,1},{1,2},{2,3},{4,5},{5,6},{6,7},{8,9},{9,10},{10,11},{12,13},{... | collective-permute-start | bytes 1572872 | tf_op jit(solution)/shard_map/ppermute | solution.py:24
  8.3 1.9 %collective-permute-start.1 = (f32[2,8,4,2048]{3,2,1,0:T(4,128)S(1)}, f32[2,8,4,2048]{3,2,1,0:T(4,128)S(1)}, u32[]{:S(2)}, u32[]{:S(2)}) collective-permute-start(f32[2,8,4,2048]{3,2,1,0:T(4,128)S(1)} %get-tuple-element.5), channel_id=1, source_target_pairs={{1,0},{2,1},{3,2},{5,4},{6,5},{7,6},{9,8},{10,9},{11,10},{13,12},{... | collective-permute-start | bytes 1572872 | tf_op jit(solution)/shard_map/ppermute | solution.py:27
  10.3 4.2 %collective-permute-done = f32[2,8,4,2048]{3,2,1,0:T(4,128)S(1)} collective-permute-done((f32[2,8,4,2048]{3,2,1,0:T(4,128)S(1)}, f32[2,8,4,2048]{3,2,1,0:T(4,128)S(1)}, u32[]{:S(2)}, u32[]{:S(2)}) %collective-permute-start) | collective-permute-done | bytes 524320 | tf_op jit(solution)/shard_map/ppermute | solution.py:24
  14.4 5.9 %collective-permute-done.1 = f32[2,8,4,2048]{3,2,1,0:T(4,128)S(1)} collective-permute-done((f32[2,8,4,2048]{3,2,1,0:T(4,128)S(1)}, f32[2,8,4,2048]{3,2,1,0:T(4,128)S(1)}, u32[]{:S(2)}, u32[]{:S(2)}) %collective-permute-start.1) | collective-permute-done | bytes 524320 | tf_op jit(solution)/shard_map/ppermute | solution.py:27
  20.3 1.1 %pad_maximum_fusion = f32[2,8,40,2048]{3,2,1,0:T(8,128)S(1)} fusion(f32[2,8,4,2048]{3,2,1,0:T(4,128)S(1)} %collective-permute-done.1, f32[1,8,32,2048]{3,2,1,0:T(8,128)S(1)} %convert_bitcast_fusion, f32[1,8,32,2048]{3,2,1,0:T(8,128)S(1)} %bitcast.39, f32[2,8,4,2048]{3,2,1,0:T(4,128)S(1)} %collective-permute-done), kind=kLoop, calls=%fused_computation | loop fusion | flops 3932160 | bytes 10485760 | tf_op jit(solution)/shard_map/concatenate | solution.py:28
  21.5 2.6 %slice_bitcast_fusion = (f32[8,40,2048]{2,1,0:T(8,128)}, f32[8,40,2048]{2,1,0:T(8,128)}) fusion(f32[2,8,40,2048]{3,2,1,0:T(8,128)S(1)} %pad_maximum_fusion), kind=kLoop, calls=%fused_computation.2 | loop fusion | bytes 10485760 | tf_op jit(solution)/shard_map/squeeze | solution.py:129
  24.1 13.6 %shard_map.50 = f32[32,8,16,128]{3,2,1,0:T(8,128)} custom-call(f32[8,40,2048]{2,1,0:T(8,128)} %get-tuple-element.3.p_ref, f32[8,40,2048]{2,1,0:T(8,128)} %get-tuple-element.2.q_ref), custom_call_target="tpu_custom_call" | custom-call | flops 78643200 | bytes 7340032 | tf_op jit(solution)/shard_map/pallas_call | solution.py:85
  37.8 8.2 %all-to-all-start = ((f32[32,8,16,128]{3,2,1,0:T(8,128)}), f32[32,8,16,128]{3,2,1,0:T(8,128)S(1)}, u32[]{:S(2)}, u32[]{:S(2)}) async-start(f32[32,8,16,128]{3,2,1,0:T(8,128)} %shard_map.50), calls=%async_computation | async-start | bytes 4194304 | tf_op jit(solution)/shard_map/all_to_all | solution.py:130
  45.9 0.2 fusion.14
  46.3 8.7 %cholesky.16 = f32[95,95]{1,0:T(8,128)S(1)} custom-call(f32[95,95]{1,0:T(8,128)S(1)} %fusion.34), custom_call_target="Cholesky" | custom-call | tf_op jit(solution)/shard_map/jit(cholesky)/cholesky | solution.py:119
  55.0 0.6 compare_reduce_fusion
  55.7 0.7 fusion.21
  56.3 7.3 %custom-call.10 = f32[1,95,95]{1,2,0:T(8,128)S(1)} custom-call(f32[1,95,95]{2,1,0:T(8,128)S(1)} %fusion.21), custom_call_target="InvertDiagBlocksLowerTriangular" | custom-call | tf_op jit(solution)/shard_map/jit(_cho_solve)/triangular_solve | solution.py:120
  63.6 0.3 fusion.13
  64.2 1.9 %all-to-all-done = f32[32,8,16,128]{3,2,1,0:T(8,128)S(1)} async-done(((f32[32,8,16,128]{3,2,1,0:T(8,128)}), f32[32,8,16,128]{3,2,1,0:T(8,128)S(1)}, u32[]{:S(2)}, u32[]{:S(2)}) %all-to-all-start) | async-done | bytes 2097184 | tf_op jit(solution)/shard_map/all_to_all | solution.py:130
  66.1 3.7 %reshape.23 = f32[256,16,2,64]{3,2,1,0:T(2,128)} reshape(f32[32,8,16,128]{3,2,1,0:T(8,128)S(1)} %all-to-all-done) | data formatting | bytes 4194304 | tf_op jit(solution)/shard_map/reshape | solution.py:132
  69.7 5.4 %copy.8 = f32[256,2,16,64]{0,3,2,1:T(8,128)S(1)} copy(f32[256,2,16,64]{3,1,2,0:T(2,128)} %bitcast.37) | data formatting | bytes 4194304 | tf_op jit(solution)/shard_map/transpose | solution.py:132
  75.1 1.9 %fusion.40 = f32[95,2048]{0,1:S(1)} fusion(f32[95,256]{1,0:T(8,128)S(1)} %fusion.31, f32[256,2048]{0,1:T(8,128)S(1)} %bitcast.36), kind=kOutput, calls=%fused_computation.61 | convolution fusion | flops 597688320 | bytes 2972672
  77.0 1.8 %fusion.9 = f32[256,2048]{0,1:S(1)} fusion(f32[95,2048]{0,1:S(1)} %fusion.40, s32[256]{0:T(256)S(1)} %bitcast.47, s32[256]{0:T(256)S(1)} %bitcast.44), kind=kOutput, calls=%fused_computation.23 | convolution fusion | flops 597834240 | bytes 2877440
  78.9 0.5 bitcast_subtract_fusion
  79.3 3.8 %collective-permute-start.2 = (f32[256,2,64]{0,2,1:T(8,128)S(1)}, f32[256,2,64]{0,2,1:T(8,128)S(1)}, u32[]{:S(2)}, u32[]{:S(2)}) collective-permute-start(f32[256,2,64]{0,2,1:T(8,128)S(1)} %get-tuple-element.8), channel_id=1, source_target_pairs={{0,1},{1,2},{2,3},{4,5},{5,6},{6,7},{8,9},{9,10},{10,11},{12,13},{... | collective-permute-start | bytes 393224 | tf_op jit(solution)/shard_map/ppermute | solution.py:24
  83.2 1.9 %collective-permute-start.3 = (f32[256,2,64]{0,2,1:T(8,128)S(1)}, f32[256,2,64]{0,2,1:T(8,128)S(1)}, u32[]{:S(2)}, u32[]{:S(2)}) collective-permute-start(f32[256,2,64]{0,2,1:T(8,128)S(1)} %get-tuple-element.9), channel_id=1, source_target_pairs={{1,0},{2,1},{3,2},{5,4},{6,5},{7,6},{9,8},{10,9},{11,10},{13,12},{... | collective-permute-start | bytes 393224 | tf_op jit(solution)/shard_map/ppermute | solution.py:27
  85.1 5.9 %collective-permute-done.3 = f32[256,2,64]{0,2,1:T(8,128)S(1)} collective-permute-done((f32[256,2,64]{0,2,1:T(8,128)S(1)}, f32[256,2,64]{0,2,1:T(8,128)S(1)}, u32[]{:S(2)}, u32[]{:S(2)}) %collective-permute-start.3) | collective-permute-done | bytes 131104 | tf_op jit(solution)/shard_map/ppermute | solution.py:27
  91.0 2.4 %collective-permute-start.4 = (f32[256,36,2]{0,2,1:T(2,128)S(1)}, f32[256,36,2]{0,2,1:T(2,128)S(1)}, u32[]{:S(2)}, u32[]{:S(2)}) collective-permute-start(f32[256,36,2]{0,2,1:T(2,128)S(1)} %get-tuple-element.6), channel_id=1, source_target_pairs={{0,4},{4,8},{8,12},{12,16},{16,20},{20,24},{24,28},{28,32},{32,36}... | collective-permute-start | bytes 221192 | tf_op jit(solution)/shard_map/ppermute | solution.py:24
  93.4 5.9 %collective-permute-start.5 = (f32[256,36,2]{0,2,1:T(2,128)S(1)}, f32[256,36,2]{0,2,1:T(2,128)S(1)}, u32[]{:S(2)}, u32[]{:S(2)}) collective-permute-start(f32[256,36,2]{0,2,1:T(2,128)S(1)} %get-tuple-element.7), channel_id=1, source_target_pairs={{4,0},{8,4},{12,8},{16,12},{20,16},{24,20},{28,24},{32,28},{36,32}... | collective-permute-start | bytes 221192 | tf_op jit(solution)/shard_map/ppermute | solution.py:27
  99.3 1.4 %collective-permute-done.5 = f32[256,36,2]{0,2,1:T(2,128)S(1)} collective-permute-done((f32[256,36,2]{0,2,1:T(2,128)S(1)}, f32[256,36,2]{0,2,1:T(2,128)S(1)}, u32[]{:S(2)}, u32[]{:S(2)}) %collective-permute-start.5) | collective-permute-done | bytes 73760 | tf_op jit(solution)/shard_map/ppermute | solution.py:27
  100.7 0.3 pad_maximum_fusion.1
  101.0 0.5 fusion
  101.5 2.1 %fusion.5 = bf16[256,32,64]{0,2,1:T(8,128)(2,1)} fusion(f32[256,32,68]{0,2,1:T(8,128)S(1)} %fusion), kind=kLoop, calls=%fused_computation.14 | loop fusion | flops 4718592 | bytes 11534336 | tf_op jit(solution)/shard_map/convert_element_type | solution.py:139
  (14 shorter events, 0.5 us)
Async XLA Ops:
  0.6 2.2 %copy-start = (f32[8,32,2048]{2,1,0:T(8,128)S(1)}, f32[8,32,2048]{2,1,0:T(8,128)}, u32[]{:S(2)}) copy-start(f32[8,32,2048]{2,1,0:T(8,128)} %param.3) | copy-start | bytes 6291460
  3.1 11.3 %collective-permute-start = (f32[2,8,4,2048]{3,2,1,0:T(4,128)S(1)}, f32[2,8,4,2048]{3,2,1,0:T(4,128)S(1)}, u32[]{:S(2)}, u32[]{:S(2)}) collective-permute-start(f32[2,8,4,2048]{3,2,1,0:T(4,128)S(1)} %get-tuple-element.4), channel_id=1, source_target_pairs={{0,1},{1,2},{2,3},{4,5},{5,6},{6,7},{8,9},{9,10},{10,11},{12,13},{... | collective-permute-start | bytes 1572872 | tf_op jit(solution)/shard_map/ppermute | solution.py:24
  8.3 12.0 %collective-permute-start.1 = (f32[2,8,4,2048]{3,2,1,0:T(4,128)S(1)}, f32[2,8,4,2048]{3,2,1,0:T(4,128)S(1)}, u32[]{:S(2)}, u32[]{:S(2)}) collective-permute-start(f32[2,8,4,2048]{3,2,1,0:T(4,128)S(1)} %get-tuple-element.5), channel_id=1, source_target_pairs={{1,0},{2,1},{3,2},{5,4},{6,5},{7,6},{9,8},{10,9},{11,10},{13,12},{... | collective-permute-start | bytes 1572872 | tf_op jit(solution)/shard_map/ppermute | solution.py:27
  37.8 8.2 %copy-start.2 = (s32[256,2]{0,1:T(2,128)S(1)}, s32[256,2]{0,1:T(2,128)}, u32[]{:S(2)}) copy-start(s32[256,2]{0,1:T(2,128)} %param.5) | copy-start | bytes 6148
  37.8 28.3 %all-to-all-start = ((f32[32,8,16,128]{3,2,1,0:T(8,128)}), f32[32,8,16,128]{3,2,1,0:T(8,128)S(1)}, u32[]{:S(2)}, u32[]{:S(2)}) async-start(f32[32,8,16,128]{3,2,1,0:T(8,128)} %shard_map.50), calls=%async_computation | async-start | bytes 4194304 | tf_op jit(solution)/shard_map/all_to_all | solution.py:130
  77.0 2.3 %copy-start.1 = (f32[95,2048]{0,1}, f32[95,2048]{0,1:S(1)}, u32[]{:S(2)}) copy-start(f32[95,2048]{0,1:S(1)} %fusion.40) | copy-start | bytes 2334724
  79.3 5.7 %collective-permute-start.2 = (f32[256,2,64]{0,2,1:T(8,128)S(1)}, f32[256,2,64]{0,2,1:T(8,128)S(1)}, u32[]{:S(2)}, u32[]{:S(2)}) collective-permute-start(f32[256,2,64]{0,2,1:T(8,128)S(1)} %get-tuple-element.8), channel_id=1, source_target_pairs={{0,1},{1,2},{2,3},{4,5},{5,6},{6,7},{8,9},{9,10},{10,11},{12,13},{... | collective-permute-start | bytes 393224 | tf_op jit(solution)/shard_map/ppermute | solution.py:24
  83.2 7.8 %collective-permute-start.3 = (f32[256,2,64]{0,2,1:T(8,128)S(1)}, f32[256,2,64]{0,2,1:T(8,128)S(1)}, u32[]{:S(2)}, u32[]{:S(2)}) collective-permute-start(f32[256,2,64]{0,2,1:T(8,128)S(1)} %get-tuple-element.9), channel_id=1, source_target_pairs={{1,0},{2,1},{3,2},{5,4},{6,5},{7,6},{9,8},{10,9},{11,10},{13,12},{... | collective-permute-start | bytes 393224 | tf_op jit(solution)/shard_map/ppermute | solution.py:27
  91.0 8.3 %collective-permute-start.4 = (f32[256,36,2]{0,2,1:T(2,128)S(1)}, f32[256,36,2]{0,2,1:T(2,128)S(1)}, u32[]{:S(2)}, u32[]{:S(2)}) collective-permute-start(f32[256,36,2]{0,2,1:T(2,128)S(1)} %get-tuple-element.6), channel_id=1, source_target_pairs={{0,4},{4,8},{8,12},{12,16},{16,20},{20,24},{24,28},{28,32},{32,36}... | collective-permute-start | bytes 221192 | tf_op jit(solution)/shard_map/ppermute | solution.py:24
  93.4 7.3 %collective-permute-start.5 = (f32[256,36,2]{0,2,1:T(2,128)S(1)}, f32[256,36,2]{0,2,1:T(2,128)S(1)}, u32[]{:S(2)}, u32[]{:S(2)}) collective-permute-start(f32[256,36,2]{0,2,1:T(2,128)S(1)} %get-tuple-element.7), channel_id=1, source_target_pairs={{4,0},{8,4},{12,8},{16,12},{20,16},{24,20},{28,24},{32,28},{36,32}... | collective-permute-start | bytes 221192 | tf_op jit(solution)/shard_map/ppermute | solution.py:27

commit v2 on v1

--- a/solution.py
+++ b/solution.py
@@ -27,6 +27,33 @@
         high = lax.ppermute(lax.slice_in_dim(block, 0, width, axis=dim), axis, backward)
         block = jnp.concatenate([low, block, high], axis=dim)
     return block
+
+
+def halo_2d(block, width):
+    nrows, nifg = lax.axis_size("rows"), lax.axis_size("ifg")
+    end_r, end_c = block.shape[1] - width, block.shape[2] - width
+
+    def send(part, step_r, step_i):
+        pairs = []
+        for i in range(nifg):
+            for r in range(nrows):
+                ti, tr = i + step_i, r + step_r
+                if 0 <= ti < nifg and 0 <= tr < nrows:
+                    pairs.append((i * nrows + r, ti * nrows + tr))
+        return lax.ppermute(part, ("ifg", "rows"), pairs)
+
+    top, bottom = block[:, end_r:], block[:, :width]
+    upper = jnp.concatenate(
+        [send(top[:, :, end_c:], 1, 1), send(top, 1, 0), send(top[:, :, :width], 1, -1)], axis=2
+    )
+    middle = jnp.concatenate(
+        [send(block[:, :, end_c:], 0, 1), block, send(block[:, :, :width], 0, -1)], axis=2
+    )
+    lower = jnp.concatenate(
+        [send(bottom[:, :, end_c:], -1, 1), send(bottom, -1, 0), send(bottom[:, :, :width], -1, -1)],
+        axis=2,
+    )
+    return jnp.concatenate([upper, middle, lower], axis=1)
 
 
 def wrapped_diff(delta):
@@ -134,7 +161,7 @@
     residual = block - jnp.einsum(
         "ie,erc->irc", design, series_block, precision=lax.Precision.HIGHEST
     )
-    padded = extended_2(residual, (("rows", 1), ("ifg", 2)), 2)
+    padded = halo_2d(residual, 2)
     filtered = binomial(binomial(padded, 1), 2)
     return (series_block, filtered.astype(jnp.bfloat16))
 

time: 105 us -> 128 us (1.22)
  waiting for transfers between devices: 19.2 us -> 32.9 us
  starting transfers between devices: 29.3 us -> 38.2 us
    ppermute x0 -> x8, starting transfers between devices: none -> 22.9 us  [send(): return lax.ppermute(part, ('ifg', 'rows'), pairs)]
    ppermute x0 -> x8, waiting for transfers between devices: none -> 20.9 us  [send(): return lax.ppermute(part, ('ifg', 'rows'), pairs)]
    ppermute x3 -> x1, starting transfers between devices: 9.73 us -> 1.92 us  [extended_2(): lax.ppermute(lax.slice_in_dim(block, 0, width, axis=dim), axis, backward)]
    ppermute x3 -> x1, waiting for transfers between devices: 13.1 us -> 5.9 us  [extended_2(): lax.ppermute(lax.slice_in_dim(block, 0, width, axis=dim), axis, backward)]
    ppermute x3 -> x1, starting transfers between devices: 11.4 us -> 5.21 us  [extended_2(): lax.ppermute(lax.slice_in_dim(block, block.shape[dim] - width, None, axis...]
    ppermute x3 -> x1, waiting for transfers between devices: 4.18 us -> 4.18 us  [extended_2(): lax.ppermute(lax.slice_in_dim(block, block.shape[dim] - width, None, axis...]
  transfers between devices with their start and end apart: 7 -> 11, of which waited for: 5 -> 7; matrix products, arithmetic and copies ran while one was open for 18% -> 14% of each run, Pallas kernels for 0% -> 0%
where the time goes in v2:
time: 128 us; the launch traced here: 127 us
  starting transfers between devices  38.2 us (30%)
  waiting for transfers between devices  32.9 us (26%)
  other arithmetic  24.9 us (19%)
  Pallas kernels  13.6 us (11%)
  local copies, waits for them, and re-layouts  12.2 us (10%)
  matrix products  4.38 us (3%)
    ppermute x8, starting transfers between devices, send(): return lax.ppermute(part, ('ifg', 'rows'), pairs)  22.9 us
    ppermute x8, waiting for transfers between devices, send(): return lax.ppermute(part, ('ifg', 'rows'), pairs)  20.9 us
    pallas_call x1, Pallas kernels, unwrap(): pl.pallas_call(functools.partial(unwrap_kernel, rows_out), grid=(n,), in_...  13.6 us
    another operation x3, other arithmetic, network_maps(): factor = jnp.linalg.cholesky(normal_matrix)  9.36 us
    all_to_all x1, starting transfers between devices, on_device(): lax.all_to_all(current, 'ifg', split_axis=0, concat_axis=0, tiled=True)  8.16 us
    another operation x2, other arithmetic, network_maps(): pseudo = jax.scipy.linalg.cho_solve((factor, True), design.T)  7.94 us
    ppermute x1, waiting for transfers between devices, extended_2(): lax.ppermute(lax.slice_in_dim(block, 0, width, axis=dim), axis, backward)  5.9 us
    transpose x1, local copies, waits for them, and re-layouts, on_device(): received.reshape(ifg, rows // 2, 2, 64).transpose(0, 2, 1, 3)  5.38 us
  transfers between devices with their start and end apart: 11, of which 7 were waited for; matrix products, arithmetic and copies ran while one was open for 14% of the time, Pallas kernels for 0%

profile of v2, /device:TPU:9, one launch (start us, length us, event | category | flops | bytes accessed | tf_op | source)
XLA Modules:
  0.0 127.2 jit_solution(11232500574960644022)
XLA Ops:
  0.6 1.9 %convert_bitcast_fusion = f32[1,8,32,2048]{3,2,1,0:T(8,128)S(1)} fusion(s32[8,32,2048]{2,1,0:T(8,128)} %param.4), kind=kLoop, calls=%fused_computation.23 | loop fusion | flops 524288 | bytes 4194304 | tf_op jit(solution)/shard_map/stack | solution.py:153
  3.1 5.2 %collective-permute-start = (f32[2,8,4,2048]{3,2,1,0:T(4,128)S(1)}, f32[2,8,4,2048]{3,2,1,0:T(4,128)S(1)}, u32[]{:S(2)}, u32[]{:S(2)}) collective-permute-start(f32[2,8,4,2048]{3,2,1,0:T(4,128)S(1)} %get-tuple-element.4), channel_id=1, source_target_pairs={{0,1},{1,2},{2,3},{4,5},{5,6},{6,7},{8,9},{9,10},{10,11},{12,13},{... | collective-permute-start | bytes 1572872 | tf_op jit(solution)/shard_map/ppermute | solution.py:24
  8.3 1.9 %collective-permute-start.1 = (f32[2,8,4,2048]{3,2,1,0:T(4,128)S(1)}, f32[2,8,4,2048]{3,2,1,0:T(4,128)S(1)}, u32[]{:S(2)}, u32[]{:S(2)}) collective-permute-start(f32[2,8,4,2048]{3,2,1,0:T(4,128)S(1)} %get-tuple-element.5), channel_id=1, source_target_pairs={{1,0},{2,1},{3,2},{5,4},{6,5},{7,6},{9,8},{10,9},{11,10},{13,12},{... | collective-permute-start | bytes 1572872 | tf_op jit(solution)/shard_map/ppermute | solution.py:27
  10.3 4.2 %collective-permute-done = f32[2,8,4,2048]{3,2,1,0:T(4,128)S(1)} collective-permute-done((f32[2,8,4,2048]{3,2,1,0:T(4,128)S(1)}, f32[2,8,4,2048]{3,2,1,0:T(4,128)S(1)}, u32[]{:S(2)}, u32[]{:S(2)}) %collective-permute-start) | collective-permute-done | bytes 524320 | tf_op jit(solution)/shard_map/ppermute | solution.py:24
  14.4 5.9 %collective-permute-done.1 = f32[2,8,4,2048]{3,2,1,0:T(4,128)S(1)} collective-permute-done((f32[2,8,4,2048]{3,2,1,0:T(4,128)S(1)}, f32[2,8,4,2048]{3,2,1,0:T(4,128)S(1)}, u32[]{:S(2)}, u32[]{:S(2)}) %collective-permute-start.1) | collective-permute-done | bytes 524320 | tf_op jit(solution)/shard_map/ppermute | solution.py:27
  20.3 1.1 pad_maximum_fusion
  21.5 2.6 %slice_bitcast_fusion = (f32[8,40,2048]{2,1,0:T(8,128)}, f32[8,40,2048]{2,1,0:T(8,128)}) fusion(f32[2,8,40,2048]{3,2,1,0:T(8,128)S(1)} %pad_maximum_fusion), kind=kLoop, calls=%fused_computation.1 | loop fusion | bytes 10485760 | tf_op jit(solution)/shard_map/squeeze | solution.py:156
  24.1 13.6 %shard_map.50 = f32[32,8,16,128]{3,2,1,0:T(8,128)} custom-call(f32[8,40,2048]{2,1,0:T(8,128)} %get-tuple-element.3.p_ref, f32[8,40,2048]{2,1,0:T(8,128)} %get-tuple-element.2.q_ref), custom_call_target="tpu_custom_call" | custom-call | flops 78643200 | bytes 7340032 | tf_op jit(solution)/shard_map/pallas_call | solution.py:112
  37.8 8.2 %all-to-all-start = ((f32[32,8,16,128]{3,2,1,0:T(8,128)}), f32[32,8,16,128]{3,2,1,0:T(8,128)S(1)}, u32[]{:S(2)}, u32[]{:S(2)}) async-start(f32[32,8,16,128]{3,2,1,0:T(8,128)} %shard_map.50), calls=%async_computation | async-start | bytes 4194304 | tf_op jit(solution)/shard_map/all_to_all | solution.py:157
  46.3 8.7 %cholesky.16 = f32[95,95]{1,0:T(8,128)S(1)} custom-call(f32[95,95]{1,0:T(8,128)S(1)} %fusion.34), custom_call_target="Cholesky" | custom-call | tf_op jit(solution)/shard_map/jit(cholesky)/cholesky | solution.py:146
  55.7 0.7 fusion.21
  56.4 7.3 %custom-call.10 = f32[1,95,95]{1,2,0:T(8,128)S(1)} custom-call(f32[1,95,95]{2,1,0:T(8,128)S(1)} %fusion.21), custom_call_target="InvertDiagBlocksLowerTriangular" | custom-call | tf_op jit(solution)/shard_map/jit(_cho_solve)/triangular_solve | solution.py:147
  64.2 1.9 %all-to-all-done = f32[32,8,16,128]{3,2,1,0:T(8,128)S(1)} async-done(((f32[32,8,16,128]{3,2,1,0:T(8,128)}), f32[32,8,16,128]{3,2,1,0:T(8,128)S(1)}, u32[]{:S(2)}, u32[]{:S(2)}) %all-to-all-start) | async-done | bytes 2097184 | tf_op jit(solution)/shard_map/all_to_all | solution.py:157
  66.1 3.7 %reshape.23 = f32[256,16,2,64]{3,2,1,0:T(2,128)} reshape(f32[32,8,16,128]{3,2,1,0:T(8,128)S(1)} %all-to-all-done) | data formatting | bytes 4194304 | tf_op jit(solution)/shard_map/reshape | solution.py:159
  69.8 5.4 %copy.8 = f32[256,2,16,64]{0,3,2,1:T(8,128)S(1)} copy(f32[256,2,16,64]{3,1,2,0:T(2,128)} %bitcast.37) | data formatting | bytes 4194304 | tf_op jit(solution)/shard_map/transpose | solution.py:159
  75.2 1.8 %fusion.42 = f32[95,2048]{0,1:S(1)} fusion(f32[95,256]{1,0:T(8,128)S(1)} %fusion.31, f32[256,2048]{0,1:T(8,128)S(1)} %bitcast.36), kind=kOutput, calls=%fused_computation.61 | convolution fusion | flops 597688320 | bytes 2972672
  77.0 1.8 %fusion.9 = f32[256,2048]{0,1:S(1)} fusion(f32[95,2048]{0,1:S(1)} %fusion.42, s32[256]{0:T(256)S(1)} %bitcast.47, s32[256]{0:T(256)S(1)} %bitcast.44), kind=kOutput, calls=%fused_computation.24 | convolution fusion | flops 597834240 | bytes 2877440
  79.4 3.4 %collective-permute-start.5 = (f32[256,32,2]{0,2,1:T(2,128)S(1)}, f32[256,32,2]{0,2,1:T(2,128)S(1)}, u32[]{:S(2)}, u32[]{:S(2)}) collective-permute-start(f32[256,32,2]{0,2,1:T(2,128)S(1)} %get-tuple-element.14), channel_id=1, source_target_pairs={{0,4},{1,5},{2,6},{3,7},{4,8},{5,9},{6,10},{7,11},{8,12},{9,13},{1... | collective-permute-start | bytes 196616 | tf_op jit(solution)/shard_map/ppermute | solution.py:43
  82.7 4.9 %collective-permute-start.6 = (f32[256,32,2]{0,2,1:T(2,128)S(1)}, f32[256,32,2]{0,2,1:T(2,128)S(1)}, u32[]{:S(2)}, u32[]{:S(2)}) collective-permute-start(f32[256,32,2]{0,2,1:T(2,128)S(1)} %get-tuple-element.15), channel_id=1, source_target_pairs={{4,0},{5,1},{6,2},{7,3},{8,4},{9,5},{10,6},{11,7},{12,8},{13,9},{1... | collective-permute-start | bytes 196616 | tf_op jit(solution)/shard_map/ppermute | solution.py:43
  87.7 4.4 %collective-permute-start.3 = (f32[256,2,64]{0,2,1:T(8,128)S(1)}, f32[256,2,64]{0,2,1:T(8,128)S(1)}, u32[]{:S(2)}, u32[]{:S(2)}) collective-permute-start(f32[256,2,64]{0,2,1:T(8,128)S(1)} %get-tuple-element.12), channel_id=1, source_target_pairs={{0,1},{1,2},{2,3},{4,5},{5,6},{6,7},{8,9},{9,10},{10,11},{12,13},{... | collective-permute-start | bytes 393224 | tf_op jit(solution)/shard_map/ppermute | solution.py:43
  92.0 1.9 %collective-permute-start.8 = (f32[256,2,64]{0,2,1:T(8,128)S(1)}, f32[256,2,64]{0,2,1:T(8,128)S(1)}, u32[]{:S(2)}, u32[]{:S(2)}) collective-permute-start(f32[256,2,64]{0,2,1:T(8,128)S(1)} %get-tuple-element.13), channel_id=1, source_target_pairs={{1,0},{2,1},{3,2},{5,4},{6,5},{7,6},{9,8},{10,9},{11,10},{13,12},{... | collective-permute-start | bytes 393224 | tf_op jit(solution)/shard_map/ppermute | solution.py:43
  94.0 2.4 %collective-permute-start.2 = (f32[256,2,2]{0,2,1:T(2,128)S(1)}, f32[256,2,2]{0,2,1:T(2,128)S(1)}, u32[]{:S(2)}, u32[]{:S(2)}) collective-permute-start(f32[256,2,2]{0,2,1:T(2,128)S(1)} %get-tuple-element.8), channel_id=1, source_target_pairs={{0,5},{1,6},{2,7},{4,9},{5,10},{6,11},{8,13},{9,14},{10,15},{12,17... | collective-permute-start | bytes 12296 | tf_op jit(solution)/shard_map/ppermute | solution.py:43
  96.3 5.6 %collective-permute-done.2 = f32[256,2,2]{0,2,1:T(2,128)S(1)} collective-permute-done((f32[256,2,2]{0,2,1:T(2,128)S(1)}, f32[256,2,2]{0,2,1:T(2,128)S(1)}, u32[]{:S(2)}, u32[]{:S(2)}) %collective-permute-start.2) | collective-permute-done | bytes 4128 | tf_op jit(solution)/shard_map/ppermute | solution.py:43
  101.9 1.9 %collective-permute-start.9 = (f32[256,2,2]{0,2,1:T(2,128)S(1)}, f32[256,2,2]{0,2,1:T(2,128)S(1)}, u32[]{:S(2)}, u32[]{:S(2)}) collective-permute-start(f32[256,2,2]{0,2,1:T(2,128)S(1)} %get-tuple-element.9), channel_id=1, source_target_pairs={{5,0},{6,1},{7,2},{9,4},{10,5},{11,6},{13,8},{14,9},{15,10},{17,12... | collective-permute-start | bytes 12296 | tf_op jit(solution)/shard_map/ppermute | solution.py:43
  103.9 5.4 %collective-permute-done.9 = f32[256,2,2]{0,2,1:T(2,128)S(1)} collective-permute-done((f32[256,2,2]{0,2,1:T(2,128)S(1)}, f32[256,2,2]{0,2,1:T(2,128)S(1)}, u32[]{:S(2)}, u32[]{:S(2)}) %collective-permute-start.9) | collective-permute-done | bytes 4128 | tf_op jit(solution)/shard_map/ppermute | solution.py:43
  109.2 1.9 %collective-permute-start.7 = (f32[256,2,2]{0,2,1:T(2,128)S(1)}, f32[256,2,2]{0,2,1:T(2,128)S(1)}, u32[]{:S(2)}, u32[]{:S(2)}) collective-permute-start(f32[256,2,2]{0,2,1:T(2,128)S(1)} %get-tuple-element.10), channel_id=1, source_target_pairs={{1,4},{2,5},{3,6},{5,8},{6,9},{7,10},{9,12},{10,13},{11,14},{13,16... | collective-permute-start | bytes 12296 | tf_op jit(solution)/shard_map/ppermute | solution.py:43
  111.2 7.2 %collective-permute-done.7 = f32[256,2,2]{0,2,1:T(2,128)S(1)} collective-permute-done((f32[256,2,2]{0,2,1:T(2,128)S(1)}, f32[256,2,2]{0,2,1:T(2,128)S(1)}, u32[]{:S(2)}, u32[]{:S(2)}) %collective-permute-start.7) | collective-permute-done | bytes 4128 | tf_op jit(solution)/shard_map/ppermute | solution.py:43
  118.4 2.2 %collective-permute-start.4 = (f32[256,2,2]{0,2,1:T(2,128)S(1)}, f32[256,2,2]{0,2,1:T(2,128)S(1)}, u32[]{:S(2)}, u32[]{:S(2)}) collective-permute-start(f32[256,2,2]{0,2,1:T(2,128)S(1)} %get-tuple-element.11), channel_id=1, source_target_pairs={{4,1},{5,2},{6,3},{8,5},{9,6},{10,7},{12,9},{13,10},{14,11},{16,13... | collective-permute-start | bytes 12296 | tf_op jit(solution)/shard_map/ppermute | solution.py:43
  120.5 2.7 %collective-permute-done.4 = f32[256,2,2]{0,2,1:T(2,128)S(1)} collective-permute-done((f32[256,2,2]{0,2,1:T(2,128)S(1)}, f32[256,2,2]{0,2,1:T(2,128)S(1)}, u32[]{:S(2)}, u32[]{:S(2)}) %collective-permute-start.4) | collective-permute-done | bytes 4128 | tf_op jit(solution)/shard_map/ppermute | solution.py:43
  123.3 0.9 maximum_maximum_fusion
  124.2 0.8 fusion
  125.1 2.1 %fusion.5 = bf16[256,32,64]{0,2,1:T(8,128)(2,1)} fusion(f32[256,32,68]{0,2,1:T(8,128)S(1)} %fusion), kind=kLoop, calls=%fused_computation.15 | loop fusion | flops 4718592 | bytes 11534336 | tf_op jit(solution)/shard_map/convert_element_type | solution.py:166
  (23 shorter events, 2.7 us)
Async XLA Ops:
  0.6 2.2 %copy-start = (f32[8,32,2048]{2,1,0:T(8,128)S(1)}, f32[8,32,2048]{2,1,0:T(8,128)}, u32[]{:S(2)}) copy-start(f32[8,32,2048]{2,1,0:T(8,128)} %param.3) | copy-start | bytes 6291460
  3.1 11.3 %collective-permute-start = (f32[2,8,4,2048]{3,2,1,0:T(4,128)S(1)}, f32[2,8,4,2048]{3,2,1,0:T(4,128)S(1)}, u32[]{:S(2)}, u32[]{:S(2)}) collective-permute-start(f32[2,8,4,2048]{3,2,1,0:T(4,128)S(1)} %get-tuple-element.4), channel_id=1, source_target_pairs={{0,1},{1,2},{2,3},{4,5},{5,6},{6,7},{8,9},{9,10},{10,11},{12,13},{... | collective-permute-start | bytes 1572872 | tf_op jit(solution)/shard_map/ppermute | solution.py:24
  8.3 12.0 %collective-permute-start.1 = (f32[2,8,4,2048]{3,2,1,0:T(4,128)S(1)}, f32[2,8,4,2048]{3,2,1,0:T(4,128)S(1)}, u32[]{:S(2)}, u32[]{:S(2)}) collective-permute-start(f32[2,8,4,2048]{3,2,1,0:T(4,128)S(1)} %get-tuple-element.5), channel_id=1, source_target_pairs={{1,0},{2,1},{3,2},{5,4},{6,5},{7,6},{9,8},{10,9},{11,10},{13,12},{... | collective-permute-start | bytes 1572872 | tf_op jit(solution)/shard_map/ppermute | solution.py:27
  37.8 8.2 %copy-start.2 = (s32[256,2]{0,1:T(2,128)S(1)}, s32[256,2]{0,1:T(2,128)}, u32[]{:S(2)}) copy-start(s32[256,2]{0,1:T(2,128)} %param.5) | copy-start | bytes 6148
  37.8 28.3 %all-to-all-start = ((f32[32,8,16,128]{3,2,1,0:T(8,128)}), f32[32,8,16,128]{3,2,1,0:T(8,128)S(1)}, u32[]{:S(2)}, u32[]{:S(2)}) async-start(f32[32,8,16,128]{3,2,1,0:T(8,128)} %shard_map.50), calls=%async_computation | async-start | bytes 4194304 | tf_op jit(solution)/shard_map/all_to_all | solution.py:157
  77.0 2.3 %copy-start.1 = (f32[95,2048]{0,1}, f32[95,2048]{0,1:S(1)}, u32[]{:S(2)}) copy-start(f32[95,2048]{0,1:S(1)} %fusion.42) | copy-start | bytes 2334724
  79.4 43.9 %collective-permute-start.5 = (f32[256,32,2]{0,2,1:T(2,128)S(1)}, f32[256,32,2]{0,2,1:T(2,128)S(1)}, u32[]{:S(2)}, u32[]{:S(2)}) collective-permute-start(f32[256,32,2]{0,2,1:T(2,128)S(1)} %get-tuple-element.14), channel_id=1, source_target_pairs={{0,4},{1,5},{2,6},{3,7},{4,8},{5,9},{6,10},{7,11},{8,12},{9,13},{1... | collective-permute-start | bytes 196616 | tf_op jit(solution)/shard_map/ppermute | solution.py:43
  82.7 40.5 %collective-permute-start.6 = (f32[256,32,2]{0,2,1:T(2,128)S(1)}, f32[256,32,2]{0,2,1:T(2,128)S(1)}, u32[]{:S(2)}, u32[]{:S(2)}) collective-permute-start(f32[256,32,2]{0,2,1:T(2,128)S(1)} %get-tuple-element.15), channel_id=1, source_target_pairs={{4,0},{5,1},{6,2},{7,3},{8,4},{9,5},{10,6},{11,7},{12,8},{13,9},{1... | collective-permute-start | bytes 196616 | tf_op jit(solution)/shard_map/ppermute | solution.py:43
  87.7 35.6 %collective-permute-start.3 = (f32[256,2,64]{0,2,1:T(8,128)S(1)}, f32[256,2,64]{0,2,1:T(8,128)S(1)}, u32[]{:S(2)}, u32[]{:S(2)}) collective-permute-start(f32[256,2,64]{0,2,1:T(8,128)S(1)} %get-tuple-element.12), channel_id=1, source_target_pairs={{0,1},{1,2},{2,3},{4,5},{5,6},{6,7},{8,9},{9,10},{10,11},{12,13},{... | collective-permute-start | bytes 393224 | tf_op jit(solution)/shard_map/ppermute | solution.py:43
  92.0 31.3 %collective-permute-start.8 = (f32[256,2,64]{0,2,1:T(8,128)S(1)}, f32[256,2,64]{0,2,1:T(8,128)S(1)}, u32[]{:S(2)}, u32[]{:S(2)}) collective-permute-start(f32[256,2,64]{0,2,1:T(8,128)S(1)} %get-tuple-element.13), channel_id=1, source_target_pairs={{1,0},{2,1},{3,2},{5,4},{6,5},{7,6},{9,8},{10,9},{11,10},{13,12},{... | collective-permute-start | bytes 393224 | tf_op jit(solution)/shard_map/ppermute | solution.py:43
  94.0 7.9 %collective-permute-start.2 = (f32[256,2,2]{0,2,1:T(2,128)S(1)}, f32[256,2,2]{0,2,1:T(2,128)S(1)}, u32[]{:S(2)}, u32[]{:S(2)}) collective-permute-start(f32[256,2,2]{0,2,1:T(2,128)S(1)} %get-tuple-element.8), channel_id=1, source_target_pairs={{0,5},{1,6},{2,7},{4,9},{5,10},{6,11},{8,13},{9,14},{10,15},{12,17... | collective-permute-start | bytes 12296 | tf_op jit(solution)/shard_map/ppermute | solution.py:43
  101.9 7.3 %collective-permute-start.9 = (f32[256,2,2]{0,2,1:T(2,128)S(1)}, f32[256,2,2]{0,2,1:T(2,128)S(1)}, u32[]{:S(2)}, u32[]{:S(2)}) collective-permute-start(f32[256,2,2]{0,2,1:T(2,128)S(1)} %get-tuple-element.9), channel_id=1, source_target_pairs={{5,0},{6,1},{7,2},{9,4},{10,5},{11,6},{13,8},{14,9},{15,10},{17,12... | collective-permute-start | bytes 12296 | tf_op jit(solution)/shard_map/ppermute | solution.py:43
  109.2 9.1 %collective-permute-start.7 = (f32[256,2,2]{0,2,1:T(2,128)S(1)}, f32[256,2,2]{0,2,1:T(2,128)S(1)}, u32[]{:S(2)}, u32[]{:S(2)}) collective-permute-start(f32[256,2,2]{0,2,1:T(2,128)S(1)} %get-tuple-element.10), channel_id=1, source_target_pairs={{1,4},{2,5},{3,6},{5,8},{6,9},{7,10},{9,12},{10,13},{11,14},{13,16... | collective-permute-start | bytes 12296 | tf_op jit(solution)/shard_map/ppermute | solution.py:43
  118.4 4.9 %collective-permute-start.4 = (f32[256,2,2]{0,2,1:T(2,128)S(1)}, f32[256,2,2]{0,2,1:T(2,128)S(1)}, u32[]{:S(2)}, u32[]{:S(2)}) collective-permute-start(f32[256,2,2]{0,2,1:T(2,128)S(1)} %get-tuple-element.11), channel_id=1, source_target_pairs={{4,1},{5,2},{6,3},{8,5},{9,6},{10,7},{12,9},{13,10},{14,11},{16,13... | collective-permute-start | bytes 12296 | tf_op jit(solution)/shard_map/ppermute | solution.py:43

commit v3 on v1

--- a/solution.py
+++ b/solution.py
@@ -35,9 +35,15 @@
     return jnp.where(delta >= PI32, above, jnp.where(delta <= -PI32, below, delta))
 
 
-def unwrap_kernel(rows_out, p_ref, q_ref, o_ref, cur_ref):
-    p = p_ref[0]
-    q = q_ref[0]
+def unwrap_kernel(rows_out, ph_ref, wt_ref, top_ref, bot_ref, o_ref, p_ref, q_ref, cur_ref):
+    p_ref[pl.ds(0, HALO), :] = top_ref[0, 0]
+    p_ref[pl.ds(HALO, rows_out), :] = ph_ref[0]
+    p_ref[pl.ds(HALO + rows_out, HALO), :] = bot_ref[0, 0]
+    q_ref[pl.ds(0, HALO), :] = top_ref[1, 0]
+    q_ref[pl.ds(HALO, rows_out), :] = wt_ref[0].astype(jnp.float32)
+    q_ref[pl.ds(HALO + rows_out, HALO), :] = bot_ref[1, 0]
+    p = p_ref[...]
+    q = q_ref[...]
     nr, nc = p.shape
     row = lax.broadcasted_iota(jnp.int32, (nr, nc), 0)
     col = lax.broadcasted_iota(jnp.int32, (nr, nc), 1)
@@ -80,22 +86,26 @@
         o_ref[2 * m + 1, 0] = odd[:, 128 * m : 128 * (m + 1)]
 
 
-def unwrap(phase_ext, quality_ext, rows_out):
-    n, nr, nc = phase_ext.shape
+def unwrap(phase, weights, top, bottom):
+    n, rows_out, nc = phase.shape
+    nr = rows_out + 2 * HALO
+    halo_spec = pl.BlockSpec((2, 1, HALO, nc), lambda i: (0, i, 0, 0))
     return pl.pallas_call(
         functools.partial(unwrap_kernel, rows_out),
         grid=(n,),
         in_specs=[
-            pl.BlockSpec((1, nr, nc), lambda i: (i, 0, 0)),
-            pl.BlockSpec((1, nr, nc), lambda i: (i, 0, 0)),
+            pl.BlockSpec((1, rows_out, nc), lambda i: (i, 0, 0)),
+            pl.BlockSpec((1, rows_out, nc), lambda i: (i, 0, 0)),
+            halo_spec,
+            halo_spec,
         ],
         out_specs=pl.BlockSpec((nc // 64, 1, rows_out // 2, 128), lambda i: (0, i, 0, 0)),
         out_shape=jax.ShapeDtypeStruct((nc // 64, n, rows_out // 2, 128), jnp.float32),
-        scratch_shapes=[pltpu.VMEM((nr, nc), jnp.float32)],
+        scratch_shapes=[pltpu.VMEM((nr, nc), jnp.float32)] * 3,
         cost_estimate=pl.CostEstimate(
             flops=120 * n * nr * nc, bytes_accessed=4 * n * nc * (2 * nr + rows_out), transcendentals=0
         ),
-    )(phase_ext, quality_ext)
+    )(phase, weights, top, bottom)
 
 
 def binomial(padded, axis):
@@ -123,10 +133,15 @@
 
 def on_device(phase, weights, network):
     design, pseudo = network_maps(network)
-    stacked = jnp.stack([phase, weights.astype(jnp.float32)])
-    extended = extended_2(stacked, (("rows", 2),), HALO)
     rows = phase.shape[1]
-    current = unwrap(extended[0], extended[1], rows)
+    count = lax.axis_size("rows")
+    forward = [(i, i + 1) for i in range(count - 1)]
+    backward = [(target, source) for source, target in forward]
+    edge_low = jnp.stack([phase[:, rows - HALO :], weights[:, rows - HALO :].astype(jnp.float32)])
+    edge_high = jnp.stack([phase[:, :HALO], weights[:, :HALO].astype(jnp.float32)])
+    top = lax.ppermute(edge_low, "rows", forward)
+    bottom = lax.ppermute(edge_high, "rows", backward)
+    current = unwrap(phase, weights, top, bottom)
     received = lax.all_to_all(current, "ifg", split_axis=0, concat_axis=0, tiled=True)
     ifg = received.shape[0] * received.shape[1]
     block = received.reshape(ifg, rows // 2, 2, 64).transpose(0, 2, 1, 3).reshape(ifg, rows, 64)

time: 105 us -> 103 us (0.981)
  other arithmetic: 24 us -> 22.3 us
    ppermute x0 -> x2, waiting for transfers between devices: none -> 10.1 us  [the longest x1 6.03 us: on_device(): bottom = lax.ppermute(edge_high, 'rows', backward)]
    ppermute x0 -> x2, starting transfers between devices: none -> 7.13 us  [the longest x1 5.21 us: on_device(): top = lax.ppermute(edge_low, 'rows', forward)]
    ppermute x3 -> x2, waiting for transfers between devices: 13.1 us -> 7.23 us  [extended_2(): lax.ppermute(lax.slice_in_dim(block, 0, width, axis=dim), axis, backward)]
    ppermute x3 -> x2, starting transfers between devices: 11.4 us -> 6.2 us  [extended_2(): lax.ppermute(lax.slice_in_dim(block, block.shape[dim] - width, None, axis...]
    ppermute x3 -> x2, waiting for transfers between devices: 4.18 us -> 0.01 us  [extended_2(): lax.ppermute(lax.slice_in_dim(block, block.shape[dim] - width, None, axis...]
    squeeze x1 -> x0, local copies, waits for them, and re-layouts: 2.64 us -> none  [on_device(): current = unwrap(extended[0], extended[1], rows)]
    ppermute x3 -> x2, starting transfers between devices: 9.73 us -> 7.81 us  [extended_2(): lax.ppermute(lax.slice_in_dim(block, 0, width, axis=dim), axis, backward)]
    another operation x0 -> x1, local copies, waits for them, and re-layouts: none -> 1.3 us  [on_device(): jnp.stack([phase[:, :HALO], weights[:, :HALO].astype(jnp.float32)])]
where the time goes in v3:
time: 103 us; the launch traced here: 102 us
  starting transfers between devices  29.3 us (28%)
  other arithmetic  22.3 us (22%)
  waiting for transfers between devices  19.2 us (19%)
  Pallas kernels  14.2 us (14%)
  local copies, waits for them, and re-layouts  11.3 us (11%)
  matrix products  4.45 us (4%)
    pallas_call x1, Pallas kernels, unwrap(): pl.pallas_call(functools.partial(unwrap_kernel, rows_out), grid=(n,), in_...  14.2 us
    another operation x3, other arithmetic, network_maps(): factor = jnp.linalg.cholesky(normal_matrix)  9.36 us
    all_to_all x1, starting transfers between devices, on_device(): lax.all_to_all(current, 'ifg', split_axis=0, concat_axis=0, tiled=True)  8.16 us
    another operation x2, other arithmetic, network_maps(): pseudo = jax.scipy.linalg.cho_solve((factor, True), design.T)  7.94 us
    ppermute x2, starting transfers between devices, extended_2(): lax.ppermute(lax.slice_in_dim(block, 0, width, axis=dim), axis, backward)  7.81 us
    ppermute x2, waiting for transfers between devices, extended_2(): lax.ppermute(lax.slice_in_dim(block, 0, width, axis=dim), axis, backward)  7.23 us
    ppermute x2, starting transfers between devices, extended_2(): lax.ppermute(lax.slice_in_dim(block, block.shape[dim] - width, None, axis...  6.2 us
    ppermute x1, waiting for transfers between devices, on_device(): bottom = lax.ppermute(edge_high, 'rows', backward)  6.03 us
  transfers between devices with their start and end apart: 7, of which 5 were waited for; matrix products, arithmetic and copies ran while one was open for 18% of the time, Pallas kernels for 0%

profile of v3, /device:TPU:9, one launch (start us, length us, event | category | flops | bytes accessed | tf_op | source)
XLA Modules:
  0.0 101.6 jit_solution(8437144823164956436)
XLA Ops:
  0.6 1.3 %slice_bitcast_fusion = (f32[1,8,4,2048]{3,2,1,0:T(4,128)S(1)}, f32[1,8,4,2048]{3,2,1,0:T(4,128)S(1)}) fusion(f32[8,32,2048]{2,1,0:T(8,128)} %ph_ref.1), kind=kLoop, calls=%fused_computation.24 | loop fusion | bytes 1048576 | tf_op jit(solution)/shard_map/stack | solution.py:141
  1.9 1.3 %convert_bitcast_fusion = (f32[1,8,4,2048]{3,2,1,0:T(4,128)S(1)}, f32[1,8,4,2048]{3,2,1,0:T(4,128)S(1)}) fusion(s32[8,32,2048]{2,1,0:T(8,128)} %wt_ref.1), kind=kLoop, calls=%fused_computation.23 | loop fusion | flops 131072 | bytes 1048576 | tf_op jit(solution)/shard_map/stack | solution.py:141
  3.3 0.1 pad_maximum_fusion.1
  3.4 5.2 %collective-permute-start = (f32[2,8,4,2048]{3,2,1,0:T(4,128)S(1)}, f32[2,8,4,2048]{3,2,1,0:T(4,128)S(1)}, u32[]{:S(2)}, u32[]{:S(2)}) collective-permute-start(f32[2,8,4,2048]{3,2,1,0:T(4,128)S(1)} %pad_maximum_fusion.1), channel_id=1, source_target_pairs={{0,1},{1,2},{2,3},{4,5},{5,6},{6,7},{8,9},{9,10},{10,11},{12,13},{... | collective-permute-start | bytes 1572872 | tf_op jit(solution)/shard_map/ppermute | solution.py:142
  8.7 1.9 %collective-permute-start.1 = (f32[2,8,4,2048]{3,2,1,0:T(4,128)S(1)}, f32[2,8,4,2048]{3,2,1,0:T(4,128)S(1)}, u32[]{:S(2)}, u32[]{:S(2)}) collective-permute-start(f32[2,8,4,2048]{3,2,1,0:T(4,128)S(1)} %pad_maximum_fusion.2), channel_id=1, source_target_pairs={{1,0},{2,1},{3,2},{5,4},{6,5},{7,6},{9,8},{10,9},{11,10},{13,12},{... | collective-permute-start | bytes 1572872 | tf_op jit(solution)/shard_map/ppermute | solution.py:143
  10.7 4.0 %collective-permute-done.top_ref = f32[2,8,4,2048]{3,2,1,0:T(4,128)S(1)} collective-permute-done((f32[2,8,4,2048]{3,2,1,0:T(4,128)S(1)}, f32[2,8,4,2048]{3,2,1,0:T(4,128)S(1)}, u32[]{:S(2)}, u32[]{:S(2)}) %collective-permute-start) | collective-permute-done | bytes 524320 | tf_op jit(solution)/shard_map/ppermute | solution.py:142
  14.7 6.0 %collective-permute-done.1.bot_ref = f32[2,8,4,2048]{3,2,1,0:T(4,128)S(1)} collective-permute-done((f32[2,8,4,2048]{3,2,1,0:T(4,128)S(1)}, f32[2,8,4,2048]{3,2,1,0:T(4,128)S(1)}, u32[]{:S(2)}, u32[]{:S(2)}) %collective-permute-start.1) | collective-permute-done | bytes 524320 | tf_op jit(solution)/shard_map/ppermute | solution.py:143
  20.8 0.8 copy-done.2
  21.5 14.2 %shard_map.50 = f32[32,8,16,128]{3,2,1,0:T(8,128)} custom-call(f32[8,32,2048]{2,1,0:T(8,128)} %ph_ref.1, s32[8,32,2048]{2,1,0:T(8,128)} %wt_ref.1, f32[2,8,4,2048]{3,2,1,0:T(4,128)} %copy-done.1, f32[2,8,4,2048]{3,2,1,0:T(4,128)} %copy-done.2), custom_call_target="tpu_custom_call" | custom-call | flops 78643200 | bytes 7340032 | tf_op jit(solution)/shard_map/pallas_call | solution.py:93
  35.7 8.2 %all-to-all-start = ((f32[32,8,16,128]{3,2,1,0:T(8,128)}), f32[32,8,16,128]{3,2,1,0:T(8,128)S(1)}, u32[]{:S(2)}, u32[]{:S(2)}) async-start(f32[32,8,16,128]{3,2,1,0:T(8,128)} %shard_map.50), calls=%async_computation | async-start | bytes 4194304 | tf_op jit(solution)/shard_map/all_to_all | solution.py:145
  43.9 0.2 fusion.14
  44.3 8.7 %cholesky.16 = f32[95,95]{1,0:T(8,128)S(1)} custom-call(f32[95,95]{1,0:T(8,128)S(1)} %fusion.34), custom_call_target="Cholesky" | custom-call | tf_op jit(solution)/shard_map/jit(cholesky)/cholesky | solution.py:129
  53.0 0.6 compare_reduce_fusion
  53.7 0.7 fusion.21
  54.3 7.3 %custom-call.10 = f32[1,95,95]{1,2,0:T(8,128)S(1)} custom-call(f32[1,95,95]{2,1,0:T(8,128)S(1)} %fusion.21), custom_call_target="InvertDiagBlocksLowerTriangular" | custom-call | tf_op jit(solution)/shard_map/jit(_cho_solve)/triangular_solve | solution.py:130
  61.6 0.3 fusion.13
  61.9 0.2 fusion.31
  62.1 1.9 %all-to-all-done = f32[32,8,16,128]{3,2,1,0:T(8,128)S(1)} async-done(((f32[32,8,16,128]{3,2,1,0:T(8,128)}), f32[32,8,16,128]{3,2,1,0:T(8,128)S(1)}, u32[]{:S(2)}, u32[]{:S(2)}) %all-to-all-start) | async-done | bytes 2097184 | tf_op jit(solution)/shard_map/all_to_all | solution.py:145
  64.1 3.7 %reshape.23 = f32[256,16,2,64]{3,2,1,0:T(2,128)} reshape(f32[32,8,16,128]{3,2,1,0:T(8,128)S(1)} %all-to-all-done) | data formatting | bytes 4194304 | tf_op jit(solution)/shard_map/reshape | solution.py:147
  67.7 5.4 %copy.8 = f32[256,2,16,64]{0,3,2,1:T(8,128)S(1)} copy(f32[256,2,16,64]{3,1,2,0:T(2,128)} %bitcast.38) | data formatting | bytes 4194304 | tf_op jit(solution)/shard_map/transpose | solution.py:147
  73.1 1.9 %fusion.40 = f32[95,2048]{0,1:S(1)} fusion(f32[95,256]{1,0:T(8,128)S(1)} %fusion.31, f32[256,2048]{0,1:T(8,128)S(1)} %bitcast.37), kind=kOutput, calls=%fused_computation.61 | convolution fusion | flops 597688320 | bytes 2972672
  75.0 1.8 %fusion.9 = f32[256,2048]{0,1:S(1)} fusion(f32[95,2048]{0,1:S(1)} %fusion.40, s32[256]{0:T(256)S(1)} %bitcast.46, s32[256]{0:T(256)S(1)} %bitcast.43), kind=kOutput, calls=%fused_computation.19 | convolution fusion | flops 597834240 | bytes 2877440
  76.8 0.5 bitcast_subtract_fusion
  77.3 3.8 %collective-permute-start.2 = (f32[256,2,64]{0,2,1:T(8,128)S(1)}, f32[256,2,64]{0,2,1:T(8,128)S(1)}, u32[]{:S(2)}, u32[]{:S(2)}) collective-permute-start(f32[256,2,64]{0,2,1:T(8,128)S(1)} %get-tuple-element.4), channel_id=1, source_target_pairs={{0,1},{1,2},{2,3},{4,5},{5,6},{6,7},{8,9},{9,10},{10,11},{12,13},{... | collective-permute-start | bytes 393224 | tf_op jit(solution)/shard_map/ppermute | solution.py:24
  81.1 1.9 %collective-permute-start.3 = (f32[256,2,64]{0,2,1:T(8,128)S(1)}, f32[256,2,64]{0,2,1:T(8,128)S(1)}, u32[]{:S(2)}, u32[]{:S(2)}) collective-permute-start(f32[256,2,64]{0,2,1:T(8,128)S(1)} %get-tuple-element.5), channel_id=1, source_target_pairs={{1,0},{2,1},{3,2},{5,4},{6,5},{7,6},{9,8},{10,9},{11,10},{13,12},{... | collective-permute-start | bytes 393224 | tf_op jit(solution)/shard_map/ppermute | solution.py:27
  83.1 5.9 %collective-permute-done.3 = f32[256,2,64]{0,2,1:T(8,128)S(1)} collective-permute-done((f32[256,2,64]{0,2,1:T(8,128)S(1)}, f32[256,2,64]{0,2,1:T(8,128)S(1)}, u32[]{:S(2)}, u32[]{:S(2)}) %collective-permute-start.3) | collective-permute-done | bytes 131104 | tf_op jit(solution)/shard_map/ppermute | solution.py:27
  89.0 2.4 %collective-permute-start.4 = (f32[256,36,2]{0,2,1:T(2,128)S(1)}, f32[256,36,2]{0,2,1:T(2,128)S(1)}, u32[]{:S(2)}, u32[]{:S(2)}) collective-permute-start(f32[256,36,2]{0,2,1:T(2,128)S(1)} %get-tuple-element.2), channel_id=1, source_target_pairs={{0,4},{4,8},{8,12},{12,16},{16,20},{20,24},{24,28},{28,32},{32,36}... | collective-permute-start | bytes 221192 | tf_op jit(solution)/shard_map/ppermute | solution.py:24
  91.4 5.9 %collective-permute-start.5 = (f32[256,36,2]{0,2,1:T(2,128)S(1)}, f32[256,36,2]{0,2,1:T(2,128)S(1)}, u32[]{:S(2)}, u32[]{:S(2)}) collective-permute-start(f32[256,36,2]{0,2,1:T(2,128)S(1)} %get-tuple-element.3), channel_id=1, source_target_pairs={{4,0},{8,4},{12,8},{16,12},{20,16},{24,20},{28,24},{32,28},{36,32}... | collective-permute-start | bytes 221192 | tf_op jit(solution)/shard_map/ppermute | solution.py:27
  97.3 1.4 %collective-permute-done.5 = f32[256,36,2]{0,2,1:T(2,128)S(1)} collective-permute-done((f32[256,36,2]{0,2,1:T(2,128)S(1)}, f32[256,36,2]{0,2,1:T(2,128)S(1)}, u32[]{:S(2)}, u32[]{:S(2)}) %collective-permute-start.5) | collective-permute-done | bytes 73760 | tf_op jit(solution)/shard_map/ppermute | solution.py:27
  98.7 0.3 pad_maximum_fusion
  99.0 0.5 fusion
  99.5 2.1 %fusion.5 = bf16[256,32,64]{0,2,1:T(8,128)(2,1)} fusion(f32[256,32,68]{0,2,1:T(8,128)S(1)} %fusion), kind=kLoop, calls=%fused_computation.11 | loop fusion | flops 4718592 | bytes 11534336 | tf_op jit(solution)/shard_map/convert_element_type | solution.py:154
  (16 shorter events, 0.4 us)
Async XLA Ops:
  3.4 11.3 %collective-permute-start = (f32[2,8,4,2048]{3,2,1,0:T(4,128)S(1)}, f32[2,8,4,2048]{3,2,1,0:T(4,128)S(1)}, u32[]{:S(2)}, u32[]{:S(2)}) collective-permute-start(f32[2,8,4,2048]{3,2,1,0:T(4,128)S(1)} %pad_maximum_fusion.1), channel_id=1, source_target_pairs={{0,1},{1,2},{2,3},{4,5},{5,6},{6,7},{8,9},{9,10},{10,11},{12,13},{... | collective-permute-start | bytes 1572872 | tf_op jit(solution)/shard_map/ppermute | solution.py:142
  8.7 12.0 %collective-permute-start.1 = (f32[2,8,4,2048]{3,2,1,0:T(4,128)S(1)}, f32[2,8,4,2048]{3,2,1,0:T(4,128)S(1)}, u32[]{:S(2)}, u32[]{:S(2)}) collective-permute-start(f32[2,8,4,2048]{3,2,1,0:T(4,128)S(1)} %pad_maximum_fusion.2), channel_id=1, source_target_pairs={{1,0},{2,1},{3,2},{5,4},{6,5},{7,6},{9,8},{10,9},{11,10},{13,12},{... | collective-permute-start | bytes 1572872 | tf_op jit(solution)/shard_map/ppermute | solution.py:143
  14.7 6.0 %copy-start.1 = (f32[2,8,4,2048]{3,2,1,0:T(4,128)}, f32[2,8,4,2048]{3,2,1,0:T(4,128)S(1)}, u32[]{:S(2)}) copy-start(f32[2,8,4,2048]{3,2,1,0:T(4,128)S(1)} %collective-permute-done.top_ref) | copy-start | bytes 1572868
  20.8 0.8 copy-start.2
  35.7 8.2 %copy-start.3 = (s32[256,2]{0,1:T(2,128)S(1)}, s32[256,2]{0,1:T(2,128)}, u32[]{:S(2)}) copy-start(s32[256,2]{0,1:T(2,128)} %param.5) | copy-start | bytes 6148
  35.7 28.3 %all-to-all-start = ((f32[32,8,16,128]{3,2,1,0:T(8,128)}), f32[32,8,16,128]{3,2,1,0:T(8,128)S(1)}, u32[]{:S(2)}, u32[]{:S(2)}) async-start(f32[32,8,16,128]{3,2,1,0:T(8,128)} %shard_map.50), calls=%async_computation | async-start | bytes 4194304 | tf_op jit(solution)/shard_map/all_to_all | solution.py:145
  75.0 2.3 %copy-start = (f32[95,2048]{0,1}, f32[95,2048]{0,1:S(1)}, u32[]{:S(2)}) copy-start(f32[95,2048]{0,1:S(1)} %fusion.40) | copy-start | bytes 2334724
  77.3 5.7 %collective-permute-start.2 = (f32[256,2,64]{0,2,1:T(8,128)S(1)}, f32[256,2,64]{0,2,1:T(8,128)S(1)}, u32[]{:S(2)}, u32[]{:S(2)}) collective-permute-start(f32[256,2,64]{0,2,1:T(8,128)S(1)} %get-tuple-element.4), channel_id=1, source_target_pairs={{0,1},{1,2},{2,3},{4,5},{5,6},{6,7},{8,9},{9,10},{10,11},{12,13},{... | collective-permute-start | bytes 393224 | tf_op jit(solution)/shard_map/ppermute | solution.py:24
  81.1 7.8 %collective-permute-start.3 = (f32[256,2,64]{0,2,1:T(8,128)S(1)}, f32[256,2,64]{0,2,1:T(8,128)S(1)}, u32[]{:S(2)}, u32[]{:S(2)}) collective-permute-start(f32[256,2,64]{0,2,1:T(8,128)S(1)} %get-tuple-element.5), channel_id=1, source_target_pairs={{1,0},{2,1},{3,2},{5,4},{6,5},{7,6},{9,8},{10,9},{11,10},{13,12},{... | collective-permute-start | bytes 393224 | tf_op jit(solution)/shard_map/ppermute | solution.py:27
  89.0 8.3 %collective-permute-start.4 = (f32[256,36,2]{0,2,1:T(2,128)S(1)}, f32[256,36,2]{0,2,1:T(2,128)S(1)}, u32[]{:S(2)}, u32[]{:S(2)}) collective-permute-start(f32[256,36,2]{0,2,1:T(2,128)S(1)} %get-tuple-element.2), channel_id=1, source_target_pairs={{0,4},{4,8},{8,12},{12,16},{16,20},{20,24},{24,28},{28,32},{32,36}... | collective-permute-start | bytes 221192 | tf_op jit(solution)/shard_map/ppermute | solution.py:24
  91.4 7.3 %collective-permute-start.5 = (f32[256,36,2]{0,2,1:T(2,128)S(1)}, f32[256,36,2]{0,2,1:T(2,128)S(1)}, u32[]{:S(2)}, u32[]{:S(2)}) collective-permute-start(f32[256,36,2]{0,2,1:T(2,128)S(1)} %get-tuple-element.3), channel_id=1, source_target_pairs={{4,0},{8,4},{12,8},{16,12},{20,16},{24,20},{28,24},{32,28},{36,32}... | collective-permute-start | bytes 221192 | tf_op jit(solution)/shard_map/ppermute | solution.py:27

commit v4 on v3

--- a/solution.py
+++ b/solution.py
@@ -62,8 +62,13 @@
     w_lt = pltpu.roll(w_rt, 1, 1)
     den = ((w_up + w_dn) + w_lt) + w_rt
     den = jnp.where(den > 0.0, den, 1.0)
-    cur = zero
-    for _ in range(SWEEPS):
+    inv = 1.0 / den
+    num = w_up * g_up
+    num = num - w_dn * g_dn
+    num = num + w_lt * g_lt
+    num = num - w_rt * g_rt
+    cur = num * inv
+    for _ in range(SWEEPS - 1):
         c_up = pltpu.roll(cur, 1, 0)
         c_dn = pltpu.roll(cur, nr - 1, 0)
         c_lt = pltpu.roll(cur, 1, 1)
@@ -72,7 +77,7 @@
         num = num + w_dn * (c_dn - g_dn)
         num = num + w_lt * (c_lt + g_lt)
         num = num + w_rt * (c_rt - g_rt)
-        cur = num / den
+        cur = num * inv
     cur_ref[...] = cur
     half = rows_out // 2
     upper = cur_ref[pl.ds(HALO, half), :]

time: 103 us -> 102 us (level)
  no operation moved by 1% of the time
where the time goes in v4:
time: 102 us
  starting transfers between devices  29.3 us (29%)
  other arithmetic  22.3 us (22%)
  waiting for transfers between devices  19.2 us (19%)
  Pallas kernels  14.1 us (14%)
  local copies, waits for them, and re-layouts  11.3 us (11%)
  matrix products  4.46 us (4%)
    pallas_call x1, Pallas kernels, unwrap(): pl.pallas_call(functools.partial(unwrap_kernel, rows_out), grid=(n,), in_...  14.1 us
    another operation x3, other arithmetic, network_maps(): factor = jnp.linalg.cholesky(normal_matrix)  9.36 us
    all_to_all x1, starting transfers between devices, on_device(): lax.all_to_all(current, 'ifg', split_axis=0, concat_axis=0, tiled=True)  8.16 us
    another operation x2, other arithmetic, network_maps(): pseudo = jax.scipy.linalg.cho_solve((factor, True), design.T)  7.94 us
    ppermute x2, starting transfers between devices, extended_2(): lax.ppermute(lax.slice_in_dim(block, 0, width, axis=dim), axis, backward)  7.82 us
    ppermute x2, waiting for transfers between devices, extended_2(): lax.ppermute(lax.slice_in_dim(block, 0, width, axis=dim), axis, backward)  7.23 us
    ppermute x2, starting transfers between devices, extended_2(): lax.ppermute(lax.slice_in_dim(block, block.shape[dim] - width, None, axis...  6.2 us
    ppermute x1, waiting for transfers between devices, on_device(): bottom = lax.ppermute(edge_high, 'rows', backward)  6.03 us
  transfers between devices with their start and end apart: 7, of which 5 were waited for; matrix products, arithmetic and copies ran while one was open for 18% of the time, Pallas kernels for 0%

profile of v4, /device:TPU:9, one launch (start us, length us, event | category | flops | bytes accessed | tf_op | source)
XLA Modules:
  0.0 101.6 jit_solution(3743150341226774703)
XLA Ops:
  0.6 1.3 %slice_bitcast_fusion = (f32[1,8,4,2048]{3,2,1,0:T(4,128)S(1)}, f32[1,8,4,2048]{3,2,1,0:T(4,128)S(1)}) fusion(f32[8,32,2048]{2,1,0:T(8,128)} %ph_ref.1), kind=kLoop, calls=%fused_computation.24 | loop fusion | bytes 1048576 | tf_op jit(solution)/shard_map/stack | solution.py:146
  1.9 1.3 %convert_bitcast_fusion = (f32[1,8,4,2048]{3,2,1,0:T(4,128)S(1)}, f32[1,8,4,2048]{3,2,1,0:T(4,128)S(1)}) fusion(s32[8,32,2048]{2,1,0:T(8,128)} %wt_ref.1), kind=kLoop, calls=%fused_computation.23 | loop fusion | flops 131072 | bytes 1048576 | tf_op jit(solution)/shard_map/stack | solution.py:146
  3.3 0.1 pad_maximum_fusion.1
  3.4 5.2 %collective-permute-start = (f32[2,8,4,2048]{3,2,1,0:T(4,128)S(1)}, f32[2,8,4,2048]{3,2,1,0:T(4,128)S(1)}, u32[]{:S(2)}, u32[]{:S(2)}) collective-permute-start(f32[2,8,4,2048]{3,2,1,0:T(4,128)S(1)} %pad_maximum_fusion.1), channel_id=1, source_target_pairs={{0,1},{1,2},{2,3},{4,5},{5,6},{6,7},{8,9},{9,10},{10,11},{12,13},{... | collective-permute-start | bytes 1572872 | tf_op jit(solution)/shard_map/ppermute | solution.py:147
  8.7 1.9 %collective-permute-start.1 = (f32[2,8,4,2048]{3,2,1,0:T(4,128)S(1)}, f32[2,8,4,2048]{3,2,1,0:T(4,128)S(1)}, u32[]{:S(2)}, u32[]{:S(2)}) collective-permute-start(f32[2,8,4,2048]{3,2,1,0:T(4,128)S(1)} %pad_maximum_fusion.2), channel_id=1, source_target_pairs={{1,0},{2,1},{3,2},{5,4},{6,5},{7,6},{9,8},{10,9},{11,10},{13,12},{... | collective-permute-start | bytes 1572872 | tf_op jit(solution)/shard_map/ppermute | solution.py:148
  10.7 4.0 %collective-permute-done.top_ref = f32[2,8,4,2048]{3,2,1,0:T(4,128)S(1)} collective-permute-done((f32[2,8,4,2048]{3,2,1,0:T(4,128)S(1)}, f32[2,8,4,2048]{3,2,1,0:T(4,128)S(1)}, u32[]{:S(2)}, u32[]{:S(2)}) %collective-permute-start) | collective-permute-done | bytes 524320 | tf_op jit(solution)/shard_map/ppermute | solution.py:147
  14.7 6.0 %collective-permute-done.1.bot_ref = f32[2,8,4,2048]{3,2,1,0:T(4,128)S(1)} collective-permute-done((f32[2,8,4,2048]{3,2,1,0:T(4,128)S(1)}, f32[2,8,4,2048]{3,2,1,0:T(4,128)S(1)}, u32[]{:S(2)}, u32[]{:S(2)}) %collective-permute-start.1) | collective-permute-done | bytes 524320 | tf_op jit(solution)/shard_map/ppermute | solution.py:148
  20.8 0.8 copy-done.2
  21.5 14.1 %shard_map.50 = f32[32,8,16,128]{3,2,1,0:T(8,128)} custom-call(f32[8,32,2048]{2,1,0:T(8,128)} %ph_ref.1, s32[8,32,2048]{2,1,0:T(8,128)} %wt_ref.1, f32[2,8,4,2048]{3,2,1,0:T(4,128)} %copy-done.1, f32[2,8,4,2048]{3,2,1,0:T(4,128)} %copy-done.2), custom_call_target="tpu_custom_call" | custom-call | flops 78643200 | bytes 7340032 | tf_op jit(solution)/shard_map/pallas_call | solution.py:98
  35.7 8.2 %all-to-all-start = ((f32[32,8,16,128]{3,2,1,0:T(8,128)}), f32[32,8,16,128]{3,2,1,0:T(8,128)S(1)}, u32[]{:S(2)}, u32[]{:S(2)}) async-start(f32[32,8,16,128]{3,2,1,0:T(8,128)} %shard_map.50), calls=%async_computation | async-start | bytes 4194304 | tf_op jit(solution)/shard_map/all_to_all | solution.py:150
  43.9 0.3 fusion.14
  44.2 8.7 %cholesky.16 = f32[95,95]{1,0:T(8,128)S(1)} custom-call(f32[95,95]{1,0:T(8,128)S(1)} %fusion.34), custom_call_target="Cholesky" | custom-call | tf_op jit(solution)/shard_map/jit(cholesky)/cholesky | solution.py:134
  53.0 0.6 compare_reduce_fusion
  53.6 0.7 fusion.21
  54.3 7.3 %custom-call.10 = f32[1,95,95]{1,2,0:T(8,128)S(1)} custom-call(f32[1,95,95]{2,1,0:T(8,128)S(1)} %fusion.21), custom_call_target="InvertDiagBlocksLowerTriangular" | custom-call | tf_op jit(solution)/shard_map/jit(_cho_solve)/triangular_solve | solution.py:135
  61.5 0.3 fusion.13
  61.8 0.2 fusion.31
  62.1 1.9 %all-to-all-done = f32[32,8,16,128]{3,2,1,0:T(8,128)S(1)} async-done(((f32[32,8,16,128]{3,2,1,0:T(8,128)}), f32[32,8,16,128]{3,2,1,0:T(8,128)S(1)}, u32[]{:S(2)}, u32[]{:S(2)}) %all-to-all-start) | async-done | bytes 2097184 | tf_op jit(solution)/shard_map/all_to_all | solution.py:150
  64.0 3.7 %reshape.23 = f32[256,16,2,64]{3,2,1,0:T(2,128)} reshape(f32[32,8,16,128]{3,2,1,0:T(8,128)S(1)} %all-to-all-done) | data formatting | bytes 4194304 | tf_op jit(solution)/shard_map/reshape | solution.py:152
  67.6 5.4 %copy.8 = f32[256,2,16,64]{0,3,2,1:T(8,128)S(1)} copy(f32[256,2,16,64]{3,1,2,0:T(2,128)} %bitcast.38) | data formatting | bytes 4194304 | tf_op jit(solution)/shard_map/transpose | solution.py:152
  73.0 1.9 %fusion.40 = f32[95,2048]{0,1:S(1)} fusion(f32[95,256]{1,0:T(8,128)S(1)} %fusion.31, f32[256,2048]{0,1:T(8,128)S(1)} %bitcast.37), kind=kOutput, calls=%fused_computation.61 | convolution fusion | flops 597688320 | bytes 2972672
  74.9 1.8 %fusion.9 = f32[256,2048]{0,1:S(1)} fusion(f32[95,2048]{0,1:S(1)} %fusion.40, s32[256]{0:T(256)S(1)} %bitcast.46, s32[256]{0:T(256)S(1)} %bitcast.43), kind=kOutput, calls=%fused_computation.19 | convolution fusion | flops 597834240 | bytes 2877440
  76.8 0.5 bitcast_subtract_fusion
  77.3 3.8 %collective-permute-start.2 = (f32[256,2,64]{0,2,1:T(8,128)S(1)}, f32[256,2,64]{0,2,1:T(8,128)S(1)}, u32[]{:S(2)}, u32[]{:S(2)}) collective-permute-start(f32[256,2,64]{0,2,1:T(8,128)S(1)} %get-tuple-element.4), channel_id=1, source_target_pairs={{0,1},{1,2},{2,3},{4,5},{5,6},{6,7},{8,9},{9,10},{10,11},{12,13},{... | collective-permute-start | bytes 393224 | tf_op jit(solution)/shard_map/ppermute | solution.py:24
  81.1 1.9 %collective-permute-start.3 = (f32[256,2,64]{0,2,1:T(8,128)S(1)}, f32[256,2,64]{0,2,1:T(8,128)S(1)}, u32[]{:S(2)}, u32[]{:S(2)}) collective-permute-start(f32[256,2,64]{0,2,1:T(8,128)S(1)} %get-tuple-element.5), channel_id=1, source_target_pairs={{1,0},{2,1},{3,2},{5,4},{6,5},{7,6},{9,8},{10,9},{11,10},{13,12},{... | collective-permute-start | bytes 393224 | tf_op jit(solution)/shard_map/ppermute | solution.py:27
  83.0 5.9 %collective-permute-done.3 = f32[256,2,64]{0,2,1:T(8,128)S(1)} collective-permute-done((f32[256,2,64]{0,2,1:T(8,128)S(1)}, f32[256,2,64]{0,2,1:T(8,128)S(1)}, u32[]{:S(2)}, u32[]{:S(2)}) %collective-permute-start.3) | collective-permute-done | bytes 131104 | tf_op jit(solution)/shard_map/ppermute | solution.py:27
  88.9 2.4 %collective-permute-start.4 = (f32[256,36,2]{0,2,1:T(2,128)S(1)}, f32[256,36,2]{0,2,1:T(2,128)S(1)}, u32[]{:S(2)}, u32[]{:S(2)}) collective-permute-start(f32[256,36,2]{0,2,1:T(2,128)S(1)} %get-tuple-element.2), channel_id=1, source_target_pairs={{0,4},{4,8},{8,12},{12,16},{16,20},{20,24},{24,28},{28,32},{32,36}... | collective-permute-start | bytes 221192 | tf_op jit(solution)/shard_map/ppermute | solution.py:24
  91.3 5.9 %collective-permute-start.5 = (f32[256,36,2]{0,2,1:T(2,128)S(1)}, f32[256,36,2]{0,2,1:T(2,128)S(1)}, u32[]{:S(2)}, u32[]{:S(2)}) collective-permute-start(f32[256,36,2]{0,2,1:T(2,128)S(1)} %get-tuple-element.3), channel_id=1, source_target_pairs={{4,0},{8,4},{12,8},{16,12},{20,16},{24,20},{28,24},{32,28},{36,32}... | collective-permute-start | bytes 221192 | tf_op jit(solution)/shard_map/ppermute | solution.py:27
  97.2 1.4 %collective-permute-done.5 = f32[256,36,2]{0,2,1:T(2,128)S(1)} collective-permute-done((f32[256,36,2]{0,2,1:T(2,128)S(1)}, f32[256,36,2]{0,2,1:T(2,128)S(1)}, u32[]{:S(2)}, u32[]{:S(2)}) %collective-permute-start.5) | collective-permute-done | bytes 73760 | tf_op jit(solution)/shard_map/ppermute | solution.py:27
  98.6 0.3 pad_maximum_fusion
  98.9 0.5 fusion
  99.4 2.1 %fusion.5 = bf16[256,32,64]{0,2,1:T(8,128)(2,1)} fusion(f32[256,32,68]{0,2,1:T(8,128)S(1)} %fusion), kind=kLoop, calls=%fused_computation.11 | loop fusion | flops 4718592 | bytes 11534336 | tf_op jit(solution)/shard_map/convert_element_type | solution.py:159
  (16 shorter events, 0.4 us)
Async XLA Ops:
  3.4 11.3 %collective-permute-start = (f32[2,8,4,2048]{3,2,1,0:T(4,128)S(1)}, f32[2,8,4,2048]{3,2,1,0:T(4,128)S(1)}, u32[]{:S(2)}, u32[]{:S(2)}) collective-permute-start(f32[2,8,4,2048]{3,2,1,0:T(4,128)S(1)} %pad_maximum_fusion.1), channel_id=1, source_target_pairs={{0,1},{1,2},{2,3},{4,5},{5,6},{6,7},{8,9},{9,10},{10,11},{12,13},{... | collective-permute-start | bytes 1572872 | tf_op jit(solution)/shard_map/ppermute | solution.py:147
  8.7 12.0 %collective-permute-start.1 = (f32[2,8,4,2048]{3,2,1,0:T(4,128)S(1)}, f32[2,8,4,2048]{3,2,1,0:T(4,128)S(1)}, u32[]{:S(2)}, u32[]{:S(2)}) collective-permute-start(f32[2,8,4,2048]{3,2,1,0:T(4,128)S(1)} %pad_maximum_fusion.2), channel_id=1, source_target_pairs={{1,0},{2,1},{3,2},{5,4},{6,5},{7,6},{9,8},{10,9},{11,10},{13,12},{... | collective-permute-start | bytes 1572872 | tf_op jit(solution)/shard_map/ppermute | solution.py:148
  14.7 6.0 %copy-start.1 = (f32[2,8,4,2048]{3,2,1,0:T(4,128)}, f32[2,8,4,2048]{3,2,1,0:T(4,128)S(1)}, u32[]{:S(2)}) copy-start(f32[2,8,4,2048]{3,2,1,0:T(4,128)S(1)} %collective-permute-done.top_ref) | copy-start | bytes 1572868
  20.8 0.8 copy-start.2
  35.7 8.2 %copy-start.3 = (s32[256,2]{0,1:T(2,128)S(1)}, s32[256,2]{0,1:T(2,128)}, u32[]{:S(2)}) copy-start(s32[256,2]{0,1:T(2,128)} %param.5) | copy-start | bytes 6148
  35.7 28.3 %all-to-all-start = ((f32[32,8,16,128]{3,2,1,0:T(8,128)}), f32[32,8,16,128]{3,2,1,0:T(8,128)S(1)}, u32[]{:S(2)}, u32[]{:S(2)}) async-start(f32[32,8,16,128]{3,2,1,0:T(8,128)} %shard_map.50), calls=%async_computation | async-start | bytes 4194304 | tf_op jit(solution)/shard_map/all_to_all | solution.py:150
  74.9 2.3 %copy-start = (f32[95,2048]{0,1}, f32[95,2048]{0,1:S(1)}, u32[]{:S(2)}) copy-start(f32[95,2048]{0,1:S(1)} %fusion.40) | copy-start | bytes 2334724
  77.3 5.7 %collective-permute-start.2 = (f32[256,2,64]{0,2,1:T(8,128)S(1)}, f32[256,2,64]{0,2,1:T(8,128)S(1)}, u32[]{:S(2)}, u32[]{:S(2)}) collective-permute-start(f32[256,2,64]{0,2,1:T(8,128)S(1)} %get-tuple-element.4), channel_id=1, source_target_pairs={{0,1},{1,2},{2,3},{4,5},{5,6},{6,7},{8,9},{9,10},{10,11},{12,13},{... | collective-permute-start | bytes 393224 | tf_op jit(solution)/shard_map/ppermute | solution.py:24
  81.1 7.8 %collective-permute-start.3 = (f32[256,2,64]{0,2,1:T(8,128)S(1)}, f32[256,2,64]{0,2,1:T(8,128)S(1)}, u32[]{:S(2)}, u32[]{:S(2)}) collective-permute-start(f32[256,2,64]{0,2,1:T(8,128)S(1)} %get-tuple-element.5), channel_id=1, source_target_pairs={{1,0},{2,1},{3,2},{5,4},{6,5},{7,6},{9,8},{10,9},{11,10},{13,12},{... | collective-permute-start | bytes 393224 | tf_op jit(solution)/shard_map/ppermute | solution.py:27
  88.9 8.3 %collective-permute-start.4 = (f32[256,36,2]{0,2,1:T(2,128)S(1)}, f32[256,36,2]{0,2,1:T(2,128)S(1)}, u32[]{:S(2)}, u32[]{:S(2)}) collective-permute-start(f32[256,36,2]{0,2,1:T(2,128)S(1)} %get-tuple-element.2), channel_id=1, source_target_pairs={{0,4},{4,8},{8,12},{12,16},{16,20},{20,24},{24,28},{28,32},{32,36}... | collective-permute-start | bytes 221192 | tf_op jit(solution)/shard_map/ppermute | solution.py:24
  91.3 7.3 %collective-permute-start.5 = (f32[256,36,2]{0,2,1:T(2,128)S(1)}, f32[256,36,2]{0,2,1:T(2,128)S(1)}, u32[]{:S(2)}, u32[]{:S(2)}) collective-permute-start(f32[256,36,2]{0,2,1:T(2,128)S(1)} %get-tuple-element.3), channel_id=1, source_target_pairs={{4,0},{8,4},{12,8},{16,12},{20,16},{24,20},{28,24},{32,28},{36,32}... | collective-permute-start | bytes 221192 | tf_op jit(solution)/shard_map/ppermute | solution.py:27

commit v5 on v4

--- a/solution.py
+++ b/solution.py
@@ -67,17 +67,15 @@
     num = num - w_dn * g_dn
     num = num + w_lt * g_lt
     num = num - w_rt * g_rt
-    cur = num * inv
+    const = num * inv
+    a_up, a_dn, a_lt, a_rt = w_up * inv, w_dn * inv, w_lt * inv, w_rt * inv
+    cur = const
     for _ in range(SWEEPS - 1):
-        c_up = pltpu.roll(cur, 1, 0)
-        c_dn = pltpu.roll(cur, nr - 1, 0)
-        c_lt = pltpu.roll(cur, 1, 1)
-        c_rt = pltpu.roll(cur, nc - 1, 1)
-        num = w_up * (c_up + g_up)
-        num = num + w_dn * (c_dn - g_dn)
-        num = num + w_lt * (c_lt + g_lt)
-        num = num + w_rt * (c_rt - g_rt)
-        cur = num * inv
+        nxt = const + a_up * pltpu.roll(cur, 1, 0)
+        nxt = nxt + a_dn * pltpu.roll(cur, nr - 1, 0)
+        nxt = nxt + a_lt * pltpu.roll(cur, 1, 1)
+        nxt = nxt + a_rt * pltpu.roll(cur, nc - 1, 1)
+        cur = nxt
     cur_ref[...] = cur
     half = rows_out // 2
     upper = cur_ref[pl.ds(HALO, half), :]

time: 102 us -> 102 us (level)
  no operation moved by 1% of the time
where the time goes in v5:
time: 102 us; the launch traced here: 101 us
  starting transfers between devices  29.3 us (29%)
  other arithmetic  22.3 us (22%)
  waiting for transfers between devices  19.2 us (19%)
  Pallas kernels  13.2 us (13%)
  local copies, waits for them, and re-layouts  11.3 us (11%)
  matrix products  4.46 us (4%)
    pallas_call x1, Pallas kernels, unwrap(): pl.pallas_call(functools.partial(unwrap_kernel, rows_out), grid=(n,), in_...  13.2 us
    another operation x3, other arithmetic, network_maps(): factor = jnp.linalg.cholesky(normal_matrix)  9.36 us
    all_to_all x1, starting transfers between devices, on_device(): lax.all_to_all(current, 'ifg', split_axis=0, concat_axis=0, tiled=True)  8.16 us
    another operation x2, other arithmetic, network_maps(): pseudo = jax.scipy.linalg.cho_solve((factor, True), design.T)  7.94 us
    ppermute x2, starting transfers between devices, extended_2(): lax.ppermute(lax.slice_in_dim(block, 0, width, axis=dim), axis, backward)  7.82 us
    ppermute x2, waiting for transfers between devices, extended_2(): lax.ppermute(lax.slice_in_dim(block, 0, width, axis=dim), axis, backward)  7.23 us
    ppermute x2, starting transfers between devices, extended_2(): lax.ppermute(lax.slice_in_dim(block, block.shape[dim] - width, None, axis...  6.2 us
    ppermute x1, waiting for transfers between devices, on_device(): bottom = lax.ppermute(edge_high, 'rows', backward)  6.03 us
  transfers between devices with their start and end apart: 7, of which 5 were waited for; matrix products, arithmetic and copies ran while one was open for 18% of the time, Pallas kernels for 0%

profile of v5, /device:TPU:9, one launch (start us, length us, event | category | flops | bytes accessed | tf_op | source)
XLA Modules:
  0.0 100.7 jit_solution(5216372210922635098)
XLA Ops:
  0.6 1.3 %slice_bitcast_fusion = (f32[1,8,4,2048]{3,2,1,0:T(4,128)S(1)}, f32[1,8,4,2048]{3,2,1,0:T(4,128)S(1)}) fusion(f32[8,32,2048]{2,1,0:T(8,128)} %ph_ref.1), kind=kLoop, calls=%fused_computation.24 | loop fusion | bytes 1048576 | tf_op jit(solution)/shard_map/stack | solution.py:144
  1.9 1.3 %convert_bitcast_fusion = (f32[1,8,4,2048]{3,2,1,0:T(4,128)S(1)}, f32[1,8,4,2048]{3,2,1,0:T(4,128)S(1)}) fusion(s32[8,32,2048]{2,1,0:T(8,128)} %wt_ref.1), kind=kLoop, calls=%fused_computation.23 | loop fusion | flops 131072 | bytes 1048576 | tf_op jit(solution)/shard_map/stack | solution.py:144
  3.3 0.1 pad_maximum_fusion.1
  3.4 5.2 %collective-permute-start = (f32[2,8,4,2048]{3,2,1,0:T(4,128)S(1)}, f32[2,8,4,2048]{3,2,1,0:T(4,128)S(1)}, u32[]{:S(2)}, u32[]{:S(2)}) collective-permute-start(f32[2,8,4,2048]{3,2,1,0:T(4,128)S(1)} %pad_maximum_fusion.1), channel_id=1, source_target_pairs={{0,1},{1,2},{2,3},{4,5},{5,6},{6,7},{8,9},{9,10},{10,11},{12,13},{... | collective-permute-start | bytes 1572872 | tf_op jit(solution)/shard_map/ppermute | solution.py:145
  8.7 1.9 %collective-permute-start.1 = (f32[2,8,4,2048]{3,2,1,0:T(4,128)S(1)}, f32[2,8,4,2048]{3,2,1,0:T(4,128)S(1)}, u32[]{:S(2)}, u32[]{:S(2)}) collective-permute-start(f32[2,8,4,2048]{3,2,1,0:T(4,128)S(1)} %pad_maximum_fusion.2), channel_id=1, source_target_pairs={{1,0},{2,1},{3,2},{5,4},{6,5},{7,6},{9,8},{10,9},{11,10},{13,12},{... | collective-permute-start | bytes 1572872 | tf_op jit(solution)/shard_map/ppermute | solution.py:146
  10.7 4.0 %collective-permute-done.top_ref = f32[2,8,4,2048]{3,2,1,0:T(4,128)S(1)} collective-permute-done((f32[2,8,4,2048]{3,2,1,0:T(4,128)S(1)}, f32[2,8,4,2048]{3,2,1,0:T(4,128)S(1)}, u32[]{:S(2)}, u32[]{:S(2)}) %collective-permute-start) | collective-permute-done | bytes 524320 | tf_op jit(solution)/shard_map/ppermute | solution.py:145
  14.7 6.0 %collective-permute-done.1.bot_ref = f32[2,8,4,2048]{3,2,1,0:T(4,128)S(1)} collective-permute-done((f32[2,8,4,2048]{3,2,1,0:T(4,128)S(1)}, f32[2,8,4,2048]{3,2,1,0:T(4,128)S(1)}, u32[]{:S(2)}, u32[]{:S(2)}) %collective-permute-start.1) | collective-permute-done | bytes 524320 | tf_op jit(solution)/shard_map/ppermute | solution.py:146
  20.8 0.8 copy-done.2
  21.5 13.2 %shard_map.50 = f32[32,8,16,128]{3,2,1,0:T(8,128)} custom-call(f32[8,32,2048]{2,1,0:T(8,128)} %ph_ref.1, s32[8,32,2048]{2,1,0:T(8,128)} %wt_ref.1, f32[2,8,4,2048]{3,2,1,0:T(4,128)} %copy-done.1, f32[2,8,4,2048]{3,2,1,0:T(4,128)} %copy-done.2), custom_call_target="tpu_custom_call" | custom-call | flops 78643200 | bytes 7340032 | tf_op jit(solution)/shard_map/pallas_call | solution.py:96
  34.8 8.2 %all-to-all-start = ((f32[32,8,16,128]{3,2,1,0:T(8,128)}), f32[32,8,16,128]{3,2,1,0:T(8,128)S(1)}, u32[]{:S(2)}, u32[]{:S(2)}) async-start(f32[32,8,16,128]{3,2,1,0:T(8,128)} %shard_map.50), calls=%async_computation | async-start | bytes 4194304 | tf_op jit(solution)/shard_map/all_to_all | solution.py:148
  43.0 0.3 fusion.14
  43.3 8.7 %cholesky.16 = f32[95,95]{1,0:T(8,128)S(1)} custom-call(f32[95,95]{1,0:T(8,128)S(1)} %fusion.34), custom_call_target="Cholesky" | custom-call | tf_op jit(solution)/shard_map/jit(cholesky)/cholesky | solution.py:132
  52.1 0.6 compare_reduce_fusion
  52.7 0.7 fusion.21
  53.4 7.3 %custom-call.10 = f32[1,95,95]{1,2,0:T(8,128)S(1)} custom-call(f32[1,95,95]{2,1,0:T(8,128)S(1)} %fusion.21), custom_call_target="InvertDiagBlocksLowerTriangular" | custom-call | tf_op jit(solution)/shard_map/jit(_cho_solve)/triangular_solve | solution.py:133
  60.7 0.3 fusion.13
  61.0 0.2 fusion.31
  61.2 1.9 %all-to-all-done = f32[32,8,16,128]{3,2,1,0:T(8,128)S(1)} async-done(((f32[32,8,16,128]{3,2,1,0:T(8,128)}), f32[32,8,16,128]{3,2,1,0:T(8,128)S(1)}, u32[]{:S(2)}, u32[]{:S(2)}) %all-to-all-start) | async-done | bytes 2097184 | tf_op jit(solution)/shard_map/all_to_all | solution.py:148
  63.1 3.7 %reshape.23 = f32[256,16,2,64]{3,2,1,0:T(2,128)} reshape(f32[32,8,16,128]{3,2,1,0:T(8,128)S(1)} %all-to-all-done) | data formatting | bytes 4194304 | tf_op jit(solution)/shard_map/reshape | solution.py:150
  66.8 5.4 %copy.8 = f32[256,2,16,64]{0,3,2,1:T(8,128)S(1)} copy(f32[256,2,16,64]{3,1,2,0:T(2,128)} %bitcast.38) | data formatting | bytes 4194304 | tf_op jit(solution)/shard_map/transpose | solution.py:150
  72.2 1.9 %fusion.40 = f32[95,2048]{0,1:S(1)} fusion(f32[95,256]{1,0:T(8,128)S(1)} %fusion.31, f32[256,2048]{0,1:T(8,128)S(1)} %bitcast.37), kind=kOutput, calls=%fused_computation.61 | convolution fusion | flops 597688320 | bytes 2972672
  74.0 1.8 %fusion.9 = f32[256,2048]{0,1:S(1)} fusion(f32[95,2048]{0,1:S(1)} %fusion.40, s32[256]{0:T(256)S(1)} %bitcast.46, s32[256]{0:T(256)S(1)} %bitcast.43), kind=kOutput, calls=%fused_computation.19 | convolution fusion | flops 597834240 | bytes 2877440
  75.9 0.5 bitcast_subtract_fusion
  76.4 3.8 %collective-permute-start.2 = (f32[256,2,64]{0,2,1:T(8,128)S(1)}, f32[256,2,64]{0,2,1:T(8,128)S(1)}, u32[]{:S(2)}, u32[]{:S(2)}) collective-permute-start(f32[256,2,64]{0,2,1:T(8,128)S(1)} %get-tuple-element.4), channel_id=1, source_target_pairs={{0,1},{1,2},{2,3},{4,5},{5,6},{6,7},{8,9},{9,10},{10,11},{12,13},{... | collective-permute-start | bytes 393224 | tf_op jit(solution)/shard_map/ppermute | solution.py:24
  80.2 1.9 %collective-permute-start.3 = (f32[256,2,64]{0,2,1:T(8,128)S(1)}, f32[256,2,64]{0,2,1:T(8,128)S(1)}, u32[]{:S(2)}, u32[]{:S(2)}) collective-permute-start(f32[256,2,64]{0,2,1:T(8,128)S(1)} %get-tuple-element.5), channel_id=1, source_target_pairs={{1,0},{2,1},{3,2},{5,4},{6,5},{7,6},{9,8},{10,9},{11,10},{13,12},{... | collective-permute-start | bytes 393224 | tf_op jit(solution)/shard_map/ppermute | solution.py:27
  82.1 5.9 %collective-permute-done.3 = f32[256,2,64]{0,2,1:T(8,128)S(1)} collective-permute-done((f32[256,2,64]{0,2,1:T(8,128)S(1)}, f32[256,2,64]{0,2,1:T(8,128)S(1)}, u32[]{:S(2)}, u32[]{:S(2)}) %collective-permute-start.3) | collective-permute-done | bytes 131104 | tf_op jit(solution)/shard_map/ppermute | solution.py:27
  88.0 2.4 %collective-permute-start.4 = (f32[256,36,2]{0,2,1:T(2,128)S(1)}, f32[256,36,2]{0,2,1:T(2,128)S(1)}, u32[]{:S(2)}, u32[]{:S(2)}) collective-permute-start(f32[256,36,2]{0,2,1:T(2,128)S(1)} %get-tuple-element.2), channel_id=1, source_target_pairs={{0,4},{4,8},{8,12},{12,16},{16,20},{20,24},{24,28},{28,32},{32,36}... | collective-permute-start | bytes 221192 | tf_op jit(solution)/shard_map/ppermute | solution.py:24
  90.4 5.9 %collective-permute-start.5 = (f32[256,36,2]{0,2,1:T(2,128)S(1)}, f32[256,36,2]{0,2,1:T(2,128)S(1)}, u32[]{:S(2)}, u32[]{:S(2)}) collective-permute-start(f32[256,36,2]{0,2,1:T(2,128)S(1)} %get-tuple-element.3), channel_id=1, source_target_pairs={{4,0},{8,4},{12,8},{16,12},{20,16},{24,20},{28,24},{32,28},{36,32}... | collective-permute-start | bytes 221192 | tf_op jit(solution)/shard_map/ppermute | solution.py:27
  96.3 1.4 %collective-permute-done.5 = f32[256,36,2]{0,2,1:T(2,128)S(1)} collective-permute-done((f32[256,36,2]{0,2,1:T(2,128)S(1)}, f32[256,36,2]{0,2,1:T(2,128)S(1)}, u32[]{:S(2)}, u32[]{:S(2)}) %collective-permute-start.5) | collective-permute-done | bytes 73760 | tf_op jit(solution)/shard_map/ppermute | solution.py:27
  97.7 0.3 pad_maximum_fusion
  98.0 0.5 fusion
  98.6 2.1 %fusion.5 = bf16[256,32,64]{0,2,1:T(8,128)(2,1)} fusion(f32[256,32,68]{0,2,1:T(8,128)S(1)} %fusion), kind=kLoop, calls=%fused_computation.11 | loop fusion | flops 4718592 | bytes 11534336 | tf_op jit(solution)/shard_map/convert_element_type | solution.py:157
  (16 shorter events, 0.4 us)
Async XLA Ops:
  3.4 11.3 %collective-permute-start = (f32[2,8,4,2048]{3,2,1,0:T(4,128)S(1)}, f32[2,8,4,2048]{3,2,1,0:T(4,128)S(1)}, u32[]{:S(2)}, u32[]{:S(2)}) collective-permute-start(f32[2,8,4,2048]{3,2,1,0:T(4,128)S(1)} %pad_maximum_fusion.1), channel_id=1, source_target_pairs={{0,1},{1,2},{2,3},{4,5},{5,6},{6,7},{8,9},{9,10},{10,11},{12,13},{... | collective-permute-start | bytes 1572872 | tf_op jit(solution)/shard_map/ppermute | solution.py:145
  8.7 12.0 %collective-permute-start.1 = (f32[2,8,4,2048]{3,2,1,0:T(4,128)S(1)}, f32[2,8,4,2048]{3,2,1,0:T(4,128)S(1)}, u32[]{:S(2)}, u32[]{:S(2)}) collective-permute-start(f32[2,8,4,2048]{3,2,1,0:T(4,128)S(1)} %pad_maximum_fusion.2), channel_id=1, source_target_pairs={{1,0},{2,1},{3,2},{5,4},{6,5},{7,6},{9,8},{10,9},{11,10},{13,12},{... | collective-permute-start | bytes 1572872 | tf_op jit(solution)/shard_map/ppermute | solution.py:146
  14.7 6.0 %copy-start.1 = (f32[2,8,4,2048]{3,2,1,0:T(4,128)}, f32[2,8,4,2048]{3,2,1,0:T(4,128)S(1)}, u32[]{:S(2)}) copy-start(f32[2,8,4,2048]{3,2,1,0:T(4,128)S(1)} %collective-permute-done.top_ref) | copy-start | bytes 1572868
  20.8 0.8 copy-start.2
  34.8 8.2 %copy-start.3 = (s32[256,2]{0,1:T(2,128)S(1)}, s32[256,2]{0,1:T(2,128)}, u32[]{:S(2)}) copy-start(s32[256,2]{0,1:T(2,128)} %param.5) | copy-start | bytes 6148
  34.8 28.3 %all-to-all-start = ((f32[32,8,16,128]{3,2,1,0:T(8,128)}), f32[32,8,16,128]{3,2,1,0:T(8,128)S(1)}, u32[]{:S(2)}, u32[]{:S(2)}) async-start(f32[32,8,16,128]{3,2,1,0:T(8,128)} %shard_map.50), calls=%async_computation | async-start | bytes 4194304 | tf_op jit(solution)/shard_map/all_to_all | solution.py:148
  74.0 2.3 %copy-start = (f32[95,2048]{0,1}, f32[95,2048]{0,1:S(1)}, u32[]{:S(2)}) copy-start(f32[95,2048]{0,1:S(1)} %fusion.40) | copy-start | bytes 2334724
  76.4 5.7 %collective-permute-start.2 = (f32[256,2,64]{0,2,1:T(8,128)S(1)}, f32[256,2,64]{0,2,1:T(8,128)S(1)}, u32[]{:S(2)}, u32[]{:S(2)}) collective-permute-start(f32[256,2,64]{0,2,1:T(8,128)S(1)} %get-tuple-element.4), channel_id=1, source_target_pairs={{0,1},{1,2},{2,3},{4,5},{5,6},{6,7},{8,9},{9,10},{10,11},{12,13},{... | collective-permute-start | bytes 393224 | tf_op jit(solution)/shard_map/ppermute | solution.py:24
  80.2 7.8 %collective-permute-start.3 = (f32[256,2,64]{0,2,1:T(8,128)S(1)}, f32[256,2,64]{0,2,1:T(8,128)S(1)}, u32[]{:S(2)}, u32[]{:S(2)}) collective-permute-start(f32[256,2,64]{0,2,1:T(8,128)S(1)} %get-tuple-element.5), channel_id=1, source_target_pairs={{1,0},{2,1},{3,2},{5,4},{6,5},{7,6},{9,8},{10,9},{11,10},{13,12},{... | collective-permute-start | bytes 393224 | tf_op jit(solution)/shard_map/ppermute | solution.py:27
  88.0 8.3 %collective-permute-start.4 = (f32[256,36,2]{0,2,1:T(2,128)S(1)}, f32[256,36,2]{0,2,1:T(2,128)S(1)}, u32[]{:S(2)}, u32[]{:S(2)}) collective-permute-start(f32[256,36,2]{0,2,1:T(2,128)S(1)} %get-tuple-element.2), channel_id=1, source_target_pairs={{0,4},{4,8},{8,12},{12,16},{16,20},{20,24},{24,28},{28,32},{32,36}... | collective-permute-start | bytes 221192 | tf_op jit(solution)/shard_map/ppermute | solution.py:24
  90.4 7.3 %collective-permute-start.5 = (f32[256,36,2]{0,2,1:T(2,128)S(1)}, f32[256,36,2]{0,2,1:T(2,128)S(1)}, u32[]{:S(2)}, u32[]{:S(2)}) collective-permute-start(f32[256,36,2]{0,2,1:T(2,128)S(1)} %get-tuple-element.3), channel_id=1, source_target_pairs={{4,0},{8,4},{12,8},{16,12},{20,16},{24,20},{28,24},{32,28},{36,32}... | collective-permute-start | bytes 221192 | tf_op jit(solution)/shard_map/ppermute | solution.py:27

commit v6 on v5

--- a/solution.py
+++ b/solution.py
@@ -10,7 +10,8 @@
 
 DATES = 96
 SWEEPS = 4
-HALO = SWEEPS
+FILTER_HALO = 2
+HALO = 8
 PI32 = float(np.float32(np.pi))
 TWO_PI_HI = float(np.float32(2 * np.pi))
 TWO_PI_LO = float(np.float32(2 * np.pi - np.float64(np.float32(2 * np.pi))))
@@ -77,9 +78,9 @@
         nxt = nxt + a_rt * pltpu.roll(cur, nc - 1, 1)
         cur = nxt
     cur_ref[...] = cur
-    half = rows_out // 2
-    upper = cur_ref[pl.ds(HALO, half), :]
-    lower = cur_ref[pl.ds(HALO + half, half), :]
+    half = rows_out // 2 + FILTER_HALO
+    upper = cur_ref[pl.ds(HALO - FILTER_HALO, half), :]
+    lower = cur_ref[pl.ds(HALO - FILTER_HALO + half, half), :]
     lane = lax.broadcasted_iota(jnp.int32, (half, nc), 1) % 128
     first = lane < 64
     even = jnp.where(first, upper, pltpu.roll(lower, 64, 1))
@@ -92,6 +93,7 @@
 def unwrap(phase, weights, top, bottom):
     n, rows_out, nc = phase.shape
     nr = rows_out + 2 * HALO
+    half = rows_out // 2 + FILTER_HALO
     halo_spec = pl.BlockSpec((2, 1, HALO, nc), lambda i: (0, i, 0, 0))
     return pl.pallas_call(
         functools.partial(unwrap_kernel, rows_out),
@@ -102,8 +104,8 @@
             halo_spec,
             halo_spec,
         ],
-        out_specs=pl.BlockSpec((nc // 64, 1, rows_out // 2, 128), lambda i: (0, i, 0, 0)),
-        out_shape=jax.ShapeDtypeStruct((nc // 64, n, rows_out // 2, 128), jnp.float32),
+        out_specs=pl.BlockSpec((nc // 64, 1, half, 128), lambda i: (0, i, 0, 0)),
+        out_shape=jax.ShapeDtypeStruct((nc // 64, n, half, 128), jnp.float32),
         scratch_shapes=[pltpu.VMEM((nr, nc), jnp.float32)] * 3,
         cost_estimate=pl.CostEstimate(
             flops=120 * n * nr * nc, bytes_accessed=4 * n * nc * (2 * nr + rows_out), transcendentals=0
@@ -147,13 +149,15 @@
     current = unwrap(phase, weights, top, bottom)
     received = lax.all_to_all(current, "ifg", split_axis=0, concat_axis=0, tiled=True)
     ifg = received.shape[0] * received.shape[1]
-    block = received.reshape(ifg, rows // 2, 2, 64).transpose(0, 2, 1, 3).reshape(ifg, rows, 64)
+    tall = rows + 2 * FILTER_HALO
+    block = received.reshape(ifg, tall // 2, 2, 64).transpose(0, 2, 1, 3).reshape(ifg, tall, 64)
     series_block = jnp.einsum("ei,irc->erc", pseudo, block, precision=lax.Precision.HIGHEST)
     residual = block - jnp.einsum(
         "ie,erc->irc", design, series_block, precision=lax.Precision.HIGHEST
     )
-    padded = extended_2(residual, (("rows", 1), ("ifg", 2)), 2)
+    padded = extended_2(residual, (("ifg", 2),), FILTER_HALO)
     filtered = binomial(binomial(padded, 1), 2)
+    series_block = series_block[:, FILTER_HALO : FILTER_HALO + rows]
     return (series_block, filtered.astype(jnp.bfloat16))
 
 

time: 102 us -> 103 us (level)
  local copies, waits for them, and re-layouts: 11.3 us -> 19.8 us
  starting transfers between devices: 29.3 us -> 23.6 us
  Pallas kernels: 13.2 us -> 15.4 us
  waiting for transfers between devices: 19.2 us -> 17.1 us
  other arithmetic: 22.3 us -> 21 us
    ppermute x2 -> x1, waiting for transfers between devices: 7.23 us -> 0.34 us  [extended_2(): lax.ppermute(lax.slice_in_dim(block, 0, width, axis=dim), axis, backward)]
    ppermute x1, waiting for transfers between devices: 4.04 us -> 9.69 us  [on_device(): top = lax.ppermute(edge_low, 'rows', forward)]
    pallas_call x0 -> x1, local copies, waits for them, and re-layouts: none -> 3.81 us  [unwrap(): pl.pallas_call(functools.partial(unwrap_kernel, rows_out), grid=(n,), in_...]
    ppermute x2 -> x1, starting transfers between devices: 6.2 us -> 2.47 us  [extended_2(): lax.ppermute(lax.slice_in_dim(block, block.shape[dim] - width, None, axis...]
    pallas_call x1, Pallas kernels: 13.2 us -> 15.4 us  [unwrap(): pl.pallas_call(functools.partial(unwrap_kernel, rows_out), grid=(n,), in_...]
    ppermute x2 -> x1, starting transfers between devices: 7.82 us -> 5.82 us  [extended_2(): lax.ppermute(lax.slice_in_dim(block, 0, width, axis=dim), axis, backward)]
    all_to_all x0 -> x1, local copies, waits for them, and re-layouts: none -> 1.9 us  [on_device(): lax.all_to_all(current, 'ifg', split_axis=0, concat_axis=0, tiled=True)]
    another operation x2, other arithmetic: 1.44 us -> 0.17 us  [on_device(): jnp.stack([phase[:, :HALO], weights[:, :HALO].astype(jnp.float32)])]
  transfers between devices with their start and end apart: 7 -> 5, of which waited for: 5 -> 4; matrix products, arithmetic and copies ran while one was open for 18% -> 19% of each run, Pallas kernels for 0% -> 0%
where the time goes in v6:
time: 103 us
  starting transfers between devices  23.6 us (23%)
  other arithmetic  21 us (20%)
  local copies, waits for them, and re-layouts  19.8 us (19%)
  waiting for transfers between devices  17.1 us (17%)
  Pallas kernels  15.4 us (15%)
  matrix products  4.87 us (5%)
    pallas_call x1, Pallas kernels, unwrap(): pl.pallas_call(functools.partial(unwrap_kernel, rows_out), grid=(n,), in_...  15.4 us
    ppermute x1, waiting for transfers between devices, on_device(): top = lax.ppermute(edge_low, 'rows', forward)  9.69 us
    another operation x3, other arithmetic, network_maps(): factor = jnp.linalg.cholesky(normal_matrix)  9.36 us
    all_to_all x1, starting transfers between devices, on_device(): lax.all_to_all(current, 'ifg', split_axis=0, concat_axis=0, tiled=True)  8.21 us
    another operation x2, other arithmetic, network_maps(): pseudo = jax.scipy.linalg.cho_solve((factor, True), design.T)  7.94 us
    ppermute x1, waiting for transfers between devices, on_device(): bottom = lax.ppermute(edge_high, 'rows', backward)  6 us
    transpose x1, local copies, waits for them, and re-layouts, on_device(): received.reshape(ifg, tall // 2, 2, 64).transpose(0, 2, 1, 3)  5.94 us
    ppermute x1, starting transfers between devices, extended_2(): lax.ppermute(lax.slice_in_dim(block, 0, width, axis=dim), axis, backward)  5.82 us
  transfers between devices with their start and end apart: 5, of which 4 were waited for; matrix products, arithmetic and copies ran while one was open for 19% of the time, Pallas kernels for 0%

profile of v6, /device:TPU:9, one launch (start us, length us, event | category | flops | bytes accessed | tf_op | source)
XLA Modules:
  0.0 102.6 jit_solution(3722505014509484245)
XLA Ops:
  0.6 1.4 %slice_bitcast_fusion = (f32[1,8,8,2048]{3,2,1,0:T(8,128)S(1)}, f32[1,8,8,2048]{3,2,1,0:T(8,128)S(1)}) fusion(f32[8,32,2048]{2,1,0:T(8,128)} %ph_ref.1), kind=kLoop, calls=%fused_computation.24 | loop fusion | bytes 2097152 | tf_op jit(solution)/shard_map/stack | solution.py:146
  2.1 0.4 copy-done
  2.7 5.2 %collective-permute-start = (f32[2,8,8,2048]{3,2,1,0:T(8,128)S(1)}, f32[2,8,8,2048]{3,2,1,0:T(8,128)S(1)}, u32[]{:S(2)}, u32[]{:S(2)}) collective-permute-start(f32[2,8,8,2048]{3,2,1,0:T(8,128)S(1)} %pad_maximum_fusion.1), channel_id=1, source_target_pairs={{0,1},{1,2},{2,3},{4,5},{5,6},{6,7},{8,9},{9,10},{10,11},{12,13},{... | collective-permute-start | bytes 3145736 | tf_op jit(solution)/shard_map/ppermute | solution.py:147
  8.0 1.9 %collective-permute-start.1 = (f32[2,8,8,2048]{3,2,1,0:T(8,128)S(1)}, f32[2,8,8,2048]{3,2,1,0:T(8,128)S(1)}, u32[]{:S(2)}, u32[]{:S(2)}) collective-permute-start(f32[2,8,8,2048]{3,2,1,0:T(8,128)S(1)} %pad_maximum_fusion.2), channel_id=1, source_target_pairs={{1,0},{2,1},{3,2},{5,4},{6,5},{7,6},{9,8},{10,9},{11,10},{13,12},{... | collective-permute-start | bytes 3145736 | tf_op jit(solution)/shard_map/ppermute | solution.py:148
  10.0 9.7 %collective-permute-done.top_ref = f32[2,8,8,2048]{3,2,1,0:T(8,128)S(1)} collective-permute-done((f32[2,8,8,2048]{3,2,1,0:T(8,128)S(1)}, f32[2,8,8,2048]{3,2,1,0:T(8,128)S(1)}, u32[]{:S(2)}, u32[]{:S(2)}) %collective-permute-start) | collective-permute-done | bytes 1048608 | tf_op jit(solution)/shard_map/ppermute | solution.py:147
  19.7 6.0 %collective-permute-done.1.bot_ref = f32[2,8,8,2048]{3,2,1,0:T(8,128)S(1)} collective-permute-done((f32[2,8,8,2048]{3,2,1,0:T(8,128)S(1)}, f32[2,8,8,2048]{3,2,1,0:T(8,128)S(1)}, u32[]{:S(2)}, u32[]{:S(2)}) %collective-permute-start.1) | collective-permute-done | bytes 1048608 | tf_op jit(solution)/shard_map/ppermute | solution.py:148
  25.7 1.0 copy-done.2
  26.6 15.4 %shard_map.50 = f32[32,8,18,128]{3,2,1,0:T(8,128)} custom-call(f32[8,32,2048]{2,1,0:T(8,128)} %ph_ref.1, s32[8,32,2048]{2,1,0:T(8,128)} %wt_ref.1, f32[2,8,8,2048]{3,2,1,0:T(8,128)} %copy-done.1, f32[2,8,8,2048]{3,2,1,0:T(8,128)} %copy-done.2), custom_call_target="tpu_custom_call" | custom-call | flops 94371840 | bytes 8388608 | tf_op jit(solution)/shard_map/pallas_call | solution.py:98
  42.0 3.8 %copy.11 = f32[32,8,18,128]{3,1,2,0:T(8,128)} copy(f32[32,8,18,128]{3,2,1,0:T(8,128)} %shard_map.50) | data formatting | bytes 4718592 | tf_op jit(solution)/shard_map/pallas_call | solution.py:98
  45.8 8.2 %all-to-all-start = ((f32[32,8,18,128]{3,1,2,0:T(8,128)}), f32[32,8,18,128]{3,1,2,0:T(8,128)}, u32[]{:S(2)}, u32[]{:S(2)}) async-start(f32[32,8,18,128]{3,1,2,0:T(8,128)} %copy.11), calls=%async_computation | async-start | bytes 4718592 | tf_op jit(solution)/shard_map/all_to_all | solution.py:150
  54.1 0.2 fusion.14
  54.3 0.1 copy.10
  54.5 8.7 %cholesky.16 = f32[95,95]{1,0:T(8,128)S(1)} custom-call(f32[95,95]{1,0:T(8,128)S(1)} %fusion.34), custom_call_target="Cholesky" | custom-call | tf_op jit(solution)/shard_map/jit(cholesky)/cholesky | solution.py:134
  63.2 0.6 compare_reduce_fusion
  63.8 0.7 fusion.21
  64.5 7.3 %custom-call.10 = f32[1,95,95]{1,2,0:T(8,128)S(1)} custom-call(f32[1,95,95]{2,1,0:T(8,128)S(1)} %fusion.21), custom_call_target="InvertDiagBlocksLowerTriangular" | custom-call | tf_op jit(solution)/shard_map/jit(_cho_solve)/triangular_solve | solution.py:135
  71.8 0.3 fusion.13
  72.1 0.2 fusion.31
  72.3 1.0 %all-to-all-done = f32[32,8,18,128]{3,1,2,0:T(8,128)} async-done(((f32[32,8,18,128]{3,1,2,0:T(8,128)}), f32[32,8,18,128]{3,1,2,0:T(8,128)}, u32[]{:S(2)}, u32[]{:S(2)}) %all-to-all-start) | async-done | bytes 2359328 | tf_op jit(solution)/shard_map/all_to_all | solution.py:150
  73.3 1.9 %copy.12 = f32[32,8,18,128]{3,1,0,2:T(8,128)S(1)} copy(f32[32,8,18,128]{3,1,2,0:T(8,128)} %all-to-all-done) | data formatting | bytes 4718592 | tf_op jit(solution)/shard_map/all_to_all | solution.py:150
  75.3 4.1 %reshape.23 = f32[256,18,2,64]{3,2,0,1:T(2,128)} reshape(f32[32,8,18,128]{3,1,0,2:T(8,128)S(1)} %copy.12) | data formatting | bytes 4718592 | tf_op jit(solution)/shard_map/reshape | solution.py:153
  79.4 5.9 %copy.13 = f32[256,2,18,64]{0,3,2,1:T(8,128)S(1)} copy(f32[256,2,18,64]{3,1,0,2:T(2,128)} %bitcast.40) | data formatting | bytes 4718592 | tf_op jit(solution)/shard_map/transpose | solution.py:153
  85.3 2.0 %fusion.40 = f32[95,2304]{0,1:S(1)} fusion(f32[95,256]{1,0:T(8,128)S(1)} %fusion.31, f32[256,2304]{0,1:T(8,128)S(1)} %bitcast.39), kind=kOutput, calls=%fused_computation.58 | convolution fusion | flops 672399360 | bytes 3332096
  87.4 2.1 %fusion.9 = f32[256,2304]{0,1:S(1)} fusion(f32[95,2304]{0,1:S(1)} %fusion.40, s32[256]{0:T(256)S(1)} %bitcast.48, s32[256]{0:T(256)S(1)} %bitcast.45), kind=kOutput, calls=%fused_computation.19 | convolution fusion | flops 672545280 | bytes 3236864
  89.4 0.4 bitcast_subtract_fusion
  89.9 2.5 %collective-permute-start.2 = (f32[256,36,2]{0,2,1:T(2,128)S(1)}, f32[256,36,2]{0,2,1:T(2,128)S(1)}, u32[]{:S(2)}, u32[]{:S(2)}) collective-permute-start(f32[256,36,2]{0,2,1:T(2,128)S(1)} %get-tuple-element.2), channel_id=1, source_target_pairs={{0,4},{4,8},{8,12},{12,16},{16,20},{20,24},{24,28},{28,32},{32,36}... | collective-permute-start | bytes 221192 | tf_op jit(solution)/shard_map/ppermute | solution.py:25
  92.4 5.8 %collective-permute-start.3 = (f32[256,36,2]{0,2,1:T(2,128)S(1)}, f32[256,36,2]{0,2,1:T(2,128)S(1)}, u32[]{:S(2)}, u32[]{:S(2)}) collective-permute-start(f32[256,36,2]{0,2,1:T(2,128)S(1)} %get-tuple-element.3), channel_id=1, source_target_pairs={{4,0},{8,4},{12,8},{16,12},{20,16},{24,20},{28,24},{32,28},{36,32}... | collective-permute-start | bytes 221192 | tf_op jit(solution)/shard_map/ppermute | solution.py:28
  98.2 1.0 %slice.98 = f32[95,32,64]{0,2,1:T(8,128)} slice(f32[95,36,64]{0,2,1:T(8,128)S(1)} %bitcast.41), slice={[0:95], [2:34], [0:64]} | slice | bytes 1556480 | tf_op jit(solution)/shard_map/slice | solution.py:160
  99.3 0.3 collective-permute-done.3
  99.6 0.3 pad_maximum_fusion
  99.9 0.5 fusion
  100.5 2.1 %fusion.5 = bf16[256,32,64]{0,2,1:T(8,128)(2,1)} fusion(f32[256,32,68]{0,2,1:T(8,128)S(1)} %fusion), kind=kLoop, calls=%fused_computation.12 | loop fusion | flops 4718592 | bytes 11534336 | tf_op jit(solution)/shard_map/convert_element_type | solution.py:161
  (14 shorter events, 0.4 us)
Async XLA Ops:
  0.6 1.9 %copy-start = (s32[8,32,2048]{2,1,0:T(8,128)S(1)}, s32[8,32,2048]{2,1,0:T(8,128)}, u32[]{:S(2)}) copy-start(s32[8,32,2048]{2,1,0:T(8,128)} %wt_ref.1) | copy-start | bytes 6291460
  2.7 16.9 %collective-permute-start = (f32[2,8,8,2048]{3,2,1,0:T(8,128)S(1)}, f32[2,8,8,2048]{3,2,1,0:T(8,128)S(1)}, u32[]{:S(2)}, u32[]{:S(2)}) collective-permute-start(f32[2,8,8,2048]{3,2,1,0:T(8,128)S(1)} %pad_maximum_fusion.1), channel_id=1, source_target_pairs={{0,1},{1,2},{2,3},{4,5},{5,6},{6,7},{8,9},{9,10},{10,11},{12,13},{... | collective-permute-start | bytes 3145736 | tf_op jit(solution)/shard_map/ppermute | solution.py:147
  8.0 17.6 %collective-permute-start.1 = (f32[2,8,8,2048]{3,2,1,0:T(8,128)S(1)}, f32[2,8,8,2048]{3,2,1,0:T(8,128)S(1)}, u32[]{:S(2)}, u32[]{:S(2)}) collective-permute-start(f32[2,8,8,2048]{3,2,1,0:T(8,128)S(1)} %pad_maximum_fusion.2), channel_id=1, source_target_pairs={{1,0},{2,1},{3,2},{5,4},{6,5},{7,6},{9,8},{10,9},{11,10},{13,12},{... | collective-permute-start | bytes 3145736 | tf_op jit(solution)/shard_map/ppermute | solution.py:148
  19.7 6.0 %copy-start.1 = (f32[2,8,8,2048]{3,2,1,0:T(8,128)}, f32[2,8,8,2048]{3,2,1,0:T(8,128)S(1)}, u32[]{:S(2)}) copy-start(f32[2,8,8,2048]{3,2,1,0:T(8,128)S(1)} %collective-permute-done.top_ref) | copy-start | bytes 3145732
  25.7 1.0 copy-start.2
  45.8 8.2 %copy-start.3 = (s32[256,2]{0,1:T(2,128)S(1)}, s32[256,2]{0,1:T(2,128)}, u32[]{:S(2)}) copy-start(s32[256,2]{0,1:T(2,128)} %param.5) | copy-start | bytes 6148
  45.8 27.5 %all-to-all-start = ((f32[32,8,18,128]{3,1,2,0:T(8,128)}), f32[32,8,18,128]{3,1,2,0:T(8,128)}, u32[]{:S(2)}, u32[]{:S(2)}) async-start(f32[32,8,18,128]{3,1,2,0:T(8,128)} %copy.11), calls=%async_computation | async-start | bytes 4718592 | tf_op jit(solution)/shard_map/all_to_all | solution.py:150
  89.9 9.4 %collective-permute-start.2 = (f32[256,36,2]{0,2,1:T(2,128)S(1)}, f32[256,36,2]{0,2,1:T(2,128)S(1)}, u32[]{:S(2)}, u32[]{:S(2)}) collective-permute-start(f32[256,36,2]{0,2,1:T(2,128)S(1)} %get-tuple-element.2), channel_id=1, source_target_pairs={{0,4},{4,8},{8,12},{12,16},{16,20},{20,24},{24,28},{28,32},{32,36}... | collective-permute-start | bytes 221192 | tf_op jit(solution)/shard_map/ppermute | solution.py:25
  92.4 7.2 %collective-permute-start.3 = (f32[256,36,2]{0,2,1:T(2,128)S(1)}, f32[256,36,2]{0,2,1:T(2,128)S(1)}, u32[]{:S(2)}, u32[]{:S(2)}) collective-permute-start(f32[256,36,2]{0,2,1:T(2,128)S(1)} %get-tuple-element.3), channel_id=1, source_target_pairs={{4,0},{8,4},{12,8},{16,12},{20,16},{24,20},{28,24},{32,28},{36,32}... | collective-permute-start | bytes 221192 | tf_op jit(solution)/shard_map/ppermute | solution.py:28

commit v7 on v3

--- a/solution.py
+++ b/solution.py
@@ -36,70 +36,75 @@
 
 
 def unwrap_kernel(rows_out, ph_ref, wt_ref, top_ref, bot_ref, o_ref, p_ref, q_ref, cur_ref):
-    p_ref[pl.ds(0, HALO), :] = top_ref[0, 0]
-    p_ref[pl.ds(HALO, rows_out), :] = ph_ref[0]
-    p_ref[pl.ds(HALO + rows_out, HALO), :] = bot_ref[0, 0]
-    q_ref[pl.ds(0, HALO), :] = top_ref[1, 0]
-    q_ref[pl.ds(HALO, rows_out), :] = wt_ref[0].astype(jnp.float32)
-    q_ref[pl.ds(HALO + rows_out, HALO), :] = bot_ref[1, 0]
-    p = p_ref[...]
-    q = q_ref[...]
-    nr, nc = p.shape
-    row = lax.broadcasted_iota(jnp.int32, (nr, nc), 0)
-    col = lax.broadcasted_iota(jnp.int32, (nr, nc), 1)
-    zero = jnp.zeros((nr, nc), jnp.float32)
-    p_dn = pltpu.roll(p, nr - 1, 0)
-    q_dn = pltpu.roll(q, nr - 1, 0)
-    g_dn = wrapped_diff(p_dn - p)
-    w_dn = jnp.where(row < nr - 1, q_dn * q, zero)
-    p_rt = pltpu.roll(p, nc - 1, 1)
-    q_rt = pltpu.roll(q, nc - 1, 1)
-    g_rt = wrapped_diff(p_rt - p)
-    w_rt = jnp.where(col < nc - 1, q_rt * q, zero)
-    g_up = pltpu.roll(g_dn, 1, 0)
-    w_up = pltpu.roll(w_dn, 1, 0)
-    g_lt = pltpu.roll(g_rt, 1, 1)
-    w_lt = pltpu.roll(w_rt, 1, 1)
-    den = ((w_up + w_dn) + w_lt) + w_rt
-    den = jnp.where(den > 0.0, den, 1.0)
-    cur = zero
-    for _ in range(SWEEPS):
-        c_up = pltpu.roll(cur, 1, 0)
-        c_dn = pltpu.roll(cur, nr - 1, 0)
-        c_lt = pltpu.roll(cur, 1, 1)
-        c_rt = pltpu.roll(cur, nc - 1, 1)
-        num = w_up * (c_up + g_up)
-        num = num + w_dn * (c_dn - g_dn)
-        num = num + w_lt * (c_lt + g_lt)
-        num = num + w_rt * (c_rt - g_rt)
-        cur = num / den
-    cur_ref[...] = cur
-    half = rows_out // 2
-    upper = cur_ref[pl.ds(HALO, half), :]
-    lower = cur_ref[pl.ds(HALO + half, half), :]
-    lane = lax.broadcasted_iota(jnp.int32, (half, nc), 1) % 128
-    first = lane < 64
-    even = jnp.where(first, upper, pltpu.roll(lower, 64, 1))
-    odd = jnp.where(first, pltpu.roll(upper, nc - 64, 1), lower)
-    for m in range(nc // 128):
-        o_ref[2 * m, 0] = even[:, 128 * m : 128 * (m + 1)]
-        o_ref[2 * m + 1, 0] = odd[:, 128 * m : 128 * (m + 1)]
+    for b in range(ph_ref.shape[0]):
+        p_ref[pl.ds(0, HALO), :] = top_ref[0, b]
+        p_ref[pl.ds(HALO, rows_out), :] = ph_ref[b]
+        p_ref[pl.ds(HALO + rows_out, HALO), :] = bot_ref[0, b]
+        q_ref[pl.ds(0, HALO), :] = top_ref[1, b]
+        q_ref[pl.ds(HALO, rows_out), :] = wt_ref[b].astype(jnp.float32)
+        q_ref[pl.ds(HALO + rows_out, HALO), :] = bot_ref[1, b]
+        p = p_ref[...]
+        q = q_ref[...]
+        nr, nc = p.shape
+        row = lax.broadcasted_iota(jnp.int32, (nr, nc), 0)
+        col = lax.broadcasted_iota(jnp.int32, (nr, nc), 1)
+        zero = jnp.zeros((nr, nc), jnp.float32)
+        p_dn = pltpu.roll(p, nr - 1, 0)
+        q_dn = pltpu.roll(q, nr - 1, 0)
+        g_dn = wrapped_diff(p_dn - p)
+        w_dn = jnp.where(row < nr - 1, q_dn * q, zero)
+        p_rt = pltpu.roll(p, nc - 1, 1)
+        q_rt = pltpu.roll(q, nc - 1, 1)
+        g_rt = wrapped_diff(p_rt - p)
+        w_rt = jnp.where(col < nc - 1, q_rt * q, zero)
+        g_up = pltpu.roll(g_dn, 1, 0)
+        w_up = pltpu.roll(w_dn, 1, 0)
+        g_lt = pltpu.roll(g_rt, 1, 1)
+        w_lt = pltpu.roll(w_rt, 1, 1)
+        den = ((w_up + w_dn) + w_lt) + w_rt
+        den = jnp.where(den > 0.0, den, 1.0)
+        inv = 1.0 / den
+        num = w_up * g_up
+        num = num - w_dn * g_dn
+        num = num + w_lt * g_lt
+        num = num - w_rt * g_rt
+        const = num * inv
+        a_up, a_dn, a_lt, a_rt = w_up * inv, w_dn * inv, w_lt * inv, w_rt * inv
+        cur = const
+        for _ in range(SWEEPS - 1):
+            nxt = const + a_up * pltpu.roll(cur, 1, 0)
+            nxt = nxt + a_dn * pltpu.roll(cur, nr - 1, 0)
+            nxt = nxt + a_lt * pltpu.roll(cur, 1, 1)
+            nxt = nxt + a_rt * pltpu.roll(cur, nc - 1, 1)
+            cur = nxt
+        cur_ref[...] = cur
+        half = rows_out // 2
+        upper = cur_ref[pl.ds(HALO, half), :]
+        lower = cur_ref[pl.ds(HALO + half, half), :]
+        lane = lax.broadcasted_iota(jnp.int32, (half, nc), 1) % 128
+        first = lane < 64
+        even = jnp.where(first, upper, pltpu.roll(lower, 64, 1))
+        odd = jnp.where(first, pltpu.roll(upper, nc - 64, 1), lower)
+        for m in range(nc // 128):
+            o_ref[2 * m, b] = even[:, 128 * m : 128 * (m + 1)]
+            o_ref[2 * m + 1, b] = odd[:, 128 * m : 128 * (m + 1)]
 
 
 def unwrap(phase, weights, top, bottom):
     n, rows_out, nc = phase.shape
     nr = rows_out + 2 * HALO
-    halo_spec = pl.BlockSpec((2, 1, HALO, nc), lambda i: (0, i, 0, 0))
+    per = 2
+    halo_spec = pl.BlockSpec((2, per, HALO, nc), lambda i: (0, i, 0, 0))
     return pl.pallas_call(
         functools.partial(unwrap_kernel, rows_out),
-        grid=(n,),
+        grid=(n // per,),
         in_specs=[
-            pl.BlockSpec((1, rows_out, nc), lambda i: (i, 0, 0)),
-            pl.BlockSpec((1, rows_out, nc), lambda i: (i, 0, 0)),
+            pl.BlockSpec((per, rows_out, nc), lambda i: (i, 0, 0)),
+            pl.BlockSpec((per, rows_out, nc), lambda i: (i, 0, 0)),
             halo_spec,
             halo_spec,
         ],
-        out_specs=pl.BlockSpec((nc // 64, 1, rows_out // 2, 128), lambda i: (0, i, 0, 0)),
+        out_specs=pl.BlockSpec((nc // 64, per, rows_out // 2, 128), lambda i: (0, i, 0, 0)),
         out_shape=jax.ShapeDtypeStruct((nc // 64, n, rows_out // 2, 128), jnp.float32),
         scratch_shapes=[pltpu.VMEM((nr, nc), jnp.float32)] * 3,
         cost_estimate=pl.CostEstimate(

time: 103 us -> 102 us (level)
  no operation moved by 1% of the time
where the time goes in v7:
time: 102 us; the launch traced here: 101 us
  starting transfers between devices  29.3 us (29%)
  other arithmetic  22.3 us (22%)
  waiting for transfers between devices  19.2 us (19%)
  Pallas kernels  13.6 us (13%)
  local copies, waits for them, and re-layouts  11.3 us (11%)
  matrix products  4.46 us (4%)
    pallas_call x1, Pallas kernels, unwrap(): pl.pallas_call(functools.partial(unwrap_kernel, rows_out), grid=(n // per...  13.6 us
    another operation x3, other arithmetic, network_maps(): factor = jnp.linalg.cholesky(normal_matrix)  9.36 us
    all_to_all x1, starting transfers between devices, on_device(): lax.all_to_all(current, 'ifg', split_axis=0, concat_axis=0, tiled=True)  8.16 us
    another operation x2, other arithmetic, network_maps(): pseudo = jax.scipy.linalg.cho_solve((factor, True), design.T)  7.94 us
    ppermute x2, starting transfers between devices, extended_2(): lax.ppermute(lax.slice_in_dim(block, 0, width, axis=dim), axis, backward)  7.81 us
    ppermute x2, waiting for transfers between devices, extended_2(): lax.ppermute(lax.slice_in_dim(block, 0, width, axis=dim), axis, backward)  7.23 us
    ppermute x2, starting transfers between devices, extended_2(): lax.ppermute(lax.slice_in_dim(block, block.shape[dim] - width, None, axis...  6.21 us
    ppermute x1, waiting for transfers between devices, on_device(): bottom = lax.ppermute(edge_high, 'rows', backward)  6.03 us
  transfers between devices with their start and end apart: 7, of which 5 were waited for; matrix products, arithmetic and copies ran while one was open for 18% of the time, Pallas kernels for 0%

profile of v7, /device:TPU:9, one launch (start us, length us, event | category | flops | bytes accessed | tf_op | source)
XLA Modules:
  0.0 101.0 jit_solution(17714358213408904723)
XLA Ops:
  0.6 1.3 %slice_bitcast_fusion = (f32[1,8,4,2048]{3,2,1,0:T(4,128)S(1)}, f32[1,8,4,2048]{3,2,1,0:T(4,128)S(1)}) fusion(f32[8,32,2048]{2,1,0:T(8,128)} %ph_ref.1), kind=kLoop, calls=%fused_computation.24 | loop fusion | bytes 1048576 | tf_op jit(solution)/shard_map/stack | solution.py:146
  1.9 1.3 %convert_bitcast_fusion = (f32[1,8,4,2048]{3,2,1,0:T(4,128)S(1)}, f32[1,8,4,2048]{3,2,1,0:T(4,128)S(1)}) fusion(s32[8,32,2048]{2,1,0:T(8,128)} %wt_ref.1), kind=kLoop, calls=%fused_computation.23 | loop fusion | flops 131072 | bytes 1048576 | tf_op jit(solution)/shard_map/stack | solution.py:146
  3.3 0.1 pad_maximum_fusion.1
  3.4 5.2 %collective-permute-start = (f32[2,8,4,2048]{3,2,1,0:T(4,128)S(1)}, f32[2,8,4,2048]{3,2,1,0:T(4,128)S(1)}, u32[]{:S(2)}, u32[]{:S(2)}) collective-permute-start(f32[2,8,4,2048]{3,2,1,0:T(4,128)S(1)} %pad_maximum_fusion.1), channel_id=1, source_target_pairs={{0,1},{1,2},{2,3},{4,5},{5,6},{6,7},{8,9},{9,10},{10,11},{12,13},{... | collective-permute-start | bytes 1572872 | tf_op jit(solution)/shard_map/ppermute | solution.py:147
  8.7 1.9 %collective-permute-start.1 = (f32[2,8,4,2048]{3,2,1,0:T(4,128)S(1)}, f32[2,8,4,2048]{3,2,1,0:T(4,128)S(1)}, u32[]{:S(2)}, u32[]{:S(2)}) collective-permute-start(f32[2,8,4,2048]{3,2,1,0:T(4,128)S(1)} %pad_maximum_fusion.2), channel_id=1, source_target_pairs={{1,0},{2,1},{3,2},{5,4},{6,5},{7,6},{9,8},{10,9},{11,10},{13,12},{... | collective-permute-start | bytes 1572872 | tf_op jit(solution)/shard_map/ppermute | solution.py:148
  10.7 4.0 %collective-permute-done.top_ref = f32[2,8,4,2048]{3,2,1,0:T(4,128)S(1)} collective-permute-done((f32[2,8,4,2048]{3,2,1,0:T(4,128)S(1)}, f32[2,8,4,2048]{3,2,1,0:T(4,128)S(1)}, u32[]{:S(2)}, u32[]{:S(2)}) %collective-permute-start) | collective-permute-done | bytes 524320 | tf_op jit(solution)/shard_map/ppermute | solution.py:147
  14.7 6.0 %collective-permute-done.1.bot_ref = f32[2,8,4,2048]{3,2,1,0:T(4,128)S(1)} collective-permute-done((f32[2,8,4,2048]{3,2,1,0:T(4,128)S(1)}, f32[2,8,4,2048]{3,2,1,0:T(4,128)S(1)}, u32[]{:S(2)}, u32[]{:S(2)}) %collective-permute-start.1) | collective-permute-done | bytes 524320 | tf_op jit(solution)/shard_map/ppermute | solution.py:148
  20.8 0.8 copy-done.2
  21.5 13.6 %shard_map.50 = f32[32,8,16,128]{3,2,1,0:T(8,128)} custom-call(f32[8,32,2048]{2,1,0:T(8,128)} %ph_ref.1, s32[8,32,2048]{2,1,0:T(8,128)} %wt_ref.1, f32[2,8,4,2048]{3,2,1,0:T(4,128)} %copy-done.1, f32[2,8,4,2048]{3,2,1,0:T(4,128)} %copy-done.2), custom_call_target="tpu_custom_call" | custom-call | flops 78643200 | bytes 7340032 | tf_op jit(solution)/shard_map/pallas_call | solution.py:98
  35.1 8.2 %all-to-all-start = ((f32[32,8,16,128]{3,2,1,0:T(8,128)}), f32[32,8,16,128]{3,2,1,0:T(8,128)S(1)}, u32[]{:S(2)}, u32[]{:S(2)}) async-start(f32[32,8,16,128]{3,2,1,0:T(8,128)} %shard_map.50), calls=%async_computation | async-start | bytes 4194304 | tf_op jit(solution)/shard_map/all_to_all | solution.py:150
  43.3 0.3 fusion.14
  43.7 8.7 %cholesky.16 = f32[95,95]{1,0:T(8,128)S(1)} custom-call(f32[95,95]{1,0:T(8,128)S(1)} %fusion.34), custom_call_target="Cholesky" | custom-call | tf_op jit(solution)/shard_map/jit(cholesky)/cholesky | solution.py:134
  52.4 0.6 compare_reduce_fusion
  53.0 0.7 fusion.21
  53.7 7.3 %custom-call.10 = f32[1,95,95]{1,2,0:T(8,128)S(1)} custom-call(f32[1,95,95]{2,1,0:T(8,128)S(1)} %fusion.21), custom_call_target="InvertDiagBlocksLowerTriangular" | custom-call | tf_op jit(solution)/shard_map/jit(_cho_solve)/triangular_solve | solution.py:135
  61.0 0.3 fusion.13
  61.3 0.2 fusion.31
  61.5 1.9 %all-to-all-done = f32[32,8,16,128]{3,2,1,0:T(8,128)S(1)} async-done(((f32[32,8,16,128]{3,2,1,0:T(8,128)}), f32[32,8,16,128]{3,2,1,0:T(8,128)S(1)}, u32[]{:S(2)}, u32[]{:S(2)}) %all-to-all-start) | async-done | bytes 2097184 | tf_op jit(solution)/shard_map/all_to_all | solution.py:150
  63.4 3.7 %reshape.23 = f32[256,16,2,64]{3,2,1,0:T(2,128)} reshape(f32[32,8,16,128]{3,2,1,0:T(8,128)S(1)} %all-to-all-done) | data formatting | bytes 4194304 | tf_op jit(solution)/shard_map/reshape | solution.py:152
  67.1 5.4 %copy.8 = f32[256,2,16,64]{0,3,2,1:T(8,128)S(1)} copy(f32[256,2,16,64]{3,1,2,0:T(2,128)} %bitcast.38) | data formatting | bytes 4194304 | tf_op jit(solution)/shard_map/transpose | solution.py:152
  72.5 1.9 %fusion.40 = f32[95,2048]{0,1:S(1)} fusion(f32[95,256]{1,0:T(8,128)S(1)} %fusion.31, f32[256,2048]{0,1:T(8,128)S(1)} %bitcast.37), kind=kOutput, calls=%fused_computation.61 | convolution fusion | flops 597688320 | bytes 2972672
  74.4 1.8 %fusion.9 = f32[256,2048]{0,1:S(1)} fusion(f32[95,2048]{0,1:S(1)} %fusion.40, s32[256]{0:T(256)S(1)} %bitcast.46, s32[256]{0:T(256)S(1)} %bitcast.43), kind=kOutput, calls=%fused_computation.19 | convolution fusion | flops 597834240 | bytes 2877440
  76.2 0.5 bitcast_subtract_fusion
  76.7 3.8 %collective-permute-start.2 = (f32[256,2,64]{0,2,1:T(8,128)S(1)}, f32[256,2,64]{0,2,1:T(8,128)S(1)}, u32[]{:S(2)}, u32[]{:S(2)}) collective-permute-start(f32[256,2,64]{0,2,1:T(8,128)S(1)} %get-tuple-element.4), channel_id=1, source_target_pairs={{0,1},{1,2},{2,3},{4,5},{5,6},{6,7},{8,9},{9,10},{10,11},{12,13},{... | collective-permute-start | bytes 393224 | tf_op jit(solution)/shard_map/ppermute | solution.py:24
  80.5 1.9 %collective-permute-start.3 = (f32[256,2,64]{0,2,1:T(8,128)S(1)}, f32[256,2,64]{0,2,1:T(8,128)S(1)}, u32[]{:S(2)}, u32[]{:S(2)}) collective-permute-start(f32[256,2,64]{0,2,1:T(8,128)S(1)} %get-tuple-element.5), channel_id=1, source_target_pairs={{1,0},{2,1},{3,2},{5,4},{6,5},{7,6},{9,8},{10,9},{11,10},{13,12},{... | collective-permute-start | bytes 393224 | tf_op jit(solution)/shard_map/ppermute | solution.py:27
  82.4 5.9 %collective-permute-done.3 = f32[256,2,64]{0,2,1:T(8,128)S(1)} collective-permute-done((f32[256,2,64]{0,2,1:T(8,128)S(1)}, f32[256,2,64]{0,2,1:T(8,128)S(1)}, u32[]{:S(2)}, u32[]{:S(2)}) %collective-permute-start.3) | collective-permute-done | bytes 131104 | tf_op jit(solution)/shard_map/ppermute | solution.py:27
  88.4 2.4 %collective-permute-start.4 = (f32[256,36,2]{0,2,1:T(2,128)S(1)}, f32[256,36,2]{0,2,1:T(2,128)S(1)}, u32[]{:S(2)}, u32[]{:S(2)}) collective-permute-start(f32[256,36,2]{0,2,1:T(2,128)S(1)} %get-tuple-element.2), channel_id=1, source_target_pairs={{0,4},{4,8},{8,12},{12,16},{16,20},{20,24},{24,28},{28,32},{32,36}... | collective-permute-start | bytes 221192 | tf_op jit(solution)/shard_map/ppermute | solution.py:24
  90.8 5.9 %collective-permute-start.5 = (f32[256,36,2]{0,2,1:T(2,128)S(1)}, f32[256,36,2]{0,2,1:T(2,128)S(1)}, u32[]{:S(2)}, u32[]{:S(2)}) collective-permute-start(f32[256,36,2]{0,2,1:T(2,128)S(1)} %get-tuple-element.3), channel_id=1, source_target_pairs={{4,0},{8,4},{12,8},{16,12},{20,16},{24,20},{28,24},{32,28},{36,32}... | collective-permute-start | bytes 221192 | tf_op jit(solution)/shard_map/ppermute | solution.py:27
  96.7 1.4 %collective-permute-done.5 = f32[256,36,2]{0,2,1:T(2,128)S(1)} collective-permute-done((f32[256,36,2]{0,2,1:T(2,128)S(1)}, f32[256,36,2]{0,2,1:T(2,128)S(1)}, u32[]{:S(2)}, u32[]{:S(2)}) %collective-permute-start.5) | collective-permute-done | bytes 73760 | tf_op jit(solution)/shard_map/ppermute | solution.py:27
  98.0 0.3 pad_maximum_fusion
  98.3 0.5 fusion
  98.9 2.1 %fusion.5 = bf16[256,32,64]{0,2,1:T(8,128)(2,1)} fusion(f32[256,32,68]{0,2,1:T(8,128)S(1)} %fusion), kind=kLoop, calls=%fused_computation.11 | loop fusion | flops 4718592 | bytes 11534336 | tf_op jit(solution)/shard_map/convert_element_type | solution.py:159
  (16 shorter events, 0.4 us)
Async XLA Ops:
  3.4 11.3 %collective-permute-start = (f32[2,8,4,2048]{3,2,1,0:T(4,128)S(1)}, f32[2,8,4,2048]{3,2,1,0:T(4,128)S(1)}, u32[]{:S(2)}, u32[]{:S(2)}) collective-permute-start(f32[2,8,4,2048]{3,2,1,0:T(4,128)S(1)} %pad_maximum_fusion.1), channel_id=1, source_target_pairs={{0,1},{1,2},{2,3},{4,5},{5,6},{6,7},{8,9},{9,10},{10,11},{12,13},{... | collective-permute-start | bytes 1572872 | tf_op jit(solution)/shard_map/ppermute | solution.py:147
  8.7 12.0 %collective-permute-start.1 = (f32[2,8,4,2048]{3,2,1,0:T(4,128)S(1)}, f32[2,8,4,2048]{3,2,1,0:T(4,128)S(1)}, u32[]{:S(2)}, u32[]{:S(2)}) collective-permute-start(f32[2,8,4,2048]{3,2,1,0:T(4,128)S(1)} %pad_maximum_fusion.2), channel_id=1, source_target_pairs={{1,0},{2,1},{3,2},{5,4},{6,5},{7,6},{9,8},{10,9},{11,10},{13,12},{... | collective-permute-start | bytes 1572872 | tf_op jit(solution)/shard_map/ppermute | solution.py:148
  14.7 6.0 %copy-start.1 = (f32[2,8,4,2048]{3,2,1,0:T(4,128)}, f32[2,8,4,2048]{3,2,1,0:T(4,128)S(1)}, u32[]{:S(2)}) copy-start(f32[2,8,4,2048]{3,2,1,0:T(4,128)S(1)} %collective-permute-done.top_ref) | copy-start | bytes 1572868
  20.8 0.8 copy-start.2
  35.1 8.2 %copy-start.3 = (s32[256,2]{0,1:T(2,128)S(1)}, s32[256,2]{0,1:T(2,128)}, u32[]{:S(2)}) copy-start(s32[256,2]{0,1:T(2,128)} %param.5) | copy-start | bytes 6148
  35.1 28.3 %all-to-all-start = ((f32[32,8,16,128]{3,2,1,0:T(8,128)}), f32[32,8,16,128]{3,2,1,0:T(8,128)S(1)}, u32[]{:S(2)}, u32[]{:S(2)}) async-start(f32[32,8,16,128]{3,2,1,0:T(8,128)} %shard_map.50), calls=%async_computation | async-start | bytes 4194304 | tf_op jit(solution)/shard_map/all_to_all | solution.py:150
  74.4 2.3 %copy-start = (f32[95,2048]{0,1}, f32[95,2048]{0,1:S(1)}, u32[]{:S(2)}) copy-start(f32[95,2048]{0,1:S(1)} %fusion.40) | copy-start | bytes 2334724
  76.7 5.7 %collective-permute-start.2 = (f32[256,2,64]{0,2,1:T(8,128)S(1)}, f32[256,2,64]{0,2,1:T(8,128)S(1)}, u32[]{:S(2)}, u32[]{:S(2)}) collective-permute-start(f32[256,2,64]{0,2,1:T(8,128)S(1)} %get-tuple-element.4), channel_id=1, source_target_pairs={{0,1},{1,2},{2,3},{4,5},{5,6},{6,7},{8,9},{9,10},{10,11},{12,13},{... | collective-permute-start | bytes 393224 | tf_op jit(solution)/shard_map/ppermute | solution.py:24
  80.5 7.8 %collective-permute-start.3 = (f32[256,2,64]{0,2,1:T(8,128)S(1)}, f32[256,2,64]{0,2,1:T(8,128)S(1)}, u32[]{:S(2)}, u32[]{:S(2)}) collective-permute-start(f32[256,2,64]{0,2,1:T(8,128)S(1)} %get-tuple-element.5), channel_id=1, source_target_pairs={{1,0},{2,1},{3,2},{5,4},{6,5},{7,6},{9,8},{10,9},{11,10},{13,12},{... | collective-permute-start | bytes 393224 | tf_op jit(solution)/shard_map/ppermute | solution.py:27
  88.4 8.3 %collective-permute-start.4 = (f32[256,36,2]{0,2,1:T(2,128)S(1)}, f32[256,36,2]{0,2,1:T(2,128)S(1)}, u32[]{:S(2)}, u32[]{:S(2)}) collective-permute-start(f32[256,36,2]{0,2,1:T(2,128)S(1)} %get-tuple-element.2), channel_id=1, source_target_pairs={{0,4},{4,8},{8,12},{12,16},{16,20},{20,24},{24,28},{28,32},{32,36}... | collective-permute-start | bytes 221192 | tf_op jit(solution)/shard_map/ppermute | solution.py:24
  90.8 7.3 %collective-permute-start.5 = (f32[256,36,2]{0,2,1:T(2,128)S(1)}, f32[256,36,2]{0,2,1:T(2,128)S(1)}, u32[]{:S(2)}, u32[]{:S(2)}) collective-permute-start(f32[256,36,2]{0,2,1:T(2,128)S(1)} %get-tuple-element.3), channel_id=1, source_target_pairs={{4,0},{8,4},{12,8},{16,12},{20,16},{24,20},{28,24},{32,28},{36,32}... | collective-permute-start | bytes 221192 | tf_op jit(solution)/shard_map/ppermute | solution.py:27

commit v8 on v7

--- a/solution.py
+++ b/solution.py
@@ -113,6 +113,46 @@
     )(phase, weights, top, bottom)
 
 
+def invert_kernel(rows, x_ref, pseudo_ref, design_ref, s_ref, r_ref):
+    ifg = pseudo_ref.shape[1]
+    pseudo = pseudo_ref[...]
+    design = design_ref[...]
+    for k in range(rows):
+        x = x_ref[pl.ds(k, ifg, stride=rows), :]
+        series = jnp.dot(pseudo, x, precision=lax.Precision.HIGHEST, preferred_element_type=jnp.float32)
+        fit = jnp.dot(design, series, precision=lax.Precision.HIGHEST, preferred_element_type=jnp.float32)
+        res_t = (x - fit).T
+        ser_t = series.T
+        r_ref[pl.ds(k * 64, 64), :] = res_t[:64]
+        r_ref[pl.ds((k + rows) * 64, 64), :] = res_t[64:]
+        s_ref[pl.ds(k * 64, 64), :] = ser_t[:64]
+        s_ref[pl.ds((k + rows) * 64, 64), :] = ser_t[64:]
+
+
+def invert(packed, pseudo, design, rows):
+    ifg = pseudo.shape[1]
+    epochs = pseudo.shape[0]
+    wide = epochs + (-epochs) % 8
+    pseudo = jnp.pad(pseudo, ((0, wide - epochs), (0, 0)))
+    design = jnp.pad(design, ((0, 0), (0, wide - epochs)))
+    whole = pl.BlockSpec(memory_space=pltpu.VMEM)
+    series_t, residual_t = pl.pallas_call(
+        functools.partial(invert_kernel, rows),
+        in_specs=[whole, whole, whole],
+        out_specs=(whole, whole),
+        out_shape=(
+            jax.ShapeDtypeStruct((2 * rows * 64, wide), jnp.float32),
+            jax.ShapeDtypeStruct((2 * rows * 64, ifg), jnp.float32),
+        ),
+        cost_estimate=pl.CostEstimate(
+            flops=4 * 6 * wide * ifg * rows * 128,
+            bytes_accessed=4 * 128 * rows * (2 * ifg + wide),
+            transcendentals=0,
+        ),
+    )(packed, pseudo, design)
+    return series_t[:, :epochs], residual_t
+
+
 def binomial(padded, axis):
     length = padded.shape[axis] - 4
 
@@ -149,11 +189,14 @@
     current = unwrap(phase, weights, top, bottom)
     received = lax.all_to_all(current, "ifg", split_axis=0, concat_axis=0, tiled=True)
     ifg = received.shape[0] * received.shape[1]
-    block = received.reshape(ifg, rows // 2, 2, 64).transpose(0, 2, 1, 3).reshape(ifg, rows, 64)
-    series_block = jnp.einsum("ei,irc->erc", pseudo, block, precision=lax.Precision.HIGHEST)
-    residual = block - jnp.einsum(
-        "ie,erc->irc", design, series_block, precision=lax.Precision.HIGHEST
-    )
+    half = rows // 2
+    series_t, residual_t = invert(received.reshape(ifg * half, 128), pseudo, design, half)
+
+    def unpack(x):
+        return x.reshape(rows, 64, x.shape[1]).transpose(2, 0, 1)
+
+    series_block = unpack(series_t)
+    residual = unpack(residual_t)
     padded = extended_2(residual, (("rows", 1), ("ifg", 2)), 2)
     filtered = binomial(binomial(padded, 1), 2)
     return (series_block, filtered.astype(jnp.bfloat16))

time: 102 us -> 100 us (0.980)
  Pallas kernels: 13.6 us -> 21.8 us
  local copies, waits for them, and re-layouts: 11.3 us -> 5.98 us
  matrix products: 4.46 us -> 1.16 us
  waiting for transfers between devices: 19.2 us -> 17.4 us
    pallas_call x0 -> x1, Pallas kernels: none -> 8.27 us  [invert(): pl.pallas_call(functools.partial(invert_kernel, rows), in_specs=[whole, w...]
    transpose x1 -> x0, local copies, waits for them, and re-layouts: 5.38 us -> none  [on_device(): received.reshape(ifg, rows // 2, 2, 64).transpose(0, 2, 1, 3)]
    unnamed x2 -> x0, matrix products: 3.69 us -> none
    reshape x1 -> x0, local copies, waits for them, and re-layouts: 3.66 us -> none  [on_device(): received.reshape(ifg, rows // 2, 2, 64).transpose(0, 2, 1, 3)]
    all_to_all x1, waiting for transfers between devices: 1.9 us -> 0.07 us  [on_device(): lax.all_to_all(current, 'ifg', split_axis=0, concat_axis=0, tiled=True)]
    unnamed x8 -> x10, local copies, waits for them, and re-layouts: 0.81 us -> 2.13 us
    pad x0 -> x2, local copies, waits for them, and re-layouts: none -> 1.31 us  [the longest x1 0.67 us: invert(): design = jnp.pad(design, ((0, 0), (0, wide - epochs)))]
    slice x1, local copies, waits for them, and re-layouts: 0.02 us -> 1.14 us  [extended_2(): lax.slice_in_dim(block, block.shape[dim] - width, None, axis=dim)]
  transfers between devices with their start and end apart: 7 -> 7, of which waited for: 5 -> 5; matrix products, arithmetic and copies ran while one was open for 18% -> 20% of each run, Pallas kernels for 0% -> 0%
where the time goes in v8:
time: 100 us; the launch traced here: 99.5 us
  starting transfers between devices  29.3 us (29%)
  other arithmetic  23 us (23%)
  Pallas kernels  21.8 us (22%)
  waiting for transfers between devices  17.4 us (17%)
  local copies, waits for them, and re-layouts  5.98 us (6%)
  matrix products  1.16 us (1%)
    pallas_call x1, Pallas kernels, unwrap(): pl.pallas_call(functools.partial(unwrap_kernel, rows_out), grid=(n // per...  13.5 us
    another operation x3, other arithmetic, network_maps(): factor = jnp.linalg.cholesky(normal_matrix)  9.36 us
    pallas_call x1, Pallas kernels, invert(): pl.pallas_call(functools.partial(invert_kernel, rows), in_specs=[whole, w...  8.27 us
    all_to_all x1, starting transfers between devices, on_device(): lax.all_to_all(current, 'ifg', split_axis=0, concat_axis=0, tiled=True)  8.16 us
    another operation x2, other arithmetic, network_maps(): pseudo = jax.scipy.linalg.cho_solve((factor, True), design.T)  7.94 us
    ppermute x2, starting transfers between devices, extended_2(): lax.ppermute(lax.slice_in_dim(block, 0, width, axis=dim), axis, backward)  7.81 us
    ppermute x2, waiting for transfers between devices, extended_2(): lax.ppermute(lax.slice_in_dim(block, 0, width, axis=dim), axis, backward)  7.23 us
    ppermute x2, starting transfers between devices, extended_2(): lax.ppermute(lax.slice_in_dim(block, block.shape[dim] - width, None, axis...  6.2 us
  transfers between devices with their start and end apart: 7, of which 5 were waited for; matrix products, arithmetic and copies ran while one was open for 20% of the time, Pallas kernels for 0%

profile of v8, /device:TPU:9, one launch (start us, length us, event | category | flops | bytes accessed | tf_op | source)
XLA Modules:
  0.0 99.5 jit_solution(16237825291549000513)
XLA Ops:
  0.6 1.3 %slice_bitcast_fusion = (f32[1,8,4,2048]{3,2,1,0:T(4,128)S(1)}, f32[1,8,4,2048]{3,2,1,0:T(4,128)S(1)}) fusion(f32[8,32,2048]{2,1,0:T(8,128)} %ph_ref.1), kind=kLoop, calls=%fused_computation.21 | loop fusion | bytes 1048576 | tf_op jit(solution)/shard_map/stack | solution.py:186
  1.9 1.3 %convert_bitcast_fusion = (f32[1,8,4,2048]{3,2,1,0:T(4,128)S(1)}, f32[1,8,4,2048]{3,2,1,0:T(4,128)S(1)}) fusion(s32[8,32,2048]{2,1,0:T(8,128)} %wt_ref.1), kind=kLoop, calls=%fused_computation.20 | loop fusion | flops 131072 | bytes 1048576 | tf_op jit(solution)/shard_map/stack | solution.py:186
  3.4 5.2 %collective-permute-start = (f32[2,8,4,2048]{3,2,1,0:T(4,128)S(1)}, f32[2,8,4,2048]{3,2,1,0:T(4,128)S(1)}, u32[]{:S(2)}, u32[]{:S(2)}) collective-permute-start(f32[2,8,4,2048]{3,2,1,0:T(4,128)S(1)} %pad_maximum_fusion.1), channel_id=1, source_target_pairs={{0,1},{1,2},{2,3},{4,5},{5,6},{6,7},{8,9},{9,10},{10,11},{12,13},{... | collective-permute-start | bytes 1572872 | tf_op jit(solution)/shard_map/ppermute | solution.py:187
  8.7 1.9 %collective-permute-start.1 = (f32[2,8,4,2048]{3,2,1,0:T(4,128)S(1)}, f32[2,8,4,2048]{3,2,1,0:T(4,128)S(1)}, u32[]{:S(2)}, u32[]{:S(2)}) collective-permute-start(f32[2,8,4,2048]{3,2,1,0:T(4,128)S(1)} %pad_maximum_fusion.2), channel_id=1, source_target_pairs={{1,0},{2,1},{3,2},{5,4},{6,5},{7,6},{9,8},{10,9},{11,10},{13,12},{... | collective-permute-start | bytes 1572872 | tf_op jit(solution)/shard_map/ppermute | solution.py:188
  10.7 4.0 %collective-permute-done.top_ref = f32[2,8,4,2048]{3,2,1,0:T(4,128)S(1)} collective-permute-done((f32[2,8,4,2048]{3,2,1,0:T(4,128)S(1)}, f32[2,8,4,2048]{3,2,1,0:T(4,128)S(1)}, u32[]{:S(2)}, u32[]{:S(2)}) %collective-permute-start) | collective-permute-done | bytes 524320 | tf_op jit(solution)/shard_map/ppermute | solution.py:187
  14.7 6.0 %collective-permute-done.1.bot_ref = f32[2,8,4,2048]{3,2,1,0:T(4,128)S(1)} collective-permute-done((f32[2,8,4,2048]{3,2,1,0:T(4,128)S(1)}, f32[2,8,4,2048]{3,2,1,0:T(4,128)S(1)}, u32[]{:S(2)}, u32[]{:S(2)}) %collective-permute-start.1) | collective-permute-done | bytes 524320 | tf_op jit(solution)/shard_map/ppermute | solution.py:188
  20.8 0.8 copy-done.3
  21.5 13.5 %shard_map.50 = f32[32,8,16,128]{3,2,1,0:T(8,128)} custom-call(f32[8,32,2048]{2,1,0:T(8,128)} %ph_ref.1, s32[8,32,2048]{2,1,0:T(8,128)} %wt_ref.1, f32[2,8,4,2048]{3,2,1,0:T(4,128)} %copy-done.2, f32[2,8,4,2048]{3,2,1,0:T(4,128)} %copy-done.3), custom_call_target="tpu_custom_call" | custom-call | flops 78643200 | bytes 7340032 | tf_op jit(solution)/shard_map/pallas_call | solution.py:98
  35.1 8.2 %all-to-all-start = ((f32[32,8,16,128]{3,2,1,0:T(8,128)}), f32[32,8,16,128]{3,2,1,0:T(8,128)S(1)}, u32[]{:S(2)}, u32[]{:S(2)}) async-start(f32[32,8,16,128]{3,2,1,0:T(8,128)} %shard_map.50), calls=%async_computation | async-start | bytes 4194304 | tf_op jit(solution)/shard_map/all_to_all | solution.py:190
  43.3 0.5 fusion.12
  43.9 8.7 %cholesky.16 = f32[95,95]{1,0:T(8,128)S(1)} custom-call(f32[95,95]{1,0:T(8,128)S(1)} %fusion.17), custom_call_target="Cholesky" | custom-call | tf_op jit(solution)/shard_map/jit(cholesky)/cholesky | solution.py:174
  52.7 0.6 compare_reduce_fusion
  53.3 0.7 fusion.13
  54.0 7.3 %custom-call.10 = f32[1,95,95]{1,2,0:T(8,128)S(1)} custom-call(f32[1,95,95]{2,1,0:T(8,128)S(1)} %fusion.13), custom_call_target="InvertDiagBlocksLowerTriangular" | custom-call | tf_op jit(solution)/shard_map/jit(_cho_solve)/triangular_solve | solution.py:175
  61.3 0.4 fusion.11
  61.6 0.2 fusion.14
  61.9 0.6 pad.8.pseudo_ref
  62.5 0.1 convert_subtract_fusion
  62.7 0.7 pad.9.design_ref
  63.4 1.3 %copy-done.1 = f32[32,8,16,128]{3,2,1,0:T(8,128)} copy-done((f32[32,8,16,128]{3,2,1,0:T(8,128)}, f32[32,8,16,128]{3,2,1,0:T(8,128)S(1)}, u32[]{:S(2)}) %copy-start.1) | copy-done | bytes 2097176
  64.7 8.3 %shard_map.51 = (f32[2048,96]{1,0:T(8,128)}, f32[2048,256]{1,0:T(8,128)}) custom-call(f32[4096,128]{1,0:T(8,128)} %bitcast.33, f32[96,256]{1,0:T(8,128)} %pad.8.pseudo_ref, f32[256,96]{1,0:T(8,128)} %pad.9.design_ref), custom_call_target="tpu_custom_call" | custom-call | flops 1207959552 | bytes 4980736 | tf_op jit(solution)/shard_map/pallas_call | solution.py:139
  73.0 1.1 %fusion.20 = (f32[256,2,64]{0,2,1:T(8,128)S(1)}, f32[256,2,64]{0,2,1:T(8,128)S(1)}) fusion(f32[256,32,64]{0,2,1:T(8,128)} %bitcast.30), kind=kLoop, calls=%fused_computation.46 | loop fusion | bytes 524288 | tf_op jit(solution)/shard_map/slice | solution.py:25
  74.1 3.8 %collective-permute-start.2 = (f32[256,2,64]{0,2,1:T(8,128)S(1)}, f32[256,2,64]{0,2,1:T(8,128)S(1)}, u32[]{:S(2)}, u32[]{:S(2)}) collective-permute-start(f32[256,2,64]{0,2,1:T(8,128)S(1)} %get-tuple-element.8), channel_id=1, source_target_pairs={{0,1},{1,2},{2,3},{4,5},{5,6},{6,7},{8,9},{9,10},{10,11},{12,13},{... | collective-permute-start | bytes 393224 | tf_op jit(solution)/shard_map/ppermute | solution.py:24
  77.9 1.9 %collective-permute-start.3 = (f32[256,2,64]{0,2,1:T(8,128)S(1)}, f32[256,2,64]{0,2,1:T(8,128)S(1)}, u32[]{:S(2)}, u32[]{:S(2)}) collective-permute-start(f32[256,2,64]{0,2,1:T(8,128)S(1)} %get-tuple-element.9), channel_id=1, source_target_pairs={{1,0},{2,1},{3,2},{5,4},{6,5},{7,6},{9,8},{10,9},{11,10},{13,12},{... | collective-permute-start | bytes 393224 | tf_op jit(solution)/shard_map/ppermute | solution.py:27
  79.9 5.9 %collective-permute-done.3 = f32[256,2,64]{0,2,1:T(8,128)S(1)} collective-permute-done((f32[256,2,64]{0,2,1:T(8,128)S(1)}, f32[256,2,64]{0,2,1:T(8,128)S(1)}, u32[]{:S(2)}, u32[]{:S(2)}) %collective-permute-start.3) | collective-permute-done | bytes 131104 | tf_op jit(solution)/shard_map/ppermute | solution.py:27
  85.7 1.1 %pad_maximum_fusion.5 = (f32[256,36,2]{0,2,1:T(2,128)S(1)}, f32[256,36,2]{0,2,1:T(2,128)S(1)}) fusion(f32[256,2,64]{0,2,1:T(8,128)S(1)} %collective-permute-done.3, f32[256,32,64]{0,2,1:T(8,128)} %bitcast.31, f32[256,2,64]{0,2,1:T(8,128)S(1)} %collective-permute-done.2), kind=kLoop, calls=%fused_computation.30 | loop fusion | flops 73728 | bytes 2506752 | tf_op jit(solution)/shard_map/slice | solution.py:25
  86.8 2.4 %collective-permute-start.4 = (f32[256,36,2]{0,2,1:T(2,128)S(1)}, f32[256,36,2]{0,2,1:T(2,128)S(1)}, u32[]{:S(2)}, u32[]{:S(2)}) collective-permute-start(f32[256,36,2]{0,2,1:T(2,128)S(1)} %get-tuple-element.6), channel_id=1, source_target_pairs={{0,4},{4,8},{8,12},{12,16},{16,20},{20,24},{24,28},{28,32},{32,36}... | collective-permute-start | bytes 221192 | tf_op jit(solution)/shard_map/ppermute | solution.py:24
  89.2 5.9 %collective-permute-start.5 = (f32[256,36,2]{0,2,1:T(2,128)S(1)}, f32[256,36,2]{0,2,1:T(2,128)S(1)}, u32[]{:S(2)}, u32[]{:S(2)}) collective-permute-start(f32[256,36,2]{0,2,1:T(2,128)S(1)} %get-tuple-element.7), channel_id=1, source_target_pairs={{4,0},{8,4},{12,8},{16,12},{20,16},{24,20},{28,24},{32,28},{36,32}... | collective-permute-start | bytes 221192 | tf_op jit(solution)/shard_map/ppermute | solution.py:27
  95.1 1.4 %collective-permute-done.5 = f32[256,36,2]{0,2,1:T(2,128)S(1)} collective-permute-done((f32[256,36,2]{0,2,1:T(2,128)S(1)}, f32[256,36,2]{0,2,1:T(2,128)S(1)}, u32[]{:S(2)}, u32[]{:S(2)}) %collective-permute-start.5) | collective-permute-done | bytes 73760 | tf_op jit(solution)/shard_map/ppermute | solution.py:27
  96.5 0.3 pad_maximum_fusion
  96.8 0.5 fusion
  97.4 2.1 %fusion.5 = bf16[256,32,64]{0,2,1:T(8,128)(2,1)} fusion(f32[256,32,68]{0,2,1:T(8,128)S(1)} %fusion), kind=kLoop, calls=%fused_computation.11 | loop fusion | flops 4718592 | bytes 11534336 | tf_op jit(solution)/shard_map/convert_element_type | solution.py:202
  (17 shorter events, 0.5 us)
Async XLA Ops:
  3.4 11.3 %collective-permute-start = (f32[2,8,4,2048]{3,2,1,0:T(4,128)S(1)}, f32[2,8,4,2048]{3,2,1,0:T(4,128)S(1)}, u32[]{:S(2)}, u32[]{:S(2)}) collective-permute-start(f32[2,8,4,2048]{3,2,1,0:T(4,128)S(1)} %pad_maximum_fusion.1), channel_id=1, source_target_pairs={{0,1},{1,2},{2,3},{4,5},{5,6},{6,7},{8,9},{9,10},{10,11},{12,13},{... | collective-permute-start | bytes 1572872 | tf_op jit(solution)/shard_map/ppermute | solution.py:187
  8.7 12.0 %collective-permute-start.1 = (f32[2,8,4,2048]{3,2,1,0:T(4,128)S(1)}, f32[2,8,4,2048]{3,2,1,0:T(4,128)S(1)}, u32[]{:S(2)}, u32[]{:S(2)}) collective-permute-start(f32[2,8,4,2048]{3,2,1,0:T(4,128)S(1)} %pad_maximum_fusion.2), channel_id=1, source_target_pairs={{1,0},{2,1},{3,2},{5,4},{6,5},{7,6},{9,8},{10,9},{11,10},{13,12},{... | collective-permute-start | bytes 1572872 | tf_op jit(solution)/shard_map/ppermute | solution.py:188
  14.7 6.0 %copy-start.2 = (f32[2,8,4,2048]{3,2,1,0:T(4,128)}, f32[2,8,4,2048]{3,2,1,0:T(4,128)S(1)}, u32[]{:S(2)}) copy-start(f32[2,8,4,2048]{3,2,1,0:T(4,128)S(1)} %collective-permute-done.top_ref) | copy-start | bytes 1572868
  20.8 0.8 copy-start.3
  35.1 8.2 %copy-start.4 = (s32[256,2]{0,1:T(2,128)S(1)}, s32[256,2]{0,1:T(2,128)}, u32[]{:S(2)}) copy-start(s32[256,2]{0,1:T(2,128)} %param.5) | copy-start | bytes 6148
  35.1 28.3 %all-to-all-start = ((f32[32,8,16,128]{3,2,1,0:T(8,128)}), f32[32,8,16,128]{3,2,1,0:T(8,128)S(1)}, u32[]{:S(2)}, u32[]{:S(2)}) async-start(f32[32,8,16,128]{3,2,1,0:T(8,128)} %shard_map.50), calls=%async_computation | async-start | bytes 4194304 | tf_op jit(solution)/shard_map/all_to_all | solution.py:190
  63.4 1.3 %copy-start.1 = (f32[32,8,16,128]{3,2,1,0:T(8,128)}, f32[32,8,16,128]{3,2,1,0:T(8,128)S(1)}, u32[]{:S(2)}) copy-start(f32[32,8,16,128]{3,2,1,0:T(8,128)S(1)} %all-to-all-done) | copy-start | bytes 6291460
  73.0 23.5 %copy-start = (f32[2048,256]{1,0:T(8,128)S(1)}, f32[2048,256]{1,0:T(8,128)}, u32[]{:S(2)}) copy-start(f32[2048,256]{1,0:T(8,128)} %get-tuple-element.5) | copy-start | bytes 6291460
  74.1 5.7 %collective-permute-start.2 = (f32[256,2,64]{0,2,1:T(8,128)S(1)}, f32[256,2,64]{0,2,1:T(8,128)S(1)}, u32[]{:S(2)}, u32[]{:S(2)}) collective-permute-start(f32[256,2,64]{0,2,1:T(8,128)S(1)} %get-tuple-element.8), channel_id=1, source_target_pairs={{0,1},{1,2},{2,3},{4,5},{5,6},{6,7},{8,9},{9,10},{10,11},{12,13},{... | collective-permute-start | bytes 393224 | tf_op jit(solution)/shard_map/ppermute | solution.py:24
  77.9 7.8 %collective-permute-start.3 = (f32[256,2,64]{0,2,1:T(8,128)S(1)}, f32[256,2,64]{0,2,1:T(8,128)S(1)}, u32[]{:S(2)}, u32[]{:S(2)}) collective-permute-start(f32[256,2,64]{0,2,1:T(8,128)S(1)} %get-tuple-element.9), channel_id=1, source_target_pairs={{1,0},{2,1},{3,2},{5,4},{6,5},{7,6},{9,8},{10,9},{11,10},{13,12},{... | collective-permute-start | bytes 393224 | tf_op jit(solution)/shard_map/ppermute | solution.py:27
  86.8 8.3 %collective-permute-start.4 = (f32[256,36,2]{0,2,1:T(2,128)S(1)}, f32[256,36,2]{0,2,1:T(2,128)S(1)}, u32[]{:S(2)}, u32[]{:S(2)}) collective-permute-start(f32[256,36,2]{0,2,1:T(2,128)S(1)} %get-tuple-element.6), channel_id=1, source_target_pairs={{0,4},{4,8},{8,12},{12,16},{16,20},{20,24},{24,28},{28,32},{32,36}... | collective-permute-start | bytes 221192 | tf_op jit(solution)/shard_map/ppermute | solution.py:24
  89.2 7.3 %collective-permute-start.5 = (f32[256,36,2]{0,2,1:T(2,128)S(1)}, f32[256,36,2]{0,2,1:T(2,128)S(1)}, u32[]{:S(2)}, u32[]{:S(2)}) collective-permute-start(f32[256,36,2]{0,2,1:T(2,128)S(1)} %get-tuple-element.7), channel_id=1, source_target_pairs={{4,0},{8,4},{12,8},{16,12},{20,16},{24,20},{28,24},{32,28},{36,32}... | collective-permute-start | bytes 221192 | tf_op jit(solution)/shard_map/ppermute | solution.py:27

commit v9 on v8

--- a/solution.py
+++ b/solution.py
@@ -119,8 +119,8 @@
     design = design_ref[...]
     for k in range(rows):
         x = x_ref[pl.ds(k, ifg, stride=rows), :]
-        series = jnp.dot(pseudo, x, precision=lax.Precision.HIGHEST, preferred_element_type=jnp.float32)
-        fit = jnp.dot(design, series, precision=lax.Precision.HIGHEST, preferred_element_type=jnp.float32)
+        series = jnp.dot(pseudo, x, precision=lax.Precision.HIGH, preferred_element_type=jnp.float32)
+        fit = jnp.dot(design, series, precision=lax.Precision.HIGH, preferred_element_type=jnp.float32)
         res_t = (x - fit).T
         ser_t = series.T
         r_ref[pl.ds(k * 64, 64), :] = res_t[:64]

time: 100 us -> 98.6 us (0.986)
  Pallas kernels: 21.8 us -> 20.1 us
    pallas_call x1, Pallas kernels: 8.27 us -> 6.56 us  [invert(): pl.pallas_call(functools.partial(invert_kernel, rows), in_specs=[whole, w...]
  transfers between devices with their start and end apart: 7 -> 7, of which waited for: 5 -> 5; matrix products, arithmetic and copies ran while one was open for 20% -> 21% of each run, Pallas kernels for 0% -> 0%
where the time goes in v9:
time: 98.6 us; the launch traced here: 97.8 us
  starting transfers between devices  29.3 us (30%)
  other arithmetic  23 us (23%)
  Pallas kernels  20.1 us (20%)
  waiting for transfers between devices  17.4 us (18%)
  local copies, waits for them, and re-layouts  5.98 us (6%)
  matrix products  1.16 us (1%)
    pallas_call x1, Pallas kernels, unwrap(): pl.pallas_call(functools.partial(unwrap_kernel, rows_out), grid=(n // per...  13.5 us
    another operation x3, other arithmetic, network_maps(): factor = jnp.linalg.cholesky(normal_matrix)  9.36 us
    all_to_all x1, starting transfers between devices, on_device(): lax.all_to_all(current, 'ifg', split_axis=0, concat_axis=0, tiled=True)  8.16 us
    another operation x2, other arithmetic, network_maps(): pseudo = jax.scipy.linalg.cho_solve((factor, True), design.T)  7.94 us
    ppermute x2, starting transfers between devices, extended_2(): lax.ppermute(lax.slice_in_dim(block, 0, width, axis=dim), axis, backward)  7.81 us
    ppermute x2, waiting for transfers between devices, extended_2(): lax.ppermute(lax.slice_in_dim(block, 0, width, axis=dim), axis, backward)  7.23 us
    pallas_call x1, Pallas kernels, invert(): pl.pallas_call(functools.partial(invert_kernel, rows), in_specs=[whole, w...  6.56 us
    ppermute x2, starting transfers between devices, extended_2(): lax.ppermute(lax.slice_in_dim(block, block.shape[dim] - width, None, axis...  6.2 us
  transfers between devices with their start and end apart: 7, of which 5 were waited for; matrix products, arithmetic and copies ran while one was open for 21% of the time, Pallas kernels for 0%

profile of v9, /device:TPU:9, one launch (start us, length us, event | category | flops | bytes accessed | tf_op | source)
XLA Modules:
  0.0 97.8 jit_solution(5350549823235692762)
XLA Ops:
  0.6 1.3 %slice_bitcast_fusion = (f32[1,8,4,2048]{3,2,1,0:T(4,128)S(1)}, f32[1,8,4,2048]{3,2,1,0:T(4,128)S(1)}) fusion(f32[8,32,2048]{2,1,0:T(8,128)} %ph_ref.1), kind=kLoop, calls=%fused_computation.21 | loop fusion | bytes 1048576 | tf_op jit(solution)/shard_map/stack | solution.py:186
  1.9 1.3 %convert_bitcast_fusion = (f32[1,8,4,2048]{3,2,1,0:T(4,128)S(1)}, f32[1,8,4,2048]{3,2,1,0:T(4,128)S(1)}) fusion(s32[8,32,2048]{2,1,0:T(8,128)} %wt_ref.1), kind=kLoop, calls=%fused_computation.20 | loop fusion | flops 131072 | bytes 1048576 | tf_op jit(solution)/shard_map/stack | solution.py:186
  3.4 5.2 %collective-permute-start = (f32[2,8,4,2048]{3,2,1,0:T(4,128)S(1)}, f32[2,8,4,2048]{3,2,1,0:T(4,128)S(1)}, u32[]{:S(2)}, u32[]{:S(2)}) collective-permute-start(f32[2,8,4,2048]{3,2,1,0:T(4,128)S(1)} %pad_maximum_fusion.1), channel_id=1, source_target_pairs={{0,1},{1,2},{2,3},{4,5},{5,6},{6,7},{8,9},{9,10},{10,11},{12,13},{... | collective-permute-start | bytes 1572872 | tf_op jit(solution)/shard_map/ppermute | solution.py:187
  8.7 1.9 %collective-permute-start.1 = (f32[2,8,4,2048]{3,2,1,0:T(4,128)S(1)}, f32[2,8,4,2048]{3,2,1,0:T(4,128)S(1)}, u32[]{:S(2)}, u32[]{:S(2)}) collective-permute-start(f32[2,8,4,2048]{3,2,1,0:T(4,128)S(1)} %pad_maximum_fusion.2), channel_id=1, source_target_pairs={{1,0},{2,1},{3,2},{5,4},{6,5},{7,6},{9,8},{10,9},{11,10},{13,12},{... | collective-permute-start | bytes 1572872 | tf_op jit(solution)/shard_map/ppermute | solution.py:188
  10.7 4.0 %collective-permute-done.top_ref = f32[2,8,4,2048]{3,2,1,0:T(4,128)S(1)} collective-permute-done((f32[2,8,4,2048]{3,2,1,0:T(4,128)S(1)}, f32[2,8,4,2048]{3,2,1,0:T(4,128)S(1)}, u32[]{:S(2)}, u32[]{:S(2)}) %collective-permute-start) | collective-permute-done | bytes 524320 | tf_op jit(solution)/shard_map/ppermute | solution.py:187
  14.7 6.0 %collective-permute-done.1.bot_ref = f32[2,8,4,2048]{3,2,1,0:T(4,128)S(1)} collective-permute-done((f32[2,8,4,2048]{3,2,1,0:T(4,128)S(1)}, f32[2,8,4,2048]{3,2,1,0:T(4,128)S(1)}, u32[]{:S(2)}, u32[]{:S(2)}) %collective-permute-start.1) | collective-permute-done | bytes 524320 | tf_op jit(solution)/shard_map/ppermute | solution.py:188
  20.8 0.8 copy-done.3
  21.5 13.5 %shard_map.50 = f32[32,8,16,128]{3,2,1,0:T(8,128)} custom-call(f32[8,32,2048]{2,1,0:T(8,128)} %ph_ref.1, s32[8,32,2048]{2,1,0:T(8,128)} %wt_ref.1, f32[2,8,4,2048]{3,2,1,0:T(4,128)} %copy-done.2, f32[2,8,4,2048]{3,2,1,0:T(4,128)} %copy-done.3), custom_call_target="tpu_custom_call" | custom-call | flops 78643200 | bytes 7340032 | tf_op jit(solution)/shard_map/pallas_call | solution.py:98
  35.1 8.2 %all-to-all-start = ((f32[32,8,16,128]{3,2,1,0:T(8,128)}), f32[32,8,16,128]{3,2,1,0:T(8,128)S(1)}, u32[]{:S(2)}, u32[]{:S(2)}) async-start(f32[32,8,16,128]{3,2,1,0:T(8,128)} %shard_map.50), calls=%async_computation | async-start | bytes 4194304 | tf_op jit(solution)/shard_map/all_to_all | solution.py:190
  43.3 0.5 fusion.12
  43.9 8.7 %cholesky.16 = f32[95,95]{1,0:T(8,128)S(1)} custom-call(f32[95,95]{1,0:T(8,128)S(1)} %fusion.17), custom_call_target="Cholesky" | custom-call | tf_op jit(solution)/shard_map/jit(cholesky)/cholesky | solution.py:174
  52.7 0.6 compare_reduce_fusion
  53.3 0.7 fusion.13
  54.0 7.3 %custom-call.10 = f32[1,95,95]{1,2,0:T(8,128)S(1)} custom-call(f32[1,95,95]{2,1,0:T(8,128)S(1)} %fusion.13), custom_call_target="InvertDiagBlocksLowerTriangular" | custom-call | tf_op jit(solution)/shard_map/jit(_cho_solve)/triangular_solve | solution.py:175
  61.3 0.4 fusion.11
  61.6 0.2 fusion.14
  61.9 0.6 pad.8.pseudo_ref
  62.5 0.1 convert_subtract_fusion
  62.7 0.7 pad.9.design_ref
  63.4 1.3 %copy-done.1 = f32[32,8,16,128]{3,2,1,0:T(8,128)} copy-done((f32[32,8,16,128]{3,2,1,0:T(8,128)}, f32[32,8,16,128]{3,2,1,0:T(8,128)S(1)}, u32[]{:S(2)}) %copy-start.1) | copy-done | bytes 2097176
  64.7 6.6 %shard_map.51 = (f32[2048,96]{1,0:T(8,128)}, f32[2048,256]{1,0:T(8,128)}) custom-call(f32[4096,128]{1,0:T(8,128)} %bitcast.33, f32[96,256]{1,0:T(8,128)} %pad.8.pseudo_ref, f32[256,96]{1,0:T(8,128)} %pad.9.design_ref), custom_call_target="tpu_custom_call" | custom-call | flops 1207959552 | bytes 4980736 | tf_op jit(solution)/shard_map/pallas_call | solution.py:139
  71.3 1.1 %fusion.20 = (f32[256,2,64]{0,2,1:T(8,128)S(1)}, f32[256,2,64]{0,2,1:T(8,128)S(1)}) fusion(f32[256,32,64]{0,2,1:T(8,128)} %bitcast.30), kind=kLoop, calls=%fused_computation.46 | loop fusion | bytes 524288 | tf_op jit(solution)/shard_map/slice | solution.py:25
  72.4 3.8 %collective-permute-start.2 = (f32[256,2,64]{0,2,1:T(8,128)S(1)}, f32[256,2,64]{0,2,1:T(8,128)S(1)}, u32[]{:S(2)}, u32[]{:S(2)}) collective-permute-start(f32[256,2,64]{0,2,1:T(8,128)S(1)} %get-tuple-element.8), channel_id=1, source_target_pairs={{0,1},{1,2},{2,3},{4,5},{5,6},{6,7},{8,9},{9,10},{10,11},{12,13},{... | collective-permute-start | bytes 393224 | tf_op jit(solution)/shard_map/ppermute | solution.py:24
  76.2 1.9 %collective-permute-start.3 = (f32[256,2,64]{0,2,1:T(8,128)S(1)}, f32[256,2,64]{0,2,1:T(8,128)S(1)}, u32[]{:S(2)}, u32[]{:S(2)}) collective-permute-start(f32[256,2,64]{0,2,1:T(8,128)S(1)} %get-tuple-element.9), channel_id=1, source_target_pairs={{1,0},{2,1},{3,2},{5,4},{6,5},{7,6},{9,8},{10,9},{11,10},{13,12},{... | collective-permute-start | bytes 393224 | tf_op jit(solution)/shard_map/ppermute | solution.py:27
  78.2 5.9 %collective-permute-done.3 = f32[256,2,64]{0,2,1:T(8,128)S(1)} collective-permute-done((f32[256,2,64]{0,2,1:T(8,128)S(1)}, f32[256,2,64]{0,2,1:T(8,128)S(1)}, u32[]{:S(2)}, u32[]{:S(2)}) %collective-permute-start.3) | collective-permute-done | bytes 131104 | tf_op jit(solution)/shard_map/ppermute | solution.py:27
  84.0 1.1 %pad_maximum_fusion.5 = (f32[256,36,2]{0,2,1:T(2,128)S(1)}, f32[256,36,2]{0,2,1:T(2,128)S(1)}) fusion(f32[256,2,64]{0,2,1:T(8,128)S(1)} %collective-permute-done.3, f32[256,32,64]{0,2,1:T(8,128)} %bitcast.31, f32[256,2,64]{0,2,1:T(8,128)S(1)} %collective-permute-done.2), kind=kLoop, calls=%fused_computation.30 | loop fusion | flops 73728 | bytes 2506752 | tf_op jit(solution)/shard_map/slice | solution.py:25
  85.1 2.4 %collective-permute-start.4 = (f32[256,36,2]{0,2,1:T(2,128)S(1)}, f32[256,36,2]{0,2,1:T(2,128)S(1)}, u32[]{:S(2)}, u32[]{:S(2)}) collective-permute-start(f32[256,36,2]{0,2,1:T(2,128)S(1)} %get-tuple-element.6), channel_id=1, source_target_pairs={{0,4},{4,8},{8,12},{12,16},{16,20},{20,24},{24,28},{28,32},{32,36}... | collective-permute-start | bytes 221192 | tf_op jit(solution)/shard_map/ppermute | solution.py:24
  87.5 5.9 %collective-permute-start.5 = (f32[256,36,2]{0,2,1:T(2,128)S(1)}, f32[256,36,2]{0,2,1:T(2,128)S(1)}, u32[]{:S(2)}, u32[]{:S(2)}) collective-permute-start(f32[256,36,2]{0,2,1:T(2,128)S(1)} %get-tuple-element.7), channel_id=1, source_target_pairs={{4,0},{8,4},{12,8},{16,12},{20,16},{24,20},{28,24},{32,28},{36,32}... | collective-permute-start | bytes 221192 | tf_op jit(solution)/shard_map/ppermute | solution.py:27
  93.4 1.4 %collective-permute-done.5 = f32[256,36,2]{0,2,1:T(2,128)S(1)} collective-permute-done((f32[256,36,2]{0,2,1:T(2,128)S(1)}, f32[256,36,2]{0,2,1:T(2,128)S(1)}, u32[]{:S(2)}, u32[]{:S(2)}) %collective-permute-start.5) | collective-permute-done | bytes 73760 | tf_op jit(solution)/shard_map/ppermute | solution.py:27
  94.8 0.3 pad_maximum_fusion
  95.1 0.5 fusion
  95.6 2.1 %fusion.5 = bf16[256,32,64]{0,2,1:T(8,128)(2,1)} fusion(f32[256,32,68]{0,2,1:T(8,128)S(1)} %fusion), kind=kLoop, calls=%fused_computation.11 | loop fusion | flops 4718592 | bytes 11534336 | tf_op jit(solution)/shard_map/convert_element_type | solution.py:202
  (17 shorter events, 0.5 us)
Async XLA Ops:
  3.4 11.3 %collective-permute-start = (f32[2,8,4,2048]{3,2,1,0:T(4,128)S(1)}, f32[2,8,4,2048]{3,2,1,0:T(4,128)S(1)}, u32[]{:S(2)}, u32[]{:S(2)}) collective-permute-start(f32[2,8,4,2048]{3,2,1,0:T(4,128)S(1)} %pad_maximum_fusion.1), channel_id=1, source_target_pairs={{0,1},{1,2},{2,3},{4,5},{5,6},{6,7},{8,9},{9,10},{10,11},{12,13},{... | collective-permute-start | bytes 1572872 | tf_op jit(solution)/shard_map/ppermute | solution.py:187
  8.7 12.0 %collective-permute-start.1 = (f32[2,8,4,2048]{3,2,1,0:T(4,128)S(1)}, f32[2,8,4,2048]{3,2,1,0:T(4,128)S(1)}, u32[]{:S(2)}, u32[]{:S(2)}) collective-permute-start(f32[2,8,4,2048]{3,2,1,0:T(4,128)S(1)} %pad_maximum_fusion.2), channel_id=1, source_target_pairs={{1,0},{2,1},{3,2},{5,4},{6,5},{7,6},{9,8},{10,9},{11,10},{13,12},{... | collective-permute-start | bytes 1572872 | tf_op jit(solution)/shard_map/ppermute | solution.py:188
  14.7 6.0 %copy-start.2 = (f32[2,8,4,2048]{3,2,1,0:T(4,128)}, f32[2,8,4,2048]{3,2,1,0:T(4,128)S(1)}, u32[]{:S(2)}) copy-start(f32[2,8,4,2048]{3,2,1,0:T(4,128)S(1)} %collective-permute-done.top_ref) | copy-start | bytes 1572868
  20.8 0.8 copy-start.3
  35.1 8.2 %copy-start.4 = (s32[256,2]{0,1:T(2,128)S(1)}, s32[256,2]{0,1:T(2,128)}, u32[]{:S(2)}) copy-start(s32[256,2]{0,1:T(2,128)} %param.5) | copy-start | bytes 6148
  35.1 28.3 %all-to-all-start = ((f32[32,8,16,128]{3,2,1,0:T(8,128)}), f32[32,8,16,128]{3,2,1,0:T(8,128)S(1)}, u32[]{:S(2)}, u32[]{:S(2)}) async-start(f32[32,8,16,128]{3,2,1,0:T(8,128)} %shard_map.50), calls=%async_computation | async-start | bytes 4194304 | tf_op jit(solution)/shard_map/all_to_all | solution.py:190
  63.4 1.3 %copy-start.1 = (f32[32,8,16,128]{3,2,1,0:T(8,128)}, f32[32,8,16,128]{3,2,1,0:T(8,128)S(1)}, u32[]{:S(2)}) copy-start(f32[32,8,16,128]{3,2,1,0:T(8,128)S(1)} %all-to-all-done) | copy-start | bytes 6291460
  71.3 23.5 %copy-start = (f32[2048,256]{1,0:T(8,128)S(1)}, f32[2048,256]{1,0:T(8,128)}, u32[]{:S(2)}) copy-start(f32[2048,256]{1,0:T(8,128)} %get-tuple-element.5) | copy-start | bytes 6291460
  72.4 5.7 %collective-permute-start.2 = (f32[256,2,64]{0,2,1:T(8,128)S(1)}, f32[256,2,64]{0,2,1:T(8,128)S(1)}, u32[]{:S(2)}, u32[]{:S(2)}) collective-permute-start(f32[256,2,64]{0,2,1:T(8,128)S(1)} %get-tuple-element.8), channel_id=1, source_target_pairs={{0,1},{1,2},{2,3},{4,5},{5,6},{6,7},{8,9},{9,10},{10,11},{12,13},{... | collective-permute-start | bytes 393224 | tf_op jit(solution)/shard_map/ppermute | solution.py:24
  76.2 7.8 %collective-permute-start.3 = (f32[256,2,64]{0,2,1:T(8,128)S(1)}, f32[256,2,64]{0,2,1:T(8,128)S(1)}, u32[]{:S(2)}, u32[]{:S(2)}) collective-permute-start(f32[256,2,64]{0,2,1:T(8,128)S(1)} %get-tuple-element.9), channel_id=1, source_target_pairs={{1,0},{2,1},{3,2},{5,4},{6,5},{7,6},{9,8},{10,9},{11,10},{13,12},{... | collective-permute-start | bytes 393224 | tf_op jit(solution)/shard_map/ppermute | solution.py:27
  85.1 8.3 %collective-permute-start.4 = (f32[256,36,2]{0,2,1:T(2,128)S(1)}, f32[256,36,2]{0,2,1:T(2,128)S(1)}, u32[]{:S(2)}, u32[]{:S(2)}) collective-permute-start(f32[256,36,2]{0,2,1:T(2,128)S(1)} %get-tuple-element.6), channel_id=1, source_target_pairs={{0,4},{4,8},{8,12},{12,16},{16,20},{20,24},{24,28},{28,32},{32,36}... | collective-permute-start | bytes 221192 | tf_op jit(solution)/shard_map/ppermute | solution.py:24
  87.5 7.3 %collective-permute-start.5 = (f32[256,36,2]{0,2,1:T(2,128)S(1)}, f32[256,36,2]{0,2,1:T(2,128)S(1)}, u32[]{:S(2)}, u32[]{:S(2)}) collective-permute-start(f32[256,36,2]{0,2,1:T(2,128)S(1)} %get-tuple-element.7), channel_id=1, source_target_pairs={{4,0},{8,4},{12,8},{16,12},{20,16},{24,20},{28,24},{32,28},{36,32}... | collective-permute-start | bytes 221192 | tf_op jit(solution)/shard_map/ppermute | solution.py:27

commit v10 on v9

--- a/solution.py
+++ b/solution.py
@@ -10,7 +10,8 @@
 
 DATES = 96
 SWEEPS = 4
-HALO = SWEEPS
+FILTER_HALO = 2
+HALO = 8
 PI32 = float(np.float32(np.pi))
 TWO_PI_HI = float(np.float32(2 * np.pi))
 TWO_PI_LO = float(np.float32(2 * np.pi - np.float64(np.float32(2 * np.pi))))
@@ -78,22 +79,23 @@
             nxt = nxt + a_rt * pltpu.roll(cur, nc - 1, 1)
             cur = nxt
         cur_ref[...] = cur
-        half = rows_out // 2
-        upper = cur_ref[pl.ds(HALO, half), :]
-        lower = cur_ref[pl.ds(HALO + half, half), :]
+        half = rows_out // 2 + FILTER_HALO
+        upper = cur_ref[pl.ds(HALO - FILTER_HALO, half), :]
+        lower = cur_ref[pl.ds(HALO - FILTER_HALO + half, half), :]
         lane = lax.broadcasted_iota(jnp.int32, (half, nc), 1) % 128
         first = lane < 64
         even = jnp.where(first, upper, pltpu.roll(lower, 64, 1))
         odd = jnp.where(first, pltpu.roll(upper, nc - 64, 1), lower)
         for m in range(nc // 128):
-            o_ref[2 * m, b] = even[:, 128 * m : 128 * (m + 1)]
-            o_ref[2 * m + 1, b] = odd[:, 128 * m : 128 * (m + 1)]
+            o_ref[2 * m, pl.ds(b * half, half), :] = even[:, 128 * m : 128 * (m + 1)]
+            o_ref[2 * m + 1, pl.ds(b * half, half), :] = odd[:, 128 * m : 128 * (m + 1)]
 
 
 def unwrap(phase, weights, top, bottom):
     n, rows_out, nc = phase.shape
     nr = rows_out + 2 * HALO
-    per = 2
+    per = 4
+    half = rows_out // 2 + FILTER_HALO
     halo_spec = pl.BlockSpec((2, per, HALO, nc), lambda i: (0, i, 0, 0))
     return pl.pallas_call(
         functools.partial(unwrap_kernel, rows_out),
@@ -104,8 +106,8 @@
             halo_spec,
             halo_spec,
         ],
-        out_specs=pl.BlockSpec((nc // 64, per, rows_out // 2, 128), lambda i: (0, i, 0, 0)),
-        out_shape=jax.ShapeDtypeStruct((nc // 64, n, rows_out // 2, 128), jnp.float32),
+        out_specs=pl.BlockSpec((nc // 64, per * half, 128), lambda i: (0, i, 0)),
+        out_shape=jax.ShapeDtypeStruct((nc // 64, n * half, 128), jnp.float32),
         scratch_shapes=[pltpu.VMEM((nr, nc), jnp.float32)] * 3,
         cost_estimate=pl.CostEstimate(
             flops=120 * n * nr * nc, bytes_accessed=4 * n * nc * (2 * nr + rows_out), transcendentals=0
@@ -115,6 +117,7 @@
 
 def invert_kernel(rows, x_ref, pseudo_ref, design_ref, s_ref, r_ref):
     ifg = pseudo_ref.shape[1]
+    own = rows - FILTER_HALO
     pseudo = pseudo_ref[...]
     design = design_ref[...]
     for k in range(rows):
@@ -125,8 +128,10 @@
         ser_t = series.T
         r_ref[pl.ds(k * 64, 64), :] = res_t[:64]
         r_ref[pl.ds((k + rows) * 64, 64), :] = res_t[64:]
-        s_ref[pl.ds(k * 64, 64), :] = ser_t[:64]
-        s_ref[pl.ds((k + rows) * 64, 64), :] = ser_t[64:]
+        if k >= FILTER_HALO:
+            s_ref[pl.ds((k - FILTER_HALO) * 64, 64), :] = ser_t[:64]
+        if k < own:
+            s_ref[pl.ds((k + own) * 64, 64), :] = ser_t[64:]
 
 
 def invert(packed, pseudo, design, rows):
@@ -141,7 +146,7 @@
         in_specs=[whole, whole, whole],
         out_specs=(whole, whole),
         out_shape=(
-            jax.ShapeDtypeStruct((2 * rows * 64, wide), jnp.float32),
+            jax.ShapeDtypeStruct((2 * (rows - FILTER_HALO) * 64, wide), jnp.float32),
             jax.ShapeDtypeStruct((2 * rows * 64, ifg), jnp.float32),
         ),
         cost_estimate=pl.CostEstimate(
@@ -188,16 +193,15 @@
     bottom = lax.ppermute(edge_high, "rows", backward)
     current = unwrap(phase, weights, top, bottom)
     received = lax.all_to_all(current, "ifg", split_axis=0, concat_axis=0, tiled=True)
-    ifg = received.shape[0] * received.shape[1]
-    half = rows // 2
-    series_t, residual_t = invert(received.reshape(ifg * half, 128), pseudo, design, half)
+    half = rows // 2 + FILTER_HALO
+    series_t, residual_t = invert(received.reshape(-1, 128), pseudo, design, half)
 
     def unpack(x):
-        return x.reshape(rows, 64, x.shape[1]).transpose(2, 0, 1)
+        return x.reshape(-1, 64, x.shape[1]).transpose(2, 0, 1)
 
     series_block = unpack(series_t)
     residual = unpack(residual_t)
-    padded = extended_2(residual, (("rows", 1), ("ifg", 2)), 2)
+    padded = extended_2(residual, (("ifg", 2),), FILTER_HALO)
     filtered = binomial(binomial(padded, 1), 2)
     return (series_block, filtered.astype(jnp.bfloat16))
 

time: 98.6 us -> 95.2 us (0.966)
  starting transfers between devices: 29.3 us -> 23.6 us
  Pallas kernels: 20.1 us -> 22.9 us
    ppermute x2 -> x1, waiting for transfers between devices: 7.23 us -> 1.38 us  [extended_2(): lax.ppermute(lax.slice_in_dim(block, 0, width, axis=dim), axis, backward)]
    ppermute x1, waiting for transfers between devices: 4.04 us -> 9.69 us  [on_device(): top = lax.ppermute(edge_low, 'rows', forward)]
    ppermute x2 -> x1, starting transfers between devices: 6.2 us -> 3.1 us  [extended_2(): lax.ppermute(lax.slice_in_dim(block, block.shape[dim] - width, None, axis...]
    pallas_call x1, Pallas kernels: 13.5 us -> 16.5 us  [unwrap(): pl.pallas_call(functools.partial(unwrap_kernel, rows_out), grid=(n // per...]
    ppermute x2 -> x1, starting transfers between devices: 7.81 us -> 5.19 us  [extended_2(): lax.ppermute(lax.slice_in_dim(block, 0, width, axis=dim), axis, backward)]
    concatenate x1, other arithmetic: 0.28 us -> 1.91 us  [extended_2(): block = jnp.concatenate([low, block, high], axis=dim)]
    another operation x2, other arithmetic: 1.44 us -> 0.17 us  [on_device(): jnp.stack([phase[:, :HALO], weights[:, :HALO].astype(jnp.float32)])]
    slice x1 -> x0, other arithmetic: 1.08 us -> none  [extended_2(): lax.slice_in_dim(block, block.shape[dim] - width, None, axis=dim)]
  transfers between devices with their start and end apart: 7 -> 5, of which waited for: 5 -> 3; matrix products, arithmetic and copies ran while one was open for 21% -> 21% of each run, Pallas kernels for 0% -> 0%
where the time goes in v10:
time: 95.2 us; the launch traced here: 94.6 us
  starting transfers between devices  23.6 us (25%)
  Pallas kernels  22.9 us (24%)
  other arithmetic  22.3 us (23%)
  waiting for transfers between devices  17.1 us (18%)
  local copies, waits for them, and re-layouts  6.8 us (7%)
  matrix products  1.15 us (1%)
    pallas_call x1, Pallas kernels, unwrap(): pl.pallas_call(functools.partial(unwrap_kernel, rows_out), grid=(n // per...  16.5 us
    ppermute x1, waiting for transfers between devices, on_device(): top = lax.ppermute(edge_low, 'rows', forward)  9.69 us
    another operation x3, other arithmetic, network_maps(): factor = jnp.linalg.cholesky(normal_matrix)  9.36 us
    all_to_all x1, starting transfers between devices, on_device(): lax.all_to_all(current, 'ifg', split_axis=0, concat_axis=0, tiled=True)  8.16 us
    another operation x2, other arithmetic, network_maps(): pseudo = jax.scipy.linalg.cho_solve((factor, True), design.T)  7.94 us
    pallas_call x1, Pallas kernels, invert(): pl.pallas_call(functools.partial(invert_kernel, rows), in_specs=[whole, w...  6.45 us
    ppermute x1, waiting for transfers between devices, on_device(): bottom = lax.ppermute(edge_high, 'rows', backward)  6 us
    ppermute x1, starting transfers between devices, on_device(): top = lax.ppermute(edge_low, 'rows', forward)  5.21 us
  transfers between devices with their start and end apart: 5, of which 3 were waited for; matrix products, arithmetic and copies ran while one was open for 21% of the time, Pallas kernels for 0%

profile of v10, /device:TPU:9, one launch (start us, length us, event | category | flops | bytes accessed | tf_op | source)
XLA Modules:
  0.0 94.6 jit_solution(4810363620377797861)
XLA Ops:
  0.6 1.4 %slice_bitcast_fusion = (f32[1,8,8,2048]{3,2,1,0:T(8,128)S(1)}, f32[1,8,8,2048]{3,2,1,0:T(8,128)S(1)}) fusion(f32[8,32,2048]{2,1,0:T(8,128)} %ph_ref.1), kind=kLoop, calls=%fused_computation.21 | loop fusion | bytes 2097152 | tf_op jit(solution)/shard_map/stack | solution.py:191
  2.1 0.4 copy-done
  2.5 0.1 convert_bitcast_fusion
  2.6 0.1 pad_maximum_fusion.1
  2.7 5.2 %collective-permute-start = (f32[2,8,8,2048]{3,2,1,0:T(8,128)S(1)}, f32[2,8,8,2048]{3,2,1,0:T(8,128)S(1)}, u32[]{:S(2)}, u32[]{:S(2)}) collective-permute-start(f32[2,8,8,2048]{3,2,1,0:T(8,128)S(1)} %pad_maximum_fusion.1), channel_id=1, source_target_pairs={{0,1},{1,2},{2,3},{4,5},{5,6},{6,7},{8,9},{9,10},{10,11},{12,13},{... | collective-permute-start | bytes 3145736 | tf_op jit(solution)/shard_map/ppermute | solution.py:192
  7.9 0.1 pad_maximum_fusion.2
  8.0 1.9 %collective-permute-start.1 = (f32[2,8,8,2048]{3,2,1,0:T(8,128)S(1)}, f32[2,8,8,2048]{3,2,1,0:T(8,128)S(1)}, u32[]{:S(2)}, u32[]{:S(2)}) collective-permute-start(f32[2,8,8,2048]{3,2,1,0:T(8,128)S(1)} %pad_maximum_fusion.2), channel_id=1, source_target_pairs={{1,0},{2,1},{3,2},{5,4},{6,5},{7,6},{9,8},{10,9},{11,10},{13,12},{... | collective-permute-start | bytes 3145736 | tf_op jit(solution)/shard_map/ppermute | solution.py:193
  10.0 9.7 %collective-permute-done.top_ref = f32[2,8,8,2048]{3,2,1,0:T(8,128)S(1)} collective-permute-done((f32[2,8,8,2048]{3,2,1,0:T(8,128)S(1)}, f32[2,8,8,2048]{3,2,1,0:T(8,128)S(1)}, u32[]{:S(2)}, u32[]{:S(2)}) %collective-permute-start) | collective-permute-done | bytes 1048608 | tf_op jit(solution)/shard_map/ppermute | solution.py:192
  19.7 6.0 %collective-permute-done.1.bot_ref = f32[2,8,8,2048]{3,2,1,0:T(8,128)S(1)} collective-permute-done((f32[2,8,8,2048]{3,2,1,0:T(8,128)S(1)}, f32[2,8,8,2048]{3,2,1,0:T(8,128)S(1)}, u32[]{:S(2)}, u32[]{:S(2)}) %collective-permute-start.1) | collective-permute-done | bytes 1048608 | tf_op jit(solution)/shard_map/ppermute | solution.py:193
  25.7 1.0 %copy-done.3 = f32[2,8,8,2048]{3,2,1,0:T(8,128)} copy-done((f32[2,8,8,2048]{3,2,1,0:T(8,128)}, f32[2,8,8,2048]{3,2,1,0:T(8,128)S(1)}, u32[]{:S(2)}) %copy-start.3) | copy-done | bytes 1048600
  26.6 16.5 %shard_map.50 = f32[32,144,128]{2,1,0:T(8,128)} custom-call(f32[8,32,2048]{2,1,0:T(8,128)} %ph_ref.1, s32[8,32,2048]{2,1,0:T(8,128)} %wt_ref.1, f32[2,8,8,2048]{3,2,1,0:T(8,128)} %copy-done.2, f32[2,8,8,2048]{3,2,1,0:T(8,128)} %copy-done.3), custom_call_target="tpu_custom_call" | custom-call | flops 94371840 | bytes 8388608 | tf_op jit(solution)/shard_map/pallas_call | solution.py:100
  43.1 8.2 %all-to-all-start = ((f32[32,144,128]{2,1,0:T(8,128)}), f32[32,144,128]{2,1,0:T(8,128)S(1)}, u32[]{:S(2)}, u32[]{:S(2)}) async-start(f32[32,144,128]{2,1,0:T(8,128)} %shard_map.50), calls=%async_computation | async-start | bytes 4718592 | tf_op jit(solution)/shard_map/all_to_all | solution.py:195
  51.3 0.5 fusion.12
  51.9 0.1 copy.5
  52.0 8.7 %cholesky.16 = f32[95,95]{1,0:T(8,128)S(1)} custom-call(f32[95,95]{1,0:T(8,128)S(1)} %fusion.17), custom_call_target="Cholesky" | custom-call | tf_op jit(solution)/shard_map/jit(cholesky)/cholesky | solution.py:179
  60.7 0.6 compare_reduce_fusion
  61.3 0.7 fusion.13
  62.0 7.3 %custom-call.10 = f32[1,95,95]{1,2,0:T(8,128)S(1)} custom-call(f32[1,95,95]{2,1,0:T(8,128)S(1)} %fusion.13), custom_call_target="InvertDiagBlocksLowerTriangular" | custom-call | tf_op jit(solution)/shard_map/jit(_cho_solve)/triangular_solve | solution.py:180
  69.3 0.4 fusion.11
  69.7 0.2 fusion.14
  69.9 0.6 pad.8.pseudo_ref
  70.6 0.1 convert_subtract_fusion
  70.7 0.7 pad.9.design_ref
  71.4 1.4 %copy-done.1 = f32[32,144,128]{2,1,0:T(8,128)} copy-done((f32[32,144,128]{2,1,0:T(8,128)}, f32[32,144,128]{2,1,0:T(8,128)S(1)}, u32[]{:S(2)}) %copy-start.1) | copy-done | bytes 2359320
  72.8 6.4 %shard_map.51 = (f32[2048,96]{1,0:T(8,128)}, f32[2304,256]{1,0:T(8,128)}) custom-call(f32[4608,128]{1,0:T(8,128)} %bitcast.32, f32[96,256]{1,0:T(8,128)} %pad.8.pseudo_ref, f32[256,96]{1,0:T(8,128)} %pad.9.design_ref), custom_call_target="tpu_custom_call" | custom-call | flops 1358954496 | bytes 5603328 | tf_op jit(solution)/shard_map/pallas_call | solution.py:144
  79.2 1.1 %fusion.20 = (f32[256,36,2]{0,2,1:T(2,128)S(1)}, f32[256,36,2]{0,2,1:T(2,128)S(1)}) fusion(f32[256,36,64]{0,2,1:T(8,128)} %bitcast.30), kind=kLoop, calls=%fused_computation.43 | loop fusion | bytes 294912 | tf_op jit(solution)/shard_map/slice | solution.py:26
  80.3 3.1 %collective-permute-start.2 = (f32[256,36,2]{0,2,1:T(2,128)S(1)}, f32[256,36,2]{0,2,1:T(2,128)S(1)}, u32[]{:S(2)}, u32[]{:S(2)}) collective-permute-start(f32[256,36,2]{0,2,1:T(2,128)S(1)} %get-tuple-element.6), channel_id=1, source_target_pairs={{0,4},{4,8},{8,12},{12,16},{16,20},{20,24},{24,28},{28,32},{32,36}... | collective-permute-start | bytes 221192 | tf_op jit(solution)/shard_map/ppermute | solution.py:25
  83.4 5.2 %collective-permute-start.3 = (f32[256,36,2]{0,2,1:T(2,128)S(1)}, f32[256,36,2]{0,2,1:T(2,128)S(1)}, u32[]{:S(2)}, u32[]{:S(2)}) collective-permute-start(f32[256,36,2]{0,2,1:T(2,128)S(1)} %get-tuple-element.7), channel_id=1, source_target_pairs={{4,0},{8,4},{12,8},{16,12},{20,16},{24,20},{28,24},{32,28},{36,32}... | collective-permute-start | bytes 221192 | tf_op jit(solution)/shard_map/ppermute | solution.py:28
  88.6 1.4 %collective-permute-done.3 = f32[256,36,2]{0,2,1:T(2,128)S(1)} collective-permute-done((f32[256,36,2]{0,2,1:T(2,128)S(1)}, f32[256,36,2]{0,2,1:T(2,128)S(1)}, u32[]{:S(2)}, u32[]{:S(2)}) %collective-permute-start.3) | collective-permute-done | bytes 73760 | tf_op jit(solution)/shard_map/ppermute | solution.py:28
  90.0 1.9 %pad_maximum_fusion = f32[256,36,68]{0,2,1:T(8,128)S(1)} fusion(f32[256,36,2]{0,2,1:T(2,128)S(1)} %collective-permute-done.3, f32[256,36,64]{0,2,1:T(8,128)} %bitcast.31, f32[256,36,2]{0,2,1:T(2,128)S(1)} %collective-permute-done.2), kind=kLoop, calls=%fused_computation | loop fusion | flops 1253376 | bytes 5013504 | tf_op jit(solution)/shard_map/concatenate | solution.py:29
  91.9 0.5 fusion
  92.5 2.1 %fusion.5 = bf16[256,32,64]{0,2,1:T(8,128)(2,1)} fusion(f32[256,32,68]{0,2,1:T(8,128)S(1)} %fusion), kind=kLoop, calls=%fused_computation.11 | loop fusion | flops 4718592 | bytes 11534336 | tf_op jit(solution)/shard_map/convert_element_type | solution.py:206
  (12 shorter events, 0.1 us)
Async XLA Ops:
  0.6 1.9 %copy-start = (s32[8,32,2048]{2,1,0:T(8,128)S(1)}, s32[8,32,2048]{2,1,0:T(8,128)}, u32[]{:S(2)}) copy-start(s32[8,32,2048]{2,1,0:T(8,128)} %wt_ref.1) | copy-start | bytes 6291460
  2.7 16.9 %collective-permute-start = (f32[2,8,8,2048]{3,2,1,0:T(8,128)S(1)}, f32[2,8,8,2048]{3,2,1,0:T(8,128)S(1)}, u32[]{:S(2)}, u32[]{:S(2)}) collective-permute-start(f32[2,8,8,2048]{3,2,1,0:T(8,128)S(1)} %pad_maximum_fusion.1), channel_id=1, source_target_pairs={{0,1},{1,2},{2,3},{4,5},{5,6},{6,7},{8,9},{9,10},{10,11},{12,13},{... | collective-permute-start | bytes 3145736 | tf_op jit(solution)/shard_map/ppermute | solution.py:192
  8.0 17.6 %collective-permute-start.1 = (f32[2,8,8,2048]{3,2,1,0:T(8,128)S(1)}, f32[2,8,8,2048]{3,2,1,0:T(8,128)S(1)}, u32[]{:S(2)}, u32[]{:S(2)}) collective-permute-start(f32[2,8,8,2048]{3,2,1,0:T(8,128)S(1)} %pad_maximum_fusion.2), channel_id=1, source_target_pairs={{1,0},{2,1},{3,2},{5,4},{6,5},{7,6},{9,8},{10,9},{11,10},{13,12},{... | collective-permute-start | bytes 3145736 | tf_op jit(solution)/shard_map/ppermute | solution.py:193
  19.7 6.0 %copy-start.2 = (f32[2,8,8,2048]{3,2,1,0:T(8,128)}, f32[2,8,8,2048]{3,2,1,0:T(8,128)S(1)}, u32[]{:S(2)}) copy-start(f32[2,8,8,2048]{3,2,1,0:T(8,128)S(1)} %collective-permute-done.top_ref) | copy-start | bytes 3145732
  25.7 1.0 %copy-start.3 = (f32[2,8,8,2048]{3,2,1,0:T(8,128)}, f32[2,8,8,2048]{3,2,1,0:T(8,128)S(1)}, u32[]{:S(2)}) copy-start(f32[2,8,8,2048]{3,2,1,0:T(8,128)S(1)} %collective-permute-done.1.bot_ref) | copy-start | bytes 3145732
  43.1 8.2 %copy-start.4 = (s32[256,2]{0,1:T(2,128)S(1)}, s32[256,2]{0,1:T(2,128)}, u32[]{:S(2)}) copy-start(s32[256,2]{0,1:T(2,128)} %param.5) | copy-start | bytes 6148
  43.1 28.3 %all-to-all-start = ((f32[32,144,128]{2,1,0:T(8,128)}), f32[32,144,128]{2,1,0:T(8,128)S(1)}, u32[]{:S(2)}, u32[]{:S(2)}) async-start(f32[32,144,128]{2,1,0:T(8,128)} %shard_map.50), calls=%async_computation | async-start | bytes 4718592 | tf_op jit(solution)/shard_map/all_to_all | solution.py:195
  71.4 1.4 %copy-start.1 = (f32[32,144,128]{2,1,0:T(8,128)}, f32[32,144,128]{2,1,0:T(8,128)S(1)}, u32[]{:S(2)}) copy-start(f32[32,144,128]{2,1,0:T(8,128)S(1)} %all-to-all-done) | copy-start | bytes 7077892
  80.3 8.3 %collective-permute-start.2 = (f32[256,36,2]{0,2,1:T(2,128)S(1)}, f32[256,36,2]{0,2,1:T(2,128)S(1)}, u32[]{:S(2)}, u32[]{:S(2)}) collective-permute-start(f32[256,36,2]{0,2,1:T(2,128)S(1)} %get-tuple-element.6), channel_id=1, source_target_pairs={{0,4},{4,8},{8,12},{12,16},{16,20},{20,24},{24,28},{28,32},{32,36}... | collective-permute-start | bytes 221192 | tf_op jit(solution)/shard_map/ppermute | solution.py:25
  83.4 6.6 %collective-permute-start.3 = (f32[256,36,2]{0,2,1:T(2,128)S(1)}, f32[256,36,2]{0,2,1:T(2,128)S(1)}, u32[]{:S(2)}, u32[]{:S(2)}) collective-permute-start(f32[256,36,2]{0,2,1:T(2,128)S(1)} %get-tuple-element.7), channel_id=1, source_target_pairs={{4,0},{8,4},{12,8},{16,12},{20,16},{24,20},{28,24},{32,28},{36,32}... | collective-permute-start | bytes 221192 | tf_op jit(solution)/shard_map/ppermute | solution.py:28

commit v11 on v10

--- a/solution.py
+++ b/solution.py
@@ -11,6 +11,7 @@
 DATES = 96
 SWEEPS = 4
 FILTER_HALO = 2
+SENT = SWEEPS + FILTER_HALO
 HALO = 8
 PI32 = float(np.float32(np.pi))
 TWO_PI_HI = float(np.float32(2 * np.pi))
@@ -38,12 +39,17 @@
 
 def unwrap_kernel(rows_out, ph_ref, wt_ref, top_ref, bot_ref, o_ref, p_ref, q_ref, cur_ref):
     for b in range(ph_ref.shape[0]):
-        p_ref[pl.ds(0, HALO), :] = top_ref[0, b]
+        spare = HALO - SENT
+        blank = jnp.zeros((spare, p_ref.shape[1]), jnp.float32)
+        for ref in (p_ref, q_ref):
+            ref[pl.ds(0, spare), :] = blank
+            ref[pl.ds(HALO + rows_out + SENT, spare), :] = blank
+        p_ref[pl.ds(spare, SENT), :] = top_ref[0, b]
         p_ref[pl.ds(HALO, rows_out), :] = ph_ref[b]
-        p_ref[pl.ds(HALO + rows_out, HALO), :] = bot_ref[0, b]
-        q_ref[pl.ds(0, HALO), :] = top_ref[1, b]
+        p_ref[pl.ds(HALO + rows_out, SENT), :] = bot_ref[0, b]
+        q_ref[pl.ds(spare, SENT), :] = top_ref[1, b]
         q_ref[pl.ds(HALO, rows_out), :] = wt_ref[b].astype(jnp.float32)
-        q_ref[pl.ds(HALO + rows_out, HALO), :] = bot_ref[1, b]
+        q_ref[pl.ds(HALO + rows_out, SENT), :] = bot_ref[1, b]
         p = p_ref[...]
         q = q_ref[...]
         nr, nc = p.shape
@@ -96,7 +102,7 @@
     nr = rows_out + 2 * HALO
     per = 4
     half = rows_out // 2 + FILTER_HALO
-    halo_spec = pl.BlockSpec((2, per, HALO, nc), lambda i: (0, i, 0, 0))
+    halo_spec = pl.BlockSpec((2, per, SENT, nc), lambda i: (0, i, 0, 0))
     return pl.pallas_call(
         functools.partial(unwrap_kernel, rows_out),
         grid=(n // per,),
@@ -187,8 +193,8 @@
     count = lax.axis_size("rows")
     forward = [(i, i + 1) for i in range(count - 1)]
     backward = [(target, source) for source, target in forward]
-    edge_low = jnp.stack([phase[:, rows - HALO :], weights[:, rows - HALO :].astype(jnp.float32)])
-    edge_high = jnp.stack([phase[:, :HALO], weights[:, :HALO].astype(jnp.float32)])
+    edge_low = jnp.stack([phase[:, rows - SENT :], weights[:, rows - SENT :].astype(jnp.float32)])
+    edge_high = jnp.stack([phase[:, :SENT], weights[:, :SENT].astype(jnp.float32)])
     top = lax.ppermute(edge_low, "rows", forward)
     bottom = lax.ppermute(edge_high, "rows", backward)
     current = unwrap(phase, weights, top, bottom)

time: 95.2 us -> 96.4 us (1.013)
  local copies, waits for them, and re-layouts: 6.8 us -> 9.03 us
  waiting for transfers between devices: 17.1 us -> 14.9 us
    ppermute x1, waiting for transfers between devices: 9.69 us -> 6.44 us  [on_device(): top = lax.ppermute(edge_low, 'rows', forward)]
    ppermute x0 -> x2, local copies, waits for them, and re-layouts: none -> 2.89 us  [the longest x1 1.44 us: on_device(): bottom = lax.ppermute(edge_high, 'rows', backward)]
    all_to_all x1, waiting for transfers between devices: 0.01 us -> 2.04 us  [on_device(): lax.all_to_all(current, 'ifg', split_axis=0, concat_axis=0, tiled=True)]
    slice x0 -> x2, local copies, waits for them, and re-layouts: none -> 1.52 us  [the longest x1 1.44 us: on_device(): phase[:, :SENT]]
    another operation x1 -> x0, local copies, waits for them, and re-layouts: 1.44 us -> none  [on_device(): jnp.stack([phase[:, :HALO], weights[:, :HALO].astype(jnp.float32)])]
    ppermute x1, starting transfers between devices: 5.19 us -> 6.32 us  [extended_2(): lax.ppermute(lax.slice_in_dim(block, 0, width, axis=dim), axis, backward)]
    ppermute x1, starting transfers between devices: 3.1 us -> 1.97 us  [extended_2(): lax.ppermute(lax.slice_in_dim(block, block.shape[dim] - width, None, axis...]
    ppermute x1, waiting for transfers between devices: 6 us -> 5 us  [on_device(): bottom = lax.ppermute(edge_high, 'rows', backward)]
  transfers between devices with their start and end apart: 5 -> 5, of which waited for: 3 -> 4; matrix products, arithmetic and copies ran while one was open for 21% -> 23% of each run, Pallas kernels for 0% -> 0%
where the time goes in v11:
time: 96.4 us; the launch traced here: 95.5 us
  starting transfers between devices  23.6 us (24%)
  Pallas kernels  23.5 us (24%)
  other arithmetic  22.6 us (23%)
  waiting for transfers between devices  14.9 us (15%)
  local copies, waits for them, and re-layouts  9.03 us (9%)
  matrix products  1.15 us (1%)
    pallas_call x1, Pallas kernels, unwrap(): pl.pallas_call(functools.partial(unwrap_kernel, rows_out), grid=(n // per...  17 us
    another operation x3, other arithmetic, network_maps(): factor = jnp.linalg.cholesky(normal_matrix)  9.36 us
    all_to_all x1, starting transfers between devices, on_device(): lax.all_to_all(current, 'ifg', split_axis=0, concat_axis=0, tiled=True)  8.16 us
    another operation x2, other arithmetic, network_maps(): pseudo = jax.scipy.linalg.cho_solve((factor, True), design.T)  7.94 us
    pallas_call x1, Pallas kernels, invert(): pl.pallas_call(functools.partial(invert_kernel, rows), in_specs=[whole, w...  6.46 us
    ppermute x1, waiting for transfers between devices, on_device(): top = lax.ppermute(edge_low, 'rows', forward)  6.44 us
    ppermute x1, starting transfers between devices, extended_2(): lax.ppermute(lax.slice_in_dim(block, 0, width, axis=dim), axis, backward)  6.32 us
    ppermute x1, starting transfers between devices, on_device(): top = lax.ppermute(edge_low, 'rows', forward)  5.21 us
  transfers between devices with their start and end apart: 5, of which 4 were waited for; matrix products, arithmetic and copies ran while one was open for 23% of the time, Pallas kernels for 0%

profile of v11, /device:TPU:9, one launch (start us, length us, event | category | flops | bytes accessed | tf_op | source)
XLA Modules:
  0.0 95.5 jit_solution(938501660534472569)
XLA Ops:
  0.6 1.4 %fusion.23 = (f32[8,6,2048]{2,1,0:T(8,128)S(1)}, f32[8,6,2048]{2,1,0:T(8,128)S(1)}) fusion(f32[8,32,2048]{2,1,0:T(8,128)} %ph_ref.1), kind=kLoop, calls=%fused_computation.46 | loop fusion | bytes 1572864 | tf_op jit(solution)/shard_map/slice | solution.py:197
  2.1 0.2 copy.26
  2.6 0.2 fusion.10
  2.9 5.2 %collective-permute-start = (f32[2,8,6,2048]{3,1,2,0:T(8,128)S(1)}, f32[2,8,6,2048]{3,1,2,0:T(8,128)S(1)}, u32[]{:S(2)}, u32[]{:S(2)}) collective-permute-start(f32[2,8,6,2048]{3,1,2,0:T(8,128)S(1)} %pad_maximum_fusion.1), channel_id=1, source_target_pairs={{0,1},{1,2},{2,3},{4,5},{5,6},{6,7},{8,9},{9,10},{10,11},{12,13},{... | collective-permute-start | bytes 2359304 | tf_op jit(solution)/shard_map/ppermute | solution.py:198
  8.2 0.2 copy.25
  8.4 0.2 fusion.9
  8.7 1.9 %collective-permute-start.1 = (f32[2,8,6,2048]{3,1,2,0:T(8,128)S(1)}, f32[2,8,6,2048]{3,1,2,0:T(8,128)S(1)}, u32[]{:S(2)}, u32[]{:S(2)}) collective-permute-start(f32[2,8,6,2048]{3,1,2,0:T(8,128)S(1)} %pad_maximum_fusion.2), channel_id=1, source_target_pairs={{1,0},{2,1},{3,2},{5,4},{6,5},{7,6},{9,8},{10,9},{11,10},{13,12},{... | collective-permute-start | bytes 2359304 | tf_op jit(solution)/shard_map/ppermute | solution.py:199
  10.6 6.4 %collective-permute-done = f32[2,8,6,2048]{3,1,2,0:T(8,128)S(1)} collective-permute-done((f32[2,8,6,2048]{3,1,2,0:T(8,128)S(1)}, f32[2,8,6,2048]{3,1,2,0:T(8,128)S(1)}, u32[]{:S(2)}, u32[]{:S(2)}) %collective-permute-start) | collective-permute-done | bytes 786464 | tf_op jit(solution)/shard_map/ppermute | solution.py:198
  17.1 1.4 %copy.10.top_ref = f32[2,8,6,2048]{3,2,1,0:T(8,128)} copy(f32[2,8,6,2048]{3,1,2,0:T(8,128)S(1)} %collective-permute-done) | data formatting | bytes 1572864 | tf_op jit(solution)/shard_map/ppermute | solution.py:198
  18.5 5.0 %collective-permute-done.1 = f32[2,8,6,2048]{3,1,2,0:T(8,128)S(1)} collective-permute-done((f32[2,8,6,2048]{3,1,2,0:T(8,128)S(1)}, f32[2,8,6,2048]{3,1,2,0:T(8,128)S(1)}, u32[]{:S(2)}, u32[]{:S(2)}) %collective-permute-start.1) | collective-permute-done | bytes 786464 | tf_op jit(solution)/shard_map/ppermute | solution.py:199
  23.5 1.4 %copy.11.bot_ref = f32[2,8,6,2048]{3,2,1,0:T(8,128)} copy(f32[2,8,6,2048]{3,1,2,0:T(8,128)S(1)} %collective-permute-done.1) | data formatting | bytes 1572864 | tf_op jit(solution)/shard_map/ppermute | solution.py:199
  25.0 17.0 %shard_map.50 = f32[32,144,128]{2,1,0:T(8,128)} custom-call(f32[8,32,2048]{2,1,0:T(8,128)} %ph_ref.1, s32[8,32,2048]{2,1,0:T(8,128)} %wt_ref.1, f32[2,8,6,2048]{3,2,1,0:T(8,128)} %copy.10.top_ref, f32[2,8,6,2048]{3,2,1,0:T(8,128)} %copy.11.bot_ref), custom_call_target="tpu_custom_call" | custom-call | flops 94371840 | bytes 8388608 | tf_op jit(solution)/shard_map/pallas_call | solution.py:106
  42.0 8.2 %all-to-all-start = ((f32[32,144,128]{2,1,0:T(8,128)}), f32[32,144,128]{2,1,0:T(8,128)S(1)}, u32[]{:S(2)}, u32[]{:S(2)}) async-start(f32[32,144,128]{2,1,0:T(8,128)} %shard_map.50), calls=%async_computation | async-start | bytes 4718592 | tf_op jit(solution)/shard_map/all_to_all | solution.py:201
  50.2 0.5 fusion.14
  50.8 8.7 %cholesky.16 = f32[95,95]{1,0:T(8,128)S(1)} custom-call(f32[95,95]{1,0:T(8,128)S(1)} %fusion.19), custom_call_target="Cholesky" | custom-call | tf_op jit(solution)/shard_map/jit(cholesky)/cholesky | solution.py:185
  59.6 0.6 compare_reduce_fusion
  60.2 0.7 fusion.15
  60.9 7.3 %custom-call.10 = f32[1,95,95]{1,2,0:T(8,128)S(1)} custom-call(f32[1,95,95]{2,1,0:T(8,128)S(1)} %fusion.15), custom_call_target="InvertDiagBlocksLowerTriangular" | custom-call | tf_op jit(solution)/shard_map/jit(_cho_solve)/triangular_solve | solution.py:186
  68.2 0.4 fusion.13
  68.5 0.2 fusion.16
  68.8 0.6 pad.8.pseudo_ref
  69.6 0.7 pad.9.design_ref
  70.2 2.0 %all-to-all-done = f32[32,144,128]{2,1,0:T(8,128)S(1)} async-done(((f32[32,144,128]{2,1,0:T(8,128)}), f32[32,144,128]{2,1,0:T(8,128)S(1)}, u32[]{:S(2)}, u32[]{:S(2)}) %all-to-all-start) | async-done | bytes 2359328 | tf_op jit(solution)/shard_map/all_to_all | solution.py:201
  72.3 1.4 %copy-done.1 = f32[32,144,128]{2,1,0:T(8,128)} copy-done((f32[32,144,128]{2,1,0:T(8,128)}, f32[32,144,128]{2,1,0:T(8,128)S(1)}, u32[]{:S(2)}) %copy-start.1) | copy-done | bytes 2359320
  73.7 6.5 %shard_map.51 = (f32[2048,96]{1,0:T(8,128)}, f32[2304,256]{1,0:T(8,128)}) custom-call(f32[4608,128]{1,0:T(8,128)} %bitcast.34, f32[96,256]{1,0:T(8,128)} %pad.8.pseudo_ref, f32[256,96]{1,0:T(8,128)} %pad.9.design_ref), custom_call_target="tpu_custom_call" | custom-call | flops 1358954496 | bytes 5603328 | tf_op jit(solution)/shard_map/pallas_call | solution.py:150
  80.1 1.1 %fusion.22 = (f32[256,36,2]{0,2,1:T(2,128)S(1)}, f32[256,36,2]{0,2,1:T(2,128)S(1)}) fusion(f32[256,36,64]{0,2,1:T(8,128)} %bitcast.32), kind=kLoop, calls=%fused_computation.45 | loop fusion | bytes 294912 | tf_op jit(solution)/shard_map/slice | solution.py:27
  81.3 2.0 %collective-permute-start.2 = (f32[256,36,2]{0,2,1:T(2,128)S(1)}, f32[256,36,2]{0,2,1:T(2,128)S(1)}, u32[]{:S(2)}, u32[]{:S(2)}) collective-permute-start(f32[256,36,2]{0,2,1:T(2,128)S(1)} %get-tuple-element.6), channel_id=1, source_target_pairs={{0,4},{4,8},{8,12},{12,16},{16,20},{20,24},{24,28},{28,32},{32,36}... | collective-permute-start | bytes 221192 | tf_op jit(solution)/shard_map/ppermute | solution.py:26
  83.2 6.3 %collective-permute-start.3 = (f32[256,36,2]{0,2,1:T(2,128)S(1)}, f32[256,36,2]{0,2,1:T(2,128)S(1)}, u32[]{:S(2)}, u32[]{:S(2)}) collective-permute-start(f32[256,36,2]{0,2,1:T(2,128)S(1)} %get-tuple-element.7), channel_id=1, source_target_pairs={{4,0},{8,4},{12,8},{16,12},{20,16},{24,20},{28,24},{32,28},{36,32}... | collective-permute-start | bytes 221192 | tf_op jit(solution)/shard_map/ppermute | solution.py:29
  89.6 1.4 %collective-permute-done.3 = f32[256,36,2]{0,2,1:T(2,128)S(1)} collective-permute-done((f32[256,36,2]{0,2,1:T(2,128)S(1)}, f32[256,36,2]{0,2,1:T(2,128)S(1)}, u32[]{:S(2)}, u32[]{:S(2)}) %collective-permute-start.3) | collective-permute-done | bytes 73760 | tf_op jit(solution)/shard_map/ppermute | solution.py:29
  90.9 1.9 %pad_maximum_fusion = f32[256,36,68]{0,2,1:T(8,128)S(1)} fusion(f32[256,36,2]{0,2,1:T(2,128)S(1)} %collective-permute-done.3, f32[256,36,64]{0,2,1:T(8,128)} %bitcast.33, f32[256,36,2]{0,2,1:T(2,128)S(1)} %collective-permute-done.2), kind=kLoop, calls=%fused_computation | loop fusion | flops 1253376 | bytes 5013504 | tf_op jit(solution)/shard_map/concatenate | solution.py:30
  92.9 0.5 fusion
  93.4 2.1 %fusion.5 = bf16[256,32,64]{0,2,1:T(8,128)(2,1)} fusion(f32[256,32,68]{0,2,1:T(8,128)S(1)} %fusion), kind=kLoop, calls=%fused_computation.11 | loop fusion | flops 4718592 | bytes 11534336 | tf_op jit(solution)/shard_map/convert_element_type | solution.py:212
  (14 shorter events, 0.7 us)
Async XLA Ops:
  0.6 1.9 %copy-start = (s32[8,32,2048]{2,1,0:T(8,128)S(1)}, s32[8,32,2048]{2,1,0:T(8,128)}, u32[]{:S(2)}) copy-start(s32[8,32,2048]{2,1,0:T(8,128)} %wt_ref.1) | copy-start | bytes 6291460
  2.9 14.1 %collective-permute-start = (f32[2,8,6,2048]{3,1,2,0:T(8,128)S(1)}, f32[2,8,6,2048]{3,1,2,0:T(8,128)S(1)}, u32[]{:S(2)}, u32[]{:S(2)}) collective-permute-start(f32[2,8,6,2048]{3,1,2,0:T(8,128)S(1)} %pad_maximum_fusion.1), channel_id=1, source_target_pairs={{0,1},{1,2},{2,3},{4,5},{5,6},{6,7},{8,9},{9,10},{10,11},{12,13},{... | collective-permute-start | bytes 2359304 | tf_op jit(solution)/shard_map/ppermute | solution.py:198
  8.7 14.8 %collective-permute-start.1 = (f32[2,8,6,2048]{3,1,2,0:T(8,128)S(1)}, f32[2,8,6,2048]{3,1,2,0:T(8,128)S(1)}, u32[]{:S(2)}, u32[]{:S(2)}) collective-permute-start(f32[2,8,6,2048]{3,1,2,0:T(8,128)S(1)} %pad_maximum_fusion.2), channel_id=1, source_target_pairs={{1,0},{2,1},{3,2},{5,4},{6,5},{7,6},{9,8},{10,9},{11,10},{13,12},{... | collective-permute-start | bytes 2359304 | tf_op jit(solution)/shard_map/ppermute | solution.py:199
  42.0 8.2 %copy-start.2 = (s32[256,2]{0,1:T(2,128)S(1)}, s32[256,2]{0,1:T(2,128)}, u32[]{:S(2)}) copy-start(s32[256,2]{0,1:T(2,128)} %param.5) | copy-start | bytes 6148
  42.0 30.3 %all-to-all-start = ((f32[32,144,128]{2,1,0:T(8,128)}), f32[32,144,128]{2,1,0:T(8,128)S(1)}, u32[]{:S(2)}, u32[]{:S(2)}) async-start(f32[32,144,128]{2,1,0:T(8,128)} %shard_map.50), calls=%async_computation | async-start | bytes 4718592 | tf_op jit(solution)/shard_map/all_to_all | solution.py:201
  72.3 1.4 %copy-start.1 = (f32[32,144,128]{2,1,0:T(8,128)}, f32[32,144,128]{2,1,0:T(8,128)S(1)}, u32[]{:S(2)}) copy-start(f32[32,144,128]{2,1,0:T(8,128)S(1)} %all-to-all-done) | copy-start | bytes 7077892
  81.3 8.3 %collective-permute-start.2 = (f32[256,36,2]{0,2,1:T(2,128)S(1)}, f32[256,36,2]{0,2,1:T(2,128)S(1)}, u32[]{:S(2)}, u32[]{:S(2)}) collective-permute-start(f32[256,36,2]{0,2,1:T(2,128)S(1)} %get-tuple-element.6), channel_id=1, source_target_pairs={{0,4},{4,8},{8,12},{12,16},{16,20},{20,24},{24,28},{28,32},{32,36}... | collective-permute-start | bytes 221192 | tf_op jit(solution)/shard_map/ppermute | solution.py:26
  83.2 7.7 %collective-permute-start.3 = (f32[256,36,2]{0,2,1:T(2,128)S(1)}, f32[256,36,2]{0,2,1:T(2,128)S(1)}, u32[]{:S(2)}, u32[]{:S(2)}) collective-permute-start(f32[256,36,2]{0,2,1:T(2,128)S(1)} %get-tuple-element.7), channel_id=1, source_target_pairs={{4,0},{8,4},{12,8},{16,12},{20,16},{24,20},{28,24},{32,28},{36,32}... | collective-permute-start | bytes 221192 | tf_op jit(solution)/shard_map/ppermute | solution.py:29

commit v12 on v11

--- a/solution.py
+++ b/solution.py
@@ -97,28 +97,41 @@
             o_ref[2 * m + 1, pl.ds(b * half, half), :] = odd[:, 128 * m : 128 * (m + 1)]
 
 
-def unwrap(phase, weights, top, bottom):
+def unwrap(phase, weights, top, bottom, part, earlier=None):
     n, rows_out, nc = phase.shape
     nr = rows_out + 2 * HALO
-    per = 4
+    per = top.shape[1]
     half = rows_out // 2 + FILTER_HALO
-    halo_spec = pl.BlockSpec((2, per, SENT, nc), lambda i: (0, i, 0, 0))
+    halo_spec = pl.BlockSpec((2, per, SENT, nc), lambda i: (0, 0, 0, 0))
+    in_specs = [
+        pl.BlockSpec((per, rows_out, nc), lambda i: (part, 0, 0)),
+        pl.BlockSpec((per, rows_out, nc), lambda i: (part, 0, 0)),
+        halo_spec,
+        halo_spec,
+    ]
+    operands = [phase, weights, top, bottom]
+    aliases = {}
+    kernel = functools.partial(unwrap_kernel, rows_out)
+    if earlier is not None:
+        in_specs.append(pl.BlockSpec(memory_space=pl.ANY))
+        operands.append(earlier)
+        aliases = {4: 0}
+
+        def kernel(ph_ref, wt_ref, top_ref, bot_ref, earlier_ref, o_ref, p_ref, q_ref, cur_ref):
+            unwrap_kernel(rows_out, ph_ref, wt_ref, top_ref, bot_ref, o_ref, p_ref, q_ref, cur_ref)
+
     return pl.pallas_call(
-        functools.partial(unwrap_kernel, rows_out),
-        grid=(n // per,),
-        in_specs=[
-            pl.BlockSpec((per, rows_out, nc), lambda i: (i, 0, 0)),
-            pl.BlockSpec((per, rows_out, nc), lambda i: (i, 0, 0)),
-            halo_spec,
-            halo_spec,
-        ],
-        out_specs=pl.BlockSpec((nc // 64, per * half, 128), lambda i: (0, i, 0)),
+        kernel,
+        grid=(1,),
+        in_specs=in_specs,
+        out_specs=pl.BlockSpec((nc // 64, per * half, 128), lambda i: (0, part, 0)),
         out_shape=jax.ShapeDtypeStruct((nc // 64, n * half, 128), jnp.float32),
         scratch_shapes=[pltpu.VMEM((nr, nc), jnp.float32)] * 3,
+        input_output_aliases=aliases,
         cost_estimate=pl.CostEstimate(
-            flops=120 * n * nr * nc, bytes_accessed=4 * n * nc * (2 * nr + rows_out), transcendentals=0
+            flops=120 * per * nr * nc, bytes_accessed=4 * per * nc * (2 * nr + rows_out), transcendentals=0
         ),
-    )(phase, weights, top, bottom)
+    )(*operands)
 
 
 def invert_kernel(rows, x_ref, pseudo_ref, design_ref, s_ref, r_ref):
@@ -195,9 +208,12 @@
     backward = [(target, source) for source, target in forward]
     edge_low = jnp.stack([phase[:, rows - SENT :], weights[:, rows - SENT :].astype(jnp.float32)])
     edge_high = jnp.stack([phase[:, :SENT], weights[:, :SENT].astype(jnp.float32)])
-    top = lax.ppermute(edge_low, "rows", forward)
-    bottom = lax.ppermute(edge_high, "rows", backward)
-    current = unwrap(phase, weights, top, bottom)
+    per = phase.shape[0] // 2
+    current = None
+    for part in range(2):
+        top = lax.ppermute(edge_low[:, part * per : (part + 1) * per], "rows", forward)
+        bottom = lax.ppermute(edge_high[:, part * per : (part + 1) * per], "rows", backward)
+        current = unwrap(phase, weights, top, bottom, part, current)
     received = lax.all_to_all(current, "ifg", split_axis=0, concat_axis=0, tiled=True)
     half = rows // 2 + FILTER_HALO
     series_t, residual_t = invert(received.reshape(-1, 128), pseudo, design, half)

time: 96.4 us -> 104 us (1.079)
  the two profiles are of different devices: /device:TPU:9 before, /device:TPU:102 now
where the time goes in v12:
time: 104 us; the launch traced here: 103 us
  starting transfers between devices  29.2 us (28%)
  Pallas kernels  26.5 us (25%)
  other arithmetic  22.3 us (21%)
  waiting for transfers between devices  14.2 us (14%)
  local copies, waits for them, and re-layouts  9.02 us (9%)
  matrix products  1.15 us (1%)
    pallas_call x2, Pallas kernels, unwrap(): pl.pallas_call(kernel, grid=(1,), in_specs=in_specs, out_specs=pl.BlockSp...  20.1 us
    ppermute x2, starting transfers between devices, on_device(): lax.ppermute(edge_high[:, part * per:(part + 1) * per], 'rows', backward)  10.3 us
    another operation x3, other arithmetic, network_maps(): factor = jnp.linalg.cholesky(normal_matrix)  9.36 us
    all_to_all x1, starting transfers between devices, on_device(): lax.all_to_all(current, 'ifg', split_axis=0, concat_axis=0, tiled=True)  8.33 us
    another operation x2, other arithmetic, network_maps(): pseudo = jax.scipy.linalg.cho_solve((factor, True), design.T)  7.94 us
    ppermute x1, waiting for transfers between devices, extended_2(): lax.ppermute(lax.slice_in_dim(block, 0, width, axis=dim), axis, backward)  7.29 us
    all_to_all x1, waiting for transfers between devices, on_device(): lax.all_to_all(current, 'ifg', split_axis=0, concat_axis=0, tiled=True)  6.89 us
    pallas_call x1, Pallas kernels, invert(): pl.pallas_call(functools.partial(invert_kernel, rows), in_specs=[whole, w...  6.45 us
  transfers between devices with their start and end apart: 7, of which 2 were waited for; matrix products, arithmetic and copies ran while one was open for 19% of the time, Pallas kernels for 10%

profile of v12, /device:TPU:102, one launch (start us, length us, event | category | flops | bytes accessed | tf_op | source)
XLA Modules:
  0.0 103.3 jit_solution(2761821296809900568)
XLA Ops:
  0.6 1.4 %slice_bitcast_fusion = (f32[1,8,6,2048]{3,2,1,0:T(8,128)S(1)}, f32[1,8,6,2048]{3,2,1,0:T(8,128)S(1)}) fusion(f32[8,32,2048]{2,1,0:T(8,128)} %ph_ref.3), kind=kLoop, calls=%fused_computation.27 | loop fusion | bytes 1572864 | tf_op jit(solution)/shard_map/stack | solution.py:210
  2.1 0.5 copy-done
  2.7 1.9 %collective-permute-start.2 = (f32[2,4,6,2048]{3,2,1,0:T(8,128)S(1)}, f32[2,4,6,2048]{3,2,1,0:T(8,128)S(1)}, u32[]{:S(2)}, u32[]{:S(2)}) collective-permute-start(f32[2,4,6,2048]{3,2,1,0:T(8,128)S(1)} %get-tuple-element.14), channel_id=1, source_target_pairs={{0,1},{1,2},{2,3},{4,5},{5,6},{6,7},{8,9},{9,10},{10,11},{12,13},{... | collective-permute-start | bytes 1179656 | tf_op jit(solution)/shard_map/ppermute | solution.py:214
  4.8 5.1 %collective-permute-start.3 = (f32[2,4,6,2048]{3,2,1,0:T(8,128)S(1)}, f32[2,4,6,2048]{3,2,1,0:T(8,128)S(1)}, u32[]{:S(2)}, u32[]{:S(2)}) collective-permute-start(f32[2,4,6,2048]{3,2,1,0:T(8,128)S(1)} %get-tuple-element.12), channel_id=1, source_target_pairs={{1,0},{2,1},{3,2},{5,4},{6,5},{7,6},{9,8},{10,9},{11,10},{13,12},{... | collective-permute-start | bytes 1179656 | tf_op jit(solution)/shard_map/ppermute | solution.py:215
  9.9 1.9 %collective-permute-start = (f32[2,4,6,2048]{3,2,1,0:T(8,128)S(1)}, f32[2,4,6,2048]{3,2,1,0:T(8,128)S(1)}, u32[]{:S(2)}, u32[]{:S(2)}) collective-permute-start(f32[2,4,6,2048]{3,2,1,0:T(8,128)S(1)} %get-tuple-element.15), channel_id=1, source_target_pairs={{0,1},{1,2},{2,3},{4,5},{5,6},{6,7},{8,9},{9,10},{10,11},{12,13},{... | collective-permute-start | bytes 1179656 | tf_op jit(solution)/shard_map/ppermute | solution.py:214
  11.9 5.1 %collective-permute-start.1 = (f32[2,4,6,2048]{3,2,1,0:T(8,128)S(1)}, f32[2,4,6,2048]{3,2,1,0:T(8,128)S(1)}, u32[]{:S(2)}, u32[]{:S(2)}) collective-permute-start(f32[2,4,6,2048]{3,2,1,0:T(8,128)S(1)} %get-tuple-element.13), channel_id=1, source_target_pairs={{1,0},{2,1},{3,2},{5,4},{6,5},{7,6},{9,8},{10,9},{11,10},{13,12},{... | collective-permute-start | bytes 1179656 | tf_op jit(solution)/shard_map/ppermute | solution.py:215
  17.1 0.8 copy-done.4
  17.8 0.8 copy-done.5
  18.6 9.9 %shard_map.50.earlier_ref = f32[32,144,128]{2,1,0:T(8,128)} custom-call(f32[8,32,2048]{2,1,0:T(8,128)} %ph_ref.3, s32[8,32,2048]{2,1,0:T(8,128)} %wt_ref.3, f32[2,4,6,2048]{3,2,1,0:T(8,128)} %copy-done.4, f32[2,4,6,2048]{3,2,1,0:T(8,128)} %copy-done.5), custom_call_target="tpu_custom_call" | custom-call | flops 47185920 | bytes 4194304 | tf_op jit(solution)/shard_map/pallas_call | solution.py:123
  28.6 0.8 copy-done.2
  29.3 0.8 copy-done.3
  30.1 10.1 %shard_map.51 = f32[32,144,128]{2,1,0:T(8,128)} custom-call(f32[8,32,2048]{2,1,0:T(8,128)} %ph_ref.3, s32[8,32,2048]{2,1,0:T(8,128)} %wt_ref.3, f32[2,4,6,2048]{3,2,1,0:T(8,128)} %copy-done.2, f32[2,4,6,2048]{3,2,1,0:T(8,128)} %copy-done.3, f32[32,144,128]{2,1,0:T(8,128)} %shard_map.50.earlier_ref), custom_call_target="tpu_custom_call", output_to_operand_aliasing={{}: (4, {})} | custom-call | flops 47185920 | bytes 4194304 | tf_op jit(solution)/shard_map/pallas_call | solution.py:123
  40.3 8.3 %all-to-all-start = ((f32[32,144,128]{2,1,0:T(8,128)}), f32[32,144,128]{2,1,0:T(8,128)S(1)}, u32[]{:S(2)}, u32[]{:S(2)}) async-start(f32[32,144,128]{2,1,0:T(8,128)} %shard_map.51), calls=%async_computation | async-start | bytes 4718592 | tf_op jit(solution)/shard_map/all_to_all | solution.py:217
  48.6 0.5 fusion.14
  49.3 8.7 %cholesky.16 = f32[95,95]{1,0:T(8,128)S(1)} custom-call(f32[95,95]{1,0:T(8,128)S(1)} %fusion.19), custom_call_target="Cholesky" | custom-call | tf_op jit(solution)/shard_map/jit(cholesky)/cholesky | solution.py:198
  58.0 0.6 compare_reduce_fusion
  58.7 0.7 fusion.15
  59.3 7.3 %custom-call.10 = f32[1,95,95]{1,2,0:T(8,128)S(1)} custom-call(f32[1,95,95]{2,1,0:T(8,128)S(1)} %fusion.15), custom_call_target="InvertDiagBlocksLowerTriangular" | custom-call | tf_op jit(solution)/shard_map/jit(_cho_solve)/triangular_solve | solution.py:199
  66.6 0.4 fusion.13
  67.0 0.2 fusion.16
  67.2 0.7 pad.8.pseudo_ref
  68.0 0.7 pad.9.design_ref
  68.7 6.9 %all-to-all-done = f32[32,144,128]{2,1,0:T(8,128)S(1)} async-done(((f32[32,144,128]{2,1,0:T(8,128)}), f32[32,144,128]{2,1,0:T(8,128)S(1)}, u32[]{:S(2)}, u32[]{:S(2)}) %all-to-all-start) | async-done | bytes 2359328 | tf_op jit(solution)/shard_map/all_to_all | solution.py:217
  75.6 1.4 %copy-done.1 = f32[32,144,128]{2,1,0:T(8,128)} copy-done((f32[32,144,128]{2,1,0:T(8,128)}, f32[32,144,128]{2,1,0:T(8,128)S(1)}, u32[]{:S(2)}) %copy-start.1) | copy-done | bytes 2359320
  77.0 6.5 %shard_map.52 = (f32[2048,96]{1,0:T(8,128)}, f32[2304,256]{1,0:T(8,128)}) custom-call(f32[4608,128]{1,0:T(8,128)} %bitcast.32, f32[96,256]{1,0:T(8,128)} %pad.8.pseudo_ref, f32[256,96]{1,0:T(8,128)} %pad.9.design_ref), custom_call_target="tpu_custom_call" | custom-call | flops 1358954496 | bytes 5603328 | tf_op jit(solution)/shard_map/pallas_call | solution.py:163
  83.5 1.1 %fusion.22 = (f32[256,36,2]{0,2,1:T(2,128)S(1)}, f32[256,36,2]{0,2,1:T(2,128)S(1)}) fusion(f32[256,36,64]{0,2,1:T(8,128)} %bitcast.30), kind=kLoop, calls=%fused_computation.49 | loop fusion | bytes 294912 | tf_op jit(solution)/shard_map/slice | solution.py:27
  84.6 4.9 %collective-permute-start.4 = (f32[256,36,2]{0,2,1:T(2,128)S(1)}, f32[256,36,2]{0,2,1:T(2,128)S(1)}, u32[]{:S(2)}, u32[]{:S(2)}) collective-permute-start(f32[256,36,2]{0,2,1:T(2,128)S(1)} %get-tuple-element.6), channel_id=1, source_target_pairs={{0,4},{4,8},{8,12},{12,16},{16,20},{20,24},{24,28},{28,32},{32,36}... | collective-permute-start | bytes 221192 | tf_op jit(solution)/shard_map/ppermute | solution.py:26
  89.5 1.9 %collective-permute-start.5 = (f32[256,36,2]{0,2,1:T(2,128)S(1)}, f32[256,36,2]{0,2,1:T(2,128)S(1)}, u32[]{:S(2)}, u32[]{:S(2)}) collective-permute-start(f32[256,36,2]{0,2,1:T(2,128)S(1)} %get-tuple-element.7), channel_id=1, source_target_pairs={{4,0},{8,4},{12,8},{16,12},{20,16},{24,20},{28,24},{32,28},{36,32}... | collective-permute-start | bytes 221192 | tf_op jit(solution)/shard_map/ppermute | solution.py:29
  91.4 7.3 %collective-permute-done.5 = f32[256,36,2]{0,2,1:T(2,128)S(1)} collective-permute-done((f32[256,36,2]{0,2,1:T(2,128)S(1)}, f32[256,36,2]{0,2,1:T(2,128)S(1)}, u32[]{:S(2)}, u32[]{:S(2)}) %collective-permute-start.5) | collective-permute-done | bytes 73760 | tf_op jit(solution)/shard_map/ppermute | solution.py:29
  98.7 1.9 %pad_maximum_fusion = f32[256,36,68]{0,2,1:T(8,128)S(1)} fusion(f32[256,36,2]{0,2,1:T(2,128)S(1)} %collective-permute-done.5, f32[256,36,64]{0,2,1:T(8,128)} %bitcast.31, f32[256,36,2]{0,2,1:T(2,128)S(1)} %collective-permute-done.4), kind=kLoop, calls=%fused_computation | loop fusion | flops 1253376 | bytes 5013504 | tf_op jit(solution)/shard_map/concatenate | solution.py:30
  100.6 0.5 fusion
  101.2 2.1 %fusion.5 = bf16[256,32,64]{0,2,1:T(8,128)(2,1)} fusion(f32[256,32,68]{0,2,1:T(8,128)S(1)} %fusion), kind=kLoop, calls=%fused_computation.11 | loop fusion | flops 4718592 | bytes 11534336 | tf_op jit(solution)/shard_map/convert_element_type | solution.py:228
  (21 shorter events, 0.6 us)
Async XLA Ops:
  0.6 1.9 %copy-start = (s32[8,32,2048]{2,1,0:T(8,128)S(1)}, s32[8,32,2048]{2,1,0:T(8,128)}, u32[]{:S(2)}) copy-start(s32[8,32,2048]{2,1,0:T(8,128)} %wt_ref.3) | copy-start | bytes 6291460
  2.7 14.3 %collective-permute-start.2 = (f32[2,4,6,2048]{3,2,1,0:T(8,128)S(1)}, f32[2,4,6,2048]{3,2,1,0:T(8,128)S(1)}, u32[]{:S(2)}, u32[]{:S(2)}) collective-permute-start(f32[2,4,6,2048]{3,2,1,0:T(8,128)S(1)} %get-tuple-element.14), channel_id=1, source_target_pairs={{0,1},{1,2},{2,3},{4,5},{5,6},{6,7},{8,9},{9,10},{10,11},{12,13},{... | collective-permute-start | bytes 1179656 | tf_op jit(solution)/shard_map/ppermute | solution.py:214
  4.8 12.3 %collective-permute-start.3 = (f32[2,4,6,2048]{3,2,1,0:T(8,128)S(1)}, f32[2,4,6,2048]{3,2,1,0:T(8,128)S(1)}, u32[]{:S(2)}, u32[]{:S(2)}) collective-permute-start(f32[2,4,6,2048]{3,2,1,0:T(8,128)S(1)} %get-tuple-element.12), channel_id=1, source_target_pairs={{1,0},{2,1},{3,2},{5,4},{6,5},{7,6},{9,8},{10,9},{11,10},{13,12},{... | collective-permute-start | bytes 1179656 | tf_op jit(solution)/shard_map/ppermute | solution.py:215
  9.9 18.6 %collective-permute-start = (f32[2,4,6,2048]{3,2,1,0:T(8,128)S(1)}, f32[2,4,6,2048]{3,2,1,0:T(8,128)S(1)}, u32[]{:S(2)}, u32[]{:S(2)}) collective-permute-start(f32[2,4,6,2048]{3,2,1,0:T(8,128)S(1)} %get-tuple-element.15), channel_id=1, source_target_pairs={{0,1},{1,2},{2,3},{4,5},{5,6},{6,7},{8,9},{9,10},{10,11},{12,13},{... | collective-permute-start | bytes 1179656 | tf_op jit(solution)/shard_map/ppermute | solution.py:214
  11.9 16.7 %collective-permute-start.1 = (f32[2,4,6,2048]{3,2,1,0:T(8,128)S(1)}, f32[2,4,6,2048]{3,2,1,0:T(8,128)S(1)}, u32[]{:S(2)}, u32[]{:S(2)}) collective-permute-start(f32[2,4,6,2048]{3,2,1,0:T(8,128)S(1)} %get-tuple-element.13), channel_id=1, source_target_pairs={{1,0},{2,1},{3,2},{5,4},{6,5},{7,6},{9,8},{10,9},{11,10},{13,12},{... | collective-permute-start | bytes 1179656 | tf_op jit(solution)/shard_map/ppermute | solution.py:215
  17.0 0.8 copy-start.4
  17.8 0.8 copy-start.5
  28.5 0.8 copy-start.2
  29.3 0.8 copy-start.3
  40.3 8.3 %copy-start.6 = (s32[256,2]{0,1:T(2,128)S(1)}, s32[256,2]{0,1:T(2,128)}, u32[]{:S(2)}) copy-start(s32[256,2]{0,1:T(2,128)} %param.5) | copy-start | bytes 6148
  40.3 35.3 %all-to-all-start = ((f32[32,144,128]{2,1,0:T(8,128)}), f32[32,144,128]{2,1,0:T(8,128)S(1)}, u32[]{:S(2)}, u32[]{:S(2)}) async-start(f32[32,144,128]{2,1,0:T(8,128)} %shard_map.51), calls=%async_computation | async-start | bytes 4718592 | tf_op jit(solution)/shard_map/all_to_all | solution.py:217
  75.6 1.4 %copy-start.1 = (f32[32,144,128]{2,1,0:T(8,128)}, f32[32,144,128]{2,1,0:T(8,128)S(1)}, u32[]{:S(2)}) copy-start(f32[32,144,128]{2,1,0:T(8,128)S(1)} %all-to-all-done) | copy-start | bytes 7077892
  84.6 6.8 %collective-permute-start.4 = (f32[256,36,2]{0,2,1:T(2,128)S(1)}, f32[256,36,2]{0,2,1:T(2,128)S(1)}, u32[]{:S(2)}, u32[]{:S(2)}) collective-permute-start(f32[256,36,2]{0,2,1:T(2,128)S(1)} %get-tuple-element.6), channel_id=1, source_target_pairs={{0,4},{4,8},{8,12},{12,16},{16,20},{20,24},{24,28},{28,32},{32,36}... | collective-permute-start | bytes 221192 | tf_op jit(solution)/shard_map/ppermute | solution.py:26
  89.5 9.3 %collective-permute-start.5 = (f32[256,36,2]{0,2,1:T(2,128)S(1)}, f32[256,36,2]{0,2,1:T(2,128)S(1)}, u32[]{:S(2)}, u32[]{:S(2)}) collective-permute-start(f32[256,36,2]{0,2,1:T(2,128)S(1)} %get-tuple-element.7), channel_id=1, source_target_pairs={{4,0},{8,4},{12,8},{16,12},{20,16},{24,20},{28,24},{32,28},{36,32}... | collective-permute-start | bytes 221192 | tf_op jit(solution)/shard_map/ppermute | solution.py:29

commit v13 on v10

--- a/solution.py
+++ b/solution.py
@@ -115,9 +115,14 @@
     )(phase, weights, top, bottom)
 
 
-def invert_kernel(rows, x_ref, pseudo_ref, design_ref, s_ref, r_ref):
+def invert_kernel(rows, x_ref, pseudo_in, design_in, s_ref, r_ref, pseudo_ref, design_ref):
     ifg = pseudo_ref.shape[1]
     own = rows - FILTER_HALO
+    epochs = pseudo_in.shape[0]
+    pseudo_ref[...] = jnp.zeros(pseudo_ref.shape, jnp.float32)
+    design_ref[...] = jnp.zeros(design_ref.shape, jnp.float32)
+    pseudo_ref[pl.ds(0, epochs), :] = pseudo_in[...]
+    design_ref[:, pl.ds(0, epochs)] = design_in[...]
     pseudo = pseudo_ref[...]
     design = design_ref[...]
     for k in range(rows):
@@ -138,13 +143,12 @@
     ifg = pseudo.shape[1]
     epochs = pseudo.shape[0]
     wide = epochs + (-epochs) % 8
-    pseudo = jnp.pad(pseudo, ((0, wide - epochs), (0, 0)))
-    design = jnp.pad(design, ((0, 0), (0, wide - epochs)))
     whole = pl.BlockSpec(memory_space=pltpu.VMEM)
     series_t, residual_t = pl.pallas_call(
         functools.partial(invert_kernel, rows),
         in_specs=[whole, whole, whole],
         out_specs=(whole, whole),
+        scratch_shapes=[pltpu.VMEM((wide, ifg), jnp.float32), pltpu.VMEM((ifg, wide), jnp.float32)],
         out_shape=(
             jax.ShapeDtypeStruct((2 * (rows - FILTER_HALO) * 64, wide), jnp.float32),
             jax.ShapeDtypeStruct((2 * rows * 64, ifg), jnp.float32),

time: 95.2 us -> 95.2 us (level)
  local copies, waits for them, and re-layouts: 6.8 us -> 5.49 us
    pad x2 -> x0, local copies, waits for them, and re-layouts: 1.31 us -> none  [the longest x1 0.67 us: invert(): design = jnp.pad(design, ((0, 0), (0, wide - epochs)))]
where the time goes in v13:
time: 95.2 us; the launch traced here: 94.6 us
  starting transfers between devices  23.6 us (25%)
  other arithmetic  22.9 us (24%)
  Pallas kernels  22.9 us (24%)
  waiting for transfers between devices  17.1 us (18%)
  local copies, waits for them, and re-layouts  5.49 us (6%)
  matrix products  1.79 us (2%)
    pallas_call x1, Pallas kernels, unwrap(): pl.pallas_call(functools.partial(unwrap_kernel, rows_out), grid=(n // per...  16.5 us
    ppermute x1, waiting for transfers between devices, on_device(): top = lax.ppermute(edge_low, 'rows', forward)  9.69 us
    another operation x3, other arithmetic, network_maps(): factor = jnp.linalg.cholesky(normal_matrix)  9.36 us
    all_to_all x1, starting transfers between devices, on_device(): lax.all_to_all(current, 'ifg', split_axis=0, concat_axis=0, tiled=True)  8.16 us
    another operation x2, other arithmetic, network_maps(): pseudo = jax.scipy.linalg.cho_solve((factor, True), design.T)  7.94 us
    pallas_call x1, Pallas kernels, invert(): pl.pallas_call(functools.partial(invert_kernel, rows), in_specs=[whole, w...  6.45 us
    ppermute x1, waiting for transfers between devices, on_device(): bottom = lax.ppermute(edge_high, 'rows', backward)  6 us
    ppermute x1, starting transfers between devices, on_device(): top = lax.ppermute(edge_low, 'rows', forward)  5.21 us
  transfers between devices with their start and end apart: 5, of which 3 were waited for; matrix products, arithmetic and copies ran while one was open for 21% of the time, Pallas kernels for 0%

profile of v13, /device:TPU:9, one launch (start us, length us, event | category | flops | bytes accessed | tf_op | source)
XLA Modules:
  0.0 94.6 jit_solution(3096970645514969551)
XLA Ops:
  0.6 0.0 copy-start
  0.6 1.4 %slice_bitcast_fusion = (f32[1,8,8,2048]{3,2,1,0:T(8,128)S(1)}, f32[1,8,8,2048]{3,2,1,0:T(8,128)S(1)}) fusion(f32[8,32,2048]{2,1,0:T(8,128)} %ph_ref.1), kind=kLoop, calls=%fused_computation.21 | loop fusion | bytes 2097152 | tf_op jit(solution)/shard_map/stack | solution.py:195
  2.1 0.4 copy-done
  2.5 0.1 convert_bitcast_fusion
  2.6 0.1 pad_maximum_fusion.1
  2.7 5.2 %collective-permute-start = (f32[2,8,8,2048]{3,2,1,0:T(8,128)S(1)}, f32[2,8,8,2048]{3,2,1,0:T(8,128)S(1)}, u32[]{:S(2)}, u32[]{:S(2)}) collective-permute-start(f32[2,8,8,2048]{3,2,1,0:T(8,128)S(1)} %pad_maximum_fusion.1), channel_id=1, source_target_pairs={{0,1},{1,2},{2,3},{4,5},{5,6},{6,7},{8,9},{9,10},{10,11},{12,13},{... | collective-permute-start | bytes 3145736 | tf_op jit(solution)/shard_map/ppermute | solution.py:196
  7.9 0.1 pad_maximum_fusion.2
  8.0 1.9 %collective-permute-start.1 = (f32[2,8,8,2048]{3,2,1,0:T(8,128)S(1)}, f32[2,8,8,2048]{3,2,1,0:T(8,128)S(1)}, u32[]{:S(2)}, u32[]{:S(2)}) collective-permute-start(f32[2,8,8,2048]{3,2,1,0:T(8,128)S(1)} %pad_maximum_fusion.2), channel_id=1, source_target_pairs={{1,0},{2,1},{3,2},{5,4},{6,5},{7,6},{9,8},{10,9},{11,10},{13,12},{... | collective-permute-start | bytes 3145736 | tf_op jit(solution)/shard_map/ppermute | solution.py:197
  10.0 9.7 %collective-permute-done.top_ref = f32[2,8,8,2048]{3,2,1,0:T(8,128)S(1)} collective-permute-done((f32[2,8,8,2048]{3,2,1,0:T(8,128)S(1)}, f32[2,8,8,2048]{3,2,1,0:T(8,128)S(1)}, u32[]{:S(2)}, u32[]{:S(2)}) %collective-permute-start) | collective-permute-done | bytes 1048608 | tf_op jit(solution)/shard_map/ppermute | solution.py:196
  19.7 6.0 %collective-permute-done.1.bot_ref = f32[2,8,8,2048]{3,2,1,0:T(8,128)S(1)} collective-permute-done((f32[2,8,8,2048]{3,2,1,0:T(8,128)S(1)}, f32[2,8,8,2048]{3,2,1,0:T(8,128)S(1)}, u32[]{:S(2)}, u32[]{:S(2)}) %collective-permute-start.1) | collective-permute-done | bytes 1048608 | tf_op jit(solution)/shard_map/ppermute | solution.py:197
  25.7 1.0 %copy-done.3 = f32[2,8,8,2048]{3,2,1,0:T(8,128)} copy-done((f32[2,8,8,2048]{3,2,1,0:T(8,128)}, f32[2,8,8,2048]{3,2,1,0:T(8,128)S(1)}, u32[]{:S(2)}) %copy-start.3) | copy-done | bytes 1048600
  26.6 16.5 %shard_map.50 = f32[32,144,128]{2,1,0:T(8,128)} custom-call(f32[8,32,2048]{2,1,0:T(8,128)} %ph_ref.1, s32[8,32,2048]{2,1,0:T(8,128)} %wt_ref.1, f32[2,8,8,2048]{3,2,1,0:T(8,128)} %copy-done.2, f32[2,8,8,2048]{3,2,1,0:T(8,128)} %copy-done.3), custom_call_target="tpu_custom_call" | custom-call | flops 94371840 | bytes 8388608 | tf_op jit(solution)/shard_map/pallas_call | solution.py:100
  43.1 8.2 %all-to-all-start = ((f32[32,144,128]{2,1,0:T(8,128)}), f32[32,144,128]{2,1,0:T(8,128)S(1)}, u32[]{:S(2)}, u32[]{:S(2)}) async-start(f32[32,144,128]{2,1,0:T(8,128)} %shard_map.50), calls=%async_computation | async-start | bytes 4718592 | tf_op jit(solution)/shard_map/all_to_all | solution.py:199
  51.3 0.5 fusion.12
  51.9 0.1 copy.5
  52.0 8.7 %cholesky.16 = f32[95,95]{1,0:T(8,128)S(1)} custom-call(f32[95,95]{1,0:T(8,128)S(1)} %fusion.17), custom_call_target="Cholesky" | custom-call | tf_op jit(solution)/shard_map/jit(cholesky)/cholesky | solution.py:183
  60.7 0.6 compare_reduce_fusion
  61.3 0.7 fusion.13
  62.0 7.3 %custom-call.10 = f32[1,95,95]{1,2,0:T(8,128)S(1)} custom-call(f32[1,95,95]{2,1,0:T(8,128)S(1)} %fusion.13), custom_call_target="InvertDiagBlocksLowerTriangular" | custom-call | tf_op jit(solution)/shard_map/jit(_cho_solve)/triangular_solve | solution.py:184
  69.3 0.8 convert_subtract_fusion.design_in
  70.1 0.4 fusion.11
  70.5 0.9 fusion.14.pseudo_in
  71.3 0.0 all-to-all-done
  71.3 1.4 %copy-done.1 = f32[32,144,128]{2,1,0:T(8,128)} copy-done((f32[32,144,128]{2,1,0:T(8,128)}, f32[32,144,128]{2,1,0:T(8,128)S(1)}, u32[]{:S(2)}) %copy-start.1) | copy-done | bytes 2359320
  72.7 6.5 %shard_map.51 = (f32[2048,96]{1,0:T(8,128)}, f32[2304,256]{1,0:T(8,128)}) custom-call(f32[4608,128]{1,0:T(8,128)} %bitcast.32, f32[95,256]{1,0:T(8,128)} %fusion.14.pseudo_in, f32[256,95]{1,0:T(8,128)} %convert_subtract_fusion.design_in), custom_call_target="tpu_custom_call" | custom-call | flops 1358954496 | bytes 5603328 | tf_op jit(solution)/shard_map/pallas_call | solution.py:147
  79.2 1.1 %fusion.20 = (f32[256,36,2]{0,2,1:T(2,128)S(1)}, f32[256,36,2]{0,2,1:T(2,128)S(1)}) fusion(f32[256,36,64]{0,2,1:T(8,128)} %bitcast.30), kind=kLoop, calls=%fused_computation.43 | loop fusion | bytes 294912 | tf_op jit(solution)/shard_map/slice | solution.py:26
  80.3 3.1 %collective-permute-start.2 = (f32[256,36,2]{0,2,1:T(2,128)S(1)}, f32[256,36,2]{0,2,1:T(2,128)S(1)}, u32[]{:S(2)}, u32[]{:S(2)}) collective-permute-start(f32[256,36,2]{0,2,1:T(2,128)S(1)} %get-tuple-element.6), channel_id=1, source_target_pairs={{0,4},{4,8},{8,12},{12,16},{16,20},{20,24},{24,28},{28,32},{32,36}... | collective-permute-start | bytes 221192 | tf_op jit(solution)/shard_map/ppermute | solution.py:25
  83.4 5.2 %collective-permute-start.3 = (f32[256,36,2]{0,2,1:T(2,128)S(1)}, f32[256,36,2]{0,2,1:T(2,128)S(1)}, u32[]{:S(2)}, u32[]{:S(2)}) collective-permute-start(f32[256,36,2]{0,2,1:T(2,128)S(1)} %get-tuple-element.7), channel_id=1, source_target_pairs={{4,0},{8,4},{12,8},{16,12},{20,16},{24,20},{28,24},{32,28},{36,32}... | collective-permute-start | bytes 221192 | tf_op jit(solution)/shard_map/ppermute | solution.py:28
  88.6 1.4 %collective-permute-done.3 = f32[256,36,2]{0,2,1:T(2,128)S(1)} collective-permute-done((f32[256,36,2]{0,2,1:T(2,128)S(1)}, f32[256,36,2]{0,2,1:T(2,128)S(1)}, u32[]{:S(2)}, u32[]{:S(2)}) %collective-permute-start.3) | collective-permute-done | bytes 73760 | tf_op jit(solution)/shard_map/ppermute | solution.py:28
  90.0 1.9 %pad_maximum_fusion = f32[256,36,68]{0,2,1:T(8,128)S(1)} fusion(f32[256,36,2]{0,2,1:T(2,128)S(1)} %collective-permute-done.3, f32[256,36,64]{0,2,1:T(8,128)} %bitcast.31, f32[256,36,2]{0,2,1:T(2,128)S(1)} %collective-permute-done.2), kind=kLoop, calls=%fused_computation | loop fusion | flops 1253376 | bytes 5013504 | tf_op jit(solution)/shard_map/concatenate | solution.py:29
  91.9 0.5 fusion
  92.5 2.1 %fusion.5 = bf16[256,32,64]{0,2,1:T(8,128)(2,1)} fusion(f32[256,32,68]{0,2,1:T(8,128)S(1)} %fusion), kind=kLoop, calls=%fused_computation.11 | loop fusion | flops 4718592 | bytes 11534336 | tf_op jit(solution)/shard_map/convert_element_type | solution.py:210
  (10 shorter events, 0.1 us)
Async XLA Ops:
  0.6 1.9 %copy-start = (s32[8,32,2048]{2,1,0:T(8,128)S(1)}, s32[8,32,2048]{2,1,0:T(8,128)}, u32[]{:S(2)}) copy-start(s32[8,32,2048]{2,1,0:T(8,128)} %wt_ref.1) | copy-start | bytes 6291460
  2.7 16.9 %collective-permute-start = (f32[2,8,8,2048]{3,2,1,0:T(8,128)S(1)}, f32[2,8,8,2048]{3,2,1,0:T(8,128)S(1)}, u32[]{:S(2)}, u32[]{:S(2)}) collective-permute-start(f32[2,8,8,2048]{3,2,1,0:T(8,128)S(1)} %pad_maximum_fusion.1), channel_id=1, source_target_pairs={{0,1},{1,2},{2,3},{4,5},{5,6},{6,7},{8,9},{9,10},{10,11},{12,13},{... | collective-permute-start | bytes 3145736 | tf_op jit(solution)/shard_map/ppermute | solution.py:196
  8.0 17.6 %collective-permute-start.1 = (f32[2,8,8,2048]{3,2,1,0:T(8,128)S(1)}, f32[2,8,8,2048]{3,2,1,0:T(8,128)S(1)}, u32[]{:S(2)}, u32[]{:S(2)}) collective-permute-start(f32[2,8,8,2048]{3,2,1,0:T(8,128)S(1)} %pad_maximum_fusion.2), channel_id=1, source_target_pairs={{1,0},{2,1},{3,2},{5,4},{6,5},{7,6},{9,8},{10,9},{11,10},{13,12},{... | collective-permute-start | bytes 3145736 | tf_op jit(solution)/shard_map/ppermute | solution.py:197
  19.7 6.0 %copy-start.2 = (f32[2,8,8,2048]{3,2,1,0:T(8,128)}, f32[2,8,8,2048]{3,2,1,0:T(8,128)S(1)}, u32[]{:S(2)}) copy-start(f32[2,8,8,2048]{3,2,1,0:T(8,128)S(1)} %collective-permute-done.top_ref) | copy-start | bytes 3145732
  25.7 1.0 %copy-start.3 = (f32[2,8,8,2048]{3,2,1,0:T(8,128)}, f32[2,8,8,2048]{3,2,1,0:T(8,128)S(1)}, u32[]{:S(2)}) copy-start(f32[2,8,8,2048]{3,2,1,0:T(8,128)S(1)} %collective-permute-done.1.bot_ref) | copy-start | bytes 3145732
  43.1 8.2 %copy-start.4 = (s32[256,2]{0,1:T(2,128)S(1)}, s32[256,2]{0,1:T(2,128)}, u32[]{:S(2)}) copy-start(s32[256,2]{0,1:T(2,128)} %param.5) | copy-start | bytes 6148
  43.1 28.2 %all-to-all-start = ((f32[32,144,128]{2,1,0:T(8,128)}), f32[32,144,128]{2,1,0:T(8,128)S(1)}, u32[]{:S(2)}, u32[]{:S(2)}) async-start(f32[32,144,128]{2,1,0:T(8,128)} %shard_map.50), calls=%async_computation | async-start | bytes 4718592 | tf_op jit(solution)/shard_map/all_to_all | solution.py:199
  71.3 1.4 %copy-start.1 = (f32[32,144,128]{2,1,0:T(8,128)}, f32[32,144,128]{2,1,0:T(8,128)S(1)}, u32[]{:S(2)}) copy-start(f32[32,144,128]{2,1,0:T(8,128)S(1)} %all-to-all-done) | copy-start | bytes 7077892
  80.3 8.3 %collective-permute-start.2 = (f32[256,36,2]{0,2,1:T(2,128)S(1)}, f32[256,36,2]{0,2,1:T(2,128)S(1)}, u32[]{:S(2)}, u32[]{:S(2)}) collective-permute-start(f32[256,36,2]{0,2,1:T(2,128)S(1)} %get-tuple-element.6), channel_id=1, source_target_pairs={{0,4},{4,8},{8,12},{12,16},{16,20},{20,24},{24,28},{28,32},{32,36}... | collective-permute-start | bytes 221192 | tf_op jit(solution)/shard_map/ppermute | solution.py:25
  83.4 6.6 %collective-permute-start.3 = (f32[256,36,2]{0,2,1:T(2,128)S(1)}, f32[256,36,2]{0,2,1:T(2,128)S(1)}, u32[]{:S(2)}, u32[]{:S(2)}) collective-permute-start(f32[256,36,2]{0,2,1:T(2,128)S(1)} %get-tuple-element.7), channel_id=1, source_target_pairs={{4,0},{8,4},{12,8},{16,12},{20,16},{24,20},{28,24},{32,28},{36,32}... | collective-permute-start | bytes 221192 | tf_op jit(solution)/shard_map/ppermute | solution.py:28

commit v14 on v13

--- a/solution.py
+++ b/solution.py
@@ -162,6 +162,47 @@
     return series_t[:, :epochs], residual_t
 
 
+def filter_kernel(res_ref, left_ref, right_ref, o_ref, pad_ref, rows_ref):
+    n_rows, n_cols = o_ref.shape[0], o_ref.shape[1]
+    h = FILTER_HALO
+    pad_ref[:, pl.ds(0, h), :] = left_ref[...]
+    pad_ref[:, pl.ds(h, n_cols), :] = res_ref[...]
+    pad_ref[:, pl.ds(h + n_cols, h), :] = right_ref[...]
+
+    def tap(ref, offset, axis, length):
+        if axis == 0:
+            return ref[pl.ds(offset, length)]
+        return ref[:, pl.ds(offset, length), :]
+
+    rows_ref[...] = (
+        tap(pad_ref, 0, 0, n_rows) + 4.0 * tap(pad_ref, 1, 0, n_rows) + 6.0 * tap(pad_ref, 2, 0, n_rows)
+        + 4.0 * tap(pad_ref, 3, 0, n_rows) + tap(pad_ref, 4, 0, n_rows)
+    ) * 0.0625
+    out = (
+        tap(rows_ref, 0, 1, n_cols) + 4.0 * tap(rows_ref, 1, 1, n_cols) + 6.0 * tap(rows_ref, 2, 1, n_cols)
+        + 4.0 * tap(rows_ref, 3, 1, n_cols) + tap(rows_ref, 4, 1, n_cols)
+    ) * 0.0625
+    o_ref[...] = out.astype(o_ref.dtype)
+
+
+def low_pass(res, left, right, rows):
+    tall, n_cols, ifg = res.shape
+    whole = pl.BlockSpec(memory_space=pltpu.VMEM)
+    return pl.pallas_call(
+        filter_kernel,
+        in_specs=[whole, whole, whole],
+        out_specs=whole,
+        out_shape=jax.ShapeDtypeStruct((rows, n_cols, ifg), jnp.bfloat16),
+        scratch_shapes=[
+            pltpu.VMEM((tall, n_cols + 2 * FILTER_HALO, ifg), jnp.float32),
+            pltpu.VMEM((rows, n_cols + 2 * FILTER_HALO, ifg), jnp.float32),
+        ],
+        cost_estimate=pl.CostEstimate(
+            flops=20 * tall * n_cols * ifg, bytes_accessed=6 * tall * n_cols * ifg, transcendentals=0
+        ),
+    )(res, left, right)
+
+
 def binomial(padded, axis):
     length = padded.shape[axis] - 4
 
@@ -204,10 +245,15 @@
         return x.reshape(-1, 64, x.shape[1]).transpose(2, 0, 1)
 
     series_block = unpack(series_t)
-    residual = unpack(residual_t)
-    padded = extended_2(residual, (("ifg", 2),), FILTER_HALO)
-    filtered = binomial(binomial(padded, 1), 2)
-    return (series_block, filtered.astype(jnp.bfloat16))
+    ifg = residual_t.shape[1]
+    res = residual_t.reshape(-1, 64, ifg)
+    count = lax.axis_size("ifg")
+    forward = [(i, i + 1) for i in range(count - 1)]
+    backward = [(target, source) for source, target in forward]
+    left = lax.ppermute(res[:, 64 - FILTER_HALO :], "ifg", forward)
+    right = lax.ppermute(res[:, :FILTER_HALO], "ifg", backward)
+    filtered = low_pass(res, left, right, rows).transpose(2, 0, 1)
+    return (series_block, filtered)
 
 
 def solution(mesh):

time: 95.2 us -> 101 us (1.061)
  Pallas kernels: 22.9 us -> 29.2 us
  waiting for transfers between devices: 17.1 us -> 21.9 us
  other arithmetic: 22.9 us -> 18.4 us
  starting transfers between devices: 23.6 us -> 22.4 us
    pallas_call x0 -> x1, Pallas kernels: none -> 6.29 us  [low_pass(): pl.pallas_call(filter_kernel, in_specs=[whole, whole, whole], out_specs=w...]
    ppermute x2, waiting for transfers between devices: 1.38 us -> 6.16 us  [the longest x1 6.16 us: on_device(): left = lax.ppermute(res[:, 64 - FILTER_HALO:], 'ifg', forward)]
    convert_element_type x1 -> x0, other arithmetic: 2.13 us -> none  [on_device(): return (series_block, filtered.astype(jnp.bfloat16))]
    concatenate x1 -> x0, other arithmetic: 1.91 us -> none  [extended_2(): block = jnp.concatenate([low, block, high], axis=dim)]
    ppermute x2, starting transfers between devices: 8.29 us -> 7.12 us  [the longest x1 5.2 us: on_device(): right = lax.ppermute(res[:, :FILTER_HALO], 'ifg', backward)]
    unnamed x10 -> x14, local copies, waits for them, and re-layouts: 2.84 us -> 3.46 us
  transfers between devices with their start and end apart: 5 -> 5, of which waited for: 3 -> 3; matrix products, arithmetic and copies ran while one was open for 21% -> 20% of each run, Pallas kernels for 0% -> 0%
where the time goes in v14:
time: 101 us
  Pallas kernels  29.2 us (29%)
  starting transfers between devices  22.4 us (22%)
  waiting for transfers between devices  21.9 us (22%)
  other arithmetic  18.4 us (18%)
  local copies, waits for them, and re-layouts  6.11 us (6%)
  matrix products  1.79 us (2%)
    pallas_call x1, Pallas kernels, unwrap(): pl.pallas_call(functools.partial(unwrap_kernel, rows_out), grid=(n // per...  16.5 us
    ppermute x1, waiting for transfers between devices, on_device(): top = lax.ppermute(edge_low, 'rows', forward)  9.69 us
    another operation x3, other arithmetic, network_maps(): factor = jnp.linalg.cholesky(normal_matrix)  9.36 us
    all_to_all x1, starting transfers between devices, on_device(): lax.all_to_all(current, 'ifg', split_axis=0, concat_axis=0, tiled=True)  8.16 us
    another operation x2, other arithmetic, network_maps(): pseudo = jax.scipy.linalg.cho_solve((factor, True), design.T)  7.94 us
    pallas_call x1, Pallas kernels, invert(): pl.pallas_call(functools.partial(invert_kernel, rows), in_specs=[whole, w...  6.47 us
    pallas_call x1, Pallas kernels, low_pass(): pl.pallas_call(filter_kernel, in_specs=[whole, whole, whole], out_specs=w...  6.29 us
    ppermute x1, waiting for transfers between devices, on_device(): left = lax.ppermute(res[:, 64 - FILTER_HALO:], 'ifg', forward)  6.16 us
  transfers between devices with their start and end apart: 5, of which 3 were waited for; matrix products, arithmetic and copies ran while one was open for 20% of the time, Pallas kernels for 0%

profile of v14, /device:TPU:9, one launch (start us, length us, event | category | flops | bytes accessed | tf_op | source)
XLA Modules:
  0.0 100.6 jit_solution(707911137623390347)
XLA Ops:
  0.6 0.0 copy-start
  0.6 1.4 %slice_bitcast_fusion = (f32[1,8,8,2048]{3,2,1,0:T(8,128)S(1)}, f32[1,8,8,2048]{3,2,1,0:T(8,128)S(1)}) fusion(f32[8,32,2048]{2,1,0:T(8,128)} %ph_ref.1), kind=kLoop, calls=%fused_computation.3 | loop fusion | bytes 2097152 | tf_op jit(solution)/shard_map/stack | solution.py:236
  2.1 0.4 copy-done
  2.5 0.1 convert_bitcast_fusion
  2.6 0.1 pad_maximum_fusion
  2.7 5.2 %collective-permute-start = (f32[2,8,8,2048]{3,2,1,0:T(8,128)S(1)}, f32[2,8,8,2048]{3,2,1,0:T(8,128)S(1)}, u32[]{:S(2)}, u32[]{:S(2)}) collective-permute-start(f32[2,8,8,2048]{3,2,1,0:T(8,128)S(1)} %pad_maximum_fusion), channel_id=1, source_target_pairs={{0,1},{1,2},{2,3},{4,5},{5,6},{6,7},{8,9},{9,10},{10,11},{12,13},{... | collective-permute-start | bytes 3145736 | tf_op jit(solution)/shard_map/ppermute | solution.py:237
  7.9 0.1 pad_maximum_fusion.1
  8.0 1.9 %collective-permute-start.1 = (f32[2,8,8,2048]{3,2,1,0:T(8,128)S(1)}, f32[2,8,8,2048]{3,2,1,0:T(8,128)S(1)}, u32[]{:S(2)}, u32[]{:S(2)}) collective-permute-start(f32[2,8,8,2048]{3,2,1,0:T(8,128)S(1)} %pad_maximum_fusion.1), channel_id=1, source_target_pairs={{1,0},{2,1},{3,2},{5,4},{6,5},{7,6},{9,8},{10,9},{11,10},{13,12},{... | collective-permute-start | bytes 3145736 | tf_op jit(solution)/shard_map/ppermute | solution.py:238
  10.0 9.7 %collective-permute-done.top_ref = f32[2,8,8,2048]{3,2,1,0:T(8,128)S(1)} collective-permute-done((f32[2,8,8,2048]{3,2,1,0:T(8,128)S(1)}, f32[2,8,8,2048]{3,2,1,0:T(8,128)S(1)}, u32[]{:S(2)}, u32[]{:S(2)}) %collective-permute-start) | collective-permute-done | bytes 1048608 | tf_op jit(solution)/shard_map/ppermute | solution.py:237
  19.7 6.0 %collective-permute-done.1.bot_ref = f32[2,8,8,2048]{3,2,1,0:T(8,128)S(1)} collective-permute-done((f32[2,8,8,2048]{3,2,1,0:T(8,128)S(1)}, f32[2,8,8,2048]{3,2,1,0:T(8,128)S(1)}, u32[]{:S(2)}, u32[]{:S(2)}) %collective-permute-start.1) | collective-permute-done | bytes 1048608 | tf_op jit(solution)/shard_map/ppermute | solution.py:238
  25.7 1.0 copy-done.3
  26.6 16.5 %shard_map.50 = f32[32,144,128]{2,1,0:T(8,128)} custom-call(f32[8,32,2048]{2,1,0:T(8,128)} %ph_ref.1, s32[8,32,2048]{2,1,0:T(8,128)} %wt_ref.1, f32[2,8,8,2048]{3,2,1,0:T(8,128)} %copy-done.2, f32[2,8,8,2048]{3,2,1,0:T(8,128)} %copy-done.3), custom_call_target="tpu_custom_call" | custom-call | flops 94371840 | bytes 8388608 | tf_op jit(solution)/shard_map/pallas_call | solution.py:100
  43.1 8.2 %all-to-all-start = ((f32[32,144,128]{2,1,0:T(8,128)}), f32[32,144,128]{2,1,0:T(8,128)S(1)}, u32[]{:S(2)}, u32[]{:S(2)}) async-start(f32[32,144,128]{2,1,0:T(8,128)} %shard_map.50), calls=%async_computation | async-start | bytes 4718592 | tf_op jit(solution)/shard_map/all_to_all | solution.py:240
  51.3 0.5 fusion.3
  51.9 0.1 copy.5
  52.0 8.7 %cholesky.16 = f32[95,95]{1,0:T(8,128)S(1)} custom-call(f32[95,95]{1,0:T(8,128)S(1)} %fusion.8), custom_call_target="Cholesky" | custom-call | tf_op jit(solution)/shard_map/jit(cholesky)/cholesky | solution.py:224
  60.7 0.6 compare_reduce_fusion
  61.4 0.7 fusion.4
  62.0 7.3 %custom-call.10 = f32[1,95,95]{1,2,0:T(8,128)S(1)} custom-call(f32[1,95,95]{2,1,0:T(8,128)S(1)} %fusion.4), custom_call_target="InvertDiagBlocksLowerTriangular" | custom-call | tf_op jit(solution)/shard_map/jit(_cho_solve)/triangular_solve | solution.py:225
  69.3 0.8 convert_subtract_fusion.design_in
  70.1 0.4 fusion.2
  70.5 0.9 fusion.5.pseudo_in
  71.3 0.0 all-to-all-done
  71.3 1.4 %copy-done.1 = f32[32,144,128]{2,1,0:T(8,128)} copy-done((f32[32,144,128]{2,1,0:T(8,128)}, f32[32,144,128]{2,1,0:T(8,128)S(1)}, u32[]{:S(2)}) %copy-start.1) | copy-done | bytes 2359320
  72.7 6.5 %shard_map.51 = (f32[2048,96]{1,0:T(8,128)}, f32[2304,256]{1,0:T(8,128)}) custom-call(f32[4608,128]{1,0:T(8,128)} %bitcast.31, f32[95,256]{1,0:T(8,128)} %fusion.5.pseudo_in, f32[256,95]{1,0:T(8,128)} %convert_subtract_fusion.design_in), custom_call_target="tpu_custom_call" | custom-call | flops 1358954496 | bytes 5603328 | tf_op jit(solution)/shard_map/pallas_call | solution.py:147
  79.2 1.1 %fusion.11 = (f32[36,2,256]{2,1,0:T(2,128)S(1)}, f32[36,2,256]{2,1,0:T(2,128)S(1)}) fusion(f32[36,64,256]{2,1,0:T(8,128)} %bitcast.29), kind=kLoop, calls=%fused_computation.25 | loop fusion | bytes 294912 | tf_op jit(solution)/shard_map/slice | solution.py:254
  80.3 5.2 %collective-permute-start.3 = (f32[36,2,256]{2,1,0:T(2,128)S(1)}, f32[36,2,256]{2,1,0:T(2,128)S(1)}, u32[]{:S(2)}, u32[]{:S(2)}) collective-permute-start(f32[36,2,256]{2,1,0:T(2,128)S(1)} %get-tuple-element.6), channel_id=1, source_target_pairs={{4,0},{8,4},{12,8},{16,12},{20,16},{24,20},{28,24},{32,28},{36,32}... | collective-permute-start | bytes 221192 | tf_op jit(solution)/shard_map/ppermute | solution.py:254
  85.5 1.9 %collective-permute-start.2 = (f32[36,2,256]{2,1,0:T(2,128)S(1)}, f32[36,2,256]{2,1,0:T(2,128)S(1)}, u32[]{:S(2)}, u32[]{:S(2)}) collective-permute-start(f32[36,2,256]{2,1,0:T(2,128)S(1)} %get-tuple-element.7), channel_id=1, source_target_pairs={{0,4},{4,8},{8,12},{12,16},{16,20},{20,24},{24,28},{28,32},{32,36}... | collective-permute-start | bytes 221192 | tf_op jit(solution)/shard_map/ppermute | solution.py:253
  87.5 0.0 collective-permute-done.3.right_ref
  87.5 6.2 %collective-permute-done.2.left_ref = f32[36,2,256]{2,1,0:T(2,128)S(1)} collective-permute-done((f32[36,2,256]{2,1,0:T(2,128)S(1)}, f32[36,2,256]{2,1,0:T(2,128)S(1)}, u32[]{:S(2)}, u32[]{:S(2)}) %collective-permute-start.2) | collective-permute-done | bytes 73760 | tf_op jit(solution)/shard_map/ppermute | solution.py:253
  93.6 0.6 copy-done.5
  94.3 6.3 %shard_map.52 = bf16[32,64,256]{2,1,0:T(8,128)(2,1)} custom-call(f32[36,64,256]{2,1,0:T(8,128)} %bitcast.30, f32[36,2,256]{2,1,0:T(2,128)} %copy-done.5, f32[36,2,256]{2,1,0:T(2,128)} %copy-done.4), custom_call_target="tpu_custom_call" | custom-call | flops 11796480 | bytes 3538944 | tf_op jit(solution)/shard_map/pallas_call | solution.py:191
  (12 shorter events, 0.1 us)
Async XLA Ops:
  0.6 1.9 %copy-start = (s32[8,32,2048]{2,1,0:T(8,128)S(1)}, s32[8,32,2048]{2,1,0:T(8,128)}, u32[]{:S(2)}) copy-start(s32[8,32,2048]{2,1,0:T(8,128)} %wt_ref.1) | copy-start | bytes 6291460
  2.7 16.9 %collective-permute-start = (f32[2,8,8,2048]{3,2,1,0:T(8,128)S(1)}, f32[2,8,8,2048]{3,2,1,0:T(8,128)S(1)}, u32[]{:S(2)}, u32[]{:S(2)}) collective-permute-start(f32[2,8,8,2048]{3,2,1,0:T(8,128)S(1)} %pad_maximum_fusion), channel_id=1, source_target_pairs={{0,1},{1,2},{2,3},{4,5},{5,6},{6,7},{8,9},{9,10},{10,11},{12,13},{... | collective-permute-start | bytes 3145736 | tf_op jit(solution)/shard_map/ppermute | solution.py:237
  8.0 17.6 %collective-permute-start.1 = (f32[2,8,8,2048]{3,2,1,0:T(8,128)S(1)}, f32[2,8,8,2048]{3,2,1,0:T(8,128)S(1)}, u32[]{:S(2)}, u32[]{:S(2)}) collective-permute-start(f32[2,8,8,2048]{3,2,1,0:T(8,128)S(1)} %pad_maximum_fusion.1), channel_id=1, source_target_pairs={{1,0},{2,1},{3,2},{5,4},{6,5},{7,6},{9,8},{10,9},{11,10},{13,12},{... | collective-permute-start | bytes 3145736 | tf_op jit(solution)/shard_map/ppermute | solution.py:238
  19.7 6.0 %copy-start.2 = (f32[2,8,8,2048]{3,2,1,0:T(8,128)}, f32[2,8,8,2048]{3,2,1,0:T(8,128)S(1)}, u32[]{:S(2)}) copy-start(f32[2,8,8,2048]{3,2,1,0:T(8,128)S(1)} %collective-permute-done.top_ref) | copy-start | bytes 3145732
  25.7 1.0 copy-start.3
  43.1 8.2 %copy-start.6 = (s32[256,2]{0,1:T(2,128)S(1)}, s32[256,2]{0,1:T(2,128)}, u32[]{:S(2)}) copy-start(s32[256,2]{0,1:T(2,128)} %param.5) | copy-start | bytes 6148
  43.1 28.2 %all-to-all-start = ((f32[32,144,128]{2,1,0:T(8,128)}), f32[32,144,128]{2,1,0:T(8,128)S(1)}, u32[]{:S(2)}, u32[]{:S(2)}) async-start(f32[32,144,128]{2,1,0:T(8,128)} %shard_map.50), calls=%async_computation | async-start | bytes 4718592 | tf_op jit(solution)/shard_map/all_to_all | solution.py:240
  71.3 1.4 %copy-start.1 = (f32[32,144,128]{2,1,0:T(8,128)}, f32[32,144,128]{2,1,0:T(8,128)S(1)}, u32[]{:S(2)}) copy-start(f32[32,144,128]{2,1,0:T(8,128)S(1)} %all-to-all-done) | copy-start | bytes 7077892
  80.3 7.1 %collective-permute-start.3 = (f32[36,2,256]{2,1,0:T(2,128)S(1)}, f32[36,2,256]{2,1,0:T(2,128)S(1)}, u32[]{:S(2)}, u32[]{:S(2)}) collective-permute-start(f32[36,2,256]{2,1,0:T(2,128)S(1)} %get-tuple-element.6), channel_id=1, source_target_pairs={{4,0},{8,4},{12,8},{16,12},{20,16},{24,20},{28,24},{32,28},{36,32}... | collective-permute-start | bytes 221192 | tf_op jit(solution)/shard_map/ppermute | solution.py:254
  85.5 8.1 %collective-permute-start.2 = (f32[36,2,256]{2,1,0:T(2,128)S(1)}, f32[36,2,256]{2,1,0:T(2,128)S(1)}, u32[]{:S(2)}, u32[]{:S(2)}) collective-permute-start(f32[36,2,256]{2,1,0:T(2,128)S(1)} %get-tuple-element.7), channel_id=1, source_target_pairs={{0,4},{4,8},{8,12},{12,16},{16,20},{20,24},{24,28},{28,32},{32,36}... | collective-permute-start | bytes 221192 | tf_op jit(solution)/shard_map/ppermute | solution.py:253
  87.5 6.2 %copy-start.4 = (f32[36,2,256]{2,1,0:T(2,128)}, f32[36,2,256]{2,1,0:T(2,128)S(1)}, u32[]{:S(2)}) copy-start(f32[36,2,256]{2,1,0:T(2,128)S(1)} %collective-permute-done.3.right_ref) | copy-start | bytes 221188
  93.6 0.6 copy-start.5

commit v15 on v13

--- a/solution.py
+++ b/solution.py
@@ -124,11 +124,14 @@
     pseudo_ref[pl.ds(0, epochs), :] = pseudo_in[...]
     design_ref[:, pl.ds(0, epochs)] = design_in[...]
     pseudo = pseudo_ref[...]
-    design = design_ref[...]
+    design_b = design_ref[...].astype(jnp.bfloat16)
     for k in range(rows):
         x = x_ref[pl.ds(k, ifg, stride=rows), :]
         series = jnp.dot(pseudo, x, precision=lax.Precision.HIGH, preferred_element_type=jnp.float32)
-        fit = jnp.dot(design, series, precision=lax.Precision.HIGH, preferred_element_type=jnp.float32)
+        series_hi = series.astype(jnp.bfloat16)
+        series_lo = (series - series_hi.astype(jnp.float32)).astype(jnp.bfloat16)
+        fit = jnp.dot(design_b, series_hi, preferred_element_type=jnp.float32)
+        fit = fit + jnp.dot(design_b, series_lo, preferred_element_type=jnp.float32)
         res_t = (x - fit).T
         ser_t = series.T
         r_ref[pl.ds(k * 64, 64), :] = res_t[:64]

time: 95.2 us -> 96.3 us (1.012)
  Pallas kernels: 22.9 us -> 24.1 us
    pallas_call x1, Pallas kernels: 6.45 us -> 7.6 us  [invert(): pl.pallas_call(functools.partial(invert_kernel, rows), in_specs=[whole, w...]
where the time goes in v15:
time: 96.3 us; the launch traced here: 95.7 us
  Pallas kernels  24.1 us (25%)
  starting transfers between devices  23.6 us (25%)
  other arithmetic  22.9 us (24%)
  waiting for transfers between devices  17.1 us (18%)
  local copies, waits for them, and re-layouts  5.49 us (6%)
  matrix products  1.79 us (2%)
    pallas_call x1, Pallas kernels, unwrap(): pl.pallas_call(functools.partial(unwrap_kernel, rows_out), grid=(n // per...  16.5 us
    ppermute x1, waiting for transfers between devices, on_device(): top = lax.ppermute(edge_low, 'rows', forward)  9.69 us
    another operation x3, other arithmetic, network_maps(): factor = jnp.linalg.cholesky(normal_matrix)  9.36 us
    all_to_all x1, starting transfers between devices, on_device(): lax.all_to_all(current, 'ifg', split_axis=0, concat_axis=0, tiled=True)  8.16 us
    another operation x2, other arithmetic, network_maps(): pseudo = jax.scipy.linalg.cho_solve((factor, True), design.T)  7.94 us
    pallas_call x1, Pallas kernels, invert(): pl.pallas_call(functools.partial(invert_kernel, rows), in_specs=[whole, w...  7.6 us
    ppermute x1, waiting for transfers between devices, on_device(): bottom = lax.ppermute(edge_high, 'rows', backward)  6 us
    ppermute x1, starting transfers between devices, on_device(): top = lax.ppermute(edge_low, 'rows', forward)  5.21 us
  transfers between devices with their start and end apart: 5, of which 3 were waited for; matrix products, arithmetic and copies ran while one was open for 21% of the time, Pallas kernels for 0%

profile of v15, /device:TPU:9, one launch (start us, length us, event | category | flops | bytes accessed | tf_op | source)
XLA Modules:
  0.0 95.7 jit_solution(11270993634729641969)
XLA Ops:
  0.6 0.0 copy-start
  0.6 1.4 %slice_bitcast_fusion = (f32[1,8,8,2048]{3,2,1,0:T(8,128)S(1)}, f32[1,8,8,2048]{3,2,1,0:T(8,128)S(1)}) fusion(f32[8,32,2048]{2,1,0:T(8,128)} %ph_ref.1), kind=kLoop, calls=%fused_computation.21 | loop fusion | bytes 2097152 | tf_op jit(solution)/shard_map/stack | solution.py:198
  2.1 0.4 copy-done
  2.5 0.1 convert_bitcast_fusion
  2.6 0.1 pad_maximum_fusion.1
  2.7 5.2 %collective-permute-start = (f32[2,8,8,2048]{3,2,1,0:T(8,128)S(1)}, f32[2,8,8,2048]{3,2,1,0:T(8,128)S(1)}, u32[]{:S(2)}, u32[]{:S(2)}) collective-permute-start(f32[2,8,8,2048]{3,2,1,0:T(8,128)S(1)} %pad_maximum_fusion.1), channel_id=1, source_target_pairs={{0,1},{1,2},{2,3},{4,5},{5,6},{6,7},{8,9},{9,10},{10,11},{12,13},{... | collective-permute-start | bytes 3145736 | tf_op jit(solution)/shard_map/ppermute | solution.py:199
  7.9 0.1 pad_maximum_fusion.2
  8.0 1.9 %collective-permute-start.1 = (f32[2,8,8,2048]{3,2,1,0:T(8,128)S(1)}, f32[2,8,8,2048]{3,2,1,0:T(8,128)S(1)}, u32[]{:S(2)}, u32[]{:S(2)}) collective-permute-start(f32[2,8,8,2048]{3,2,1,0:T(8,128)S(1)} %pad_maximum_fusion.2), channel_id=1, source_target_pairs={{1,0},{2,1},{3,2},{5,4},{6,5},{7,6},{9,8},{10,9},{11,10},{13,12},{... | collective-permute-start | bytes 3145736 | tf_op jit(solution)/shard_map/ppermute | solution.py:200
  10.0 9.7 %collective-permute-done.top_ref = f32[2,8,8,2048]{3,2,1,0:T(8,128)S(1)} collective-permute-done((f32[2,8,8,2048]{3,2,1,0:T(8,128)S(1)}, f32[2,8,8,2048]{3,2,1,0:T(8,128)S(1)}, u32[]{:S(2)}, u32[]{:S(2)}) %collective-permute-start) | collective-permute-done | bytes 1048608 | tf_op jit(solution)/shard_map/ppermute | solution.py:199
  19.7 6.0 %collective-permute-done.1.bot_ref = f32[2,8,8,2048]{3,2,1,0:T(8,128)S(1)} collective-permute-done((f32[2,8,8,2048]{3,2,1,0:T(8,128)S(1)}, f32[2,8,8,2048]{3,2,1,0:T(8,128)S(1)}, u32[]{:S(2)}, u32[]{:S(2)}) %collective-permute-start.1) | collective-permute-done | bytes 1048608 | tf_op jit(solution)/shard_map/ppermute | solution.py:200
  25.7 1.0 %copy-done.3 = f32[2,8,8,2048]{3,2,1,0:T(8,128)} copy-done((f32[2,8,8,2048]{3,2,1,0:T(8,128)}, f32[2,8,8,2048]{3,2,1,0:T(8,128)S(1)}, u32[]{:S(2)}) %copy-start.3) | copy-done | bytes 1048600
  26.6 16.5 %shard_map.50 = f32[32,144,128]{2,1,0:T(8,128)} custom-call(f32[8,32,2048]{2,1,0:T(8,128)} %ph_ref.1, s32[8,32,2048]{2,1,0:T(8,128)} %wt_ref.1, f32[2,8,8,2048]{3,2,1,0:T(8,128)} %copy-done.2, f32[2,8,8,2048]{3,2,1,0:T(8,128)} %copy-done.3), custom_call_target="tpu_custom_call" | custom-call | flops 94371840 | bytes 8388608 | tf_op jit(solution)/shard_map/pallas_call | solution.py:100
  43.1 8.2 %all-to-all-start = ((f32[32,144,128]{2,1,0:T(8,128)}), f32[32,144,128]{2,1,0:T(8,128)S(1)}, u32[]{:S(2)}, u32[]{:S(2)}) async-start(f32[32,144,128]{2,1,0:T(8,128)} %shard_map.50), calls=%async_computation | async-start | bytes 4718592 | tf_op jit(solution)/shard_map/all_to_all | solution.py:202
  51.3 0.5 fusion.12
  51.9 0.1 copy.5
  52.0 8.7 %cholesky.16 = f32[95,95]{1,0:T(8,128)S(1)} custom-call(f32[95,95]{1,0:T(8,128)S(1)} %fusion.17), custom_call_target="Cholesky" | custom-call | tf_op jit(solution)/shard_map/jit(cholesky)/cholesky | solution.py:186
  60.7 0.6 compare_reduce_fusion
  61.3 0.7 fusion.13
  62.0 7.3 %custom-call.10 = f32[1,95,95]{1,2,0:T(8,128)S(1)} custom-call(f32[1,95,95]{2,1,0:T(8,128)S(1)} %fusion.13), custom_call_target="InvertDiagBlocksLowerTriangular" | custom-call | tf_op jit(solution)/shard_map/jit(_cho_solve)/triangular_solve | solution.py:187
  69.3 0.8 convert_subtract_fusion.design_in
  70.1 0.4 fusion.11
  70.5 0.9 fusion.14.pseudo_in
  71.3 1.4 %copy-done.1 = f32[32,144,128]{2,1,0:T(8,128)} copy-done((f32[32,144,128]{2,1,0:T(8,128)}, f32[32,144,128]{2,1,0:T(8,128)S(1)}, u32[]{:S(2)}) %copy-start.1) | copy-done | bytes 2359320
  72.7 7.6 %shard_map.51 = (f32[2048,96]{1,0:T(8,128)}, f32[2304,256]{1,0:T(8,128)}) custom-call(f32[4608,128]{1,0:T(8,128)} %bitcast.32, f32[95,256]{1,0:T(8,128)} %fusion.14.pseudo_in, f32[256,95]{1,0:T(8,128)} %convert_subtract_fusion.design_in), custom_call_target="tpu_custom_call" | custom-call | flops 1358954496 | bytes 5603328 | tf_op jit(solution)/shard_map/pallas_call | solution.py:150
  80.3 1.1 %fusion.20 = (f32[256,36,2]{0,2,1:T(2,128)S(1)}, f32[256,36,2]{0,2,1:T(2,128)S(1)}) fusion(f32[256,36,64]{0,2,1:T(8,128)} %bitcast.30), kind=kLoop, calls=%fused_computation.43 | loop fusion | bytes 294912 | tf_op jit(solution)/shard_map/slice | solution.py:26
  81.4 3.1 %collective-permute-start.2 = (f32[256,36,2]{0,2,1:T(2,128)S(1)}, f32[256,36,2]{0,2,1:T(2,128)S(1)}, u32[]{:S(2)}, u32[]{:S(2)}) collective-permute-start(f32[256,36,2]{0,2,1:T(2,128)S(1)} %get-tuple-element.6), channel_id=1, source_target_pairs={{0,4},{4,8},{8,12},{12,16},{16,20},{20,24},{24,28},{28,32},{32,36}... | collective-permute-start | bytes 221192 | tf_op jit(solution)/shard_map/ppermute | solution.py:25
  84.5 5.2 %collective-permute-start.3 = (f32[256,36,2]{0,2,1:T(2,128)S(1)}, f32[256,36,2]{0,2,1:T(2,128)S(1)}, u32[]{:S(2)}, u32[]{:S(2)}) collective-permute-start(f32[256,36,2]{0,2,1:T(2,128)S(1)} %get-tuple-element.7), channel_id=1, source_target_pairs={{4,0},{8,4},{12,8},{16,12},{20,16},{24,20},{28,24},{32,28},{36,32}... | collective-permute-start | bytes 221192 | tf_op jit(solution)/shard_map/ppermute | solution.py:28
  89.8 0.0 collective-permute-done.2
  89.8 1.4 %collective-permute-done.3 = f32[256,36,2]{0,2,1:T(2,128)S(1)} collective-permute-done((f32[256,36,2]{0,2,1:T(2,128)S(1)}, f32[256,36,2]{0,2,1:T(2,128)S(1)}, u32[]{:S(2)}, u32[]{:S(2)}) %collective-permute-start.3) | collective-permute-done | bytes 73760 | tf_op jit(solution)/shard_map/ppermute | solution.py:28
  91.1 1.9 %pad_maximum_fusion = f32[256,36,68]{0,2,1:T(8,128)S(1)} fusion(f32[256,36,2]{0,2,1:T(2,128)S(1)} %collective-permute-done.3, f32[256,36,64]{0,2,1:T(8,128)} %bitcast.31, f32[256,36,2]{0,2,1:T(2,128)S(1)} %collective-permute-done.2), kind=kLoop, calls=%fused_computation | loop fusion | flops 1253376 | bytes 5013504 | tf_op jit(solution)/shard_map/concatenate | solution.py:29
  93.0 0.5 fusion
  93.6 2.1 %fusion.5 = bf16[256,32,64]{0,2,1:T(8,128)(2,1)} fusion(f32[256,32,68]{0,2,1:T(8,128)S(1)} %fusion), kind=kLoop, calls=%fused_computation.11 | loop fusion | flops 4718592 | bytes 11534336 | tf_op jit(solution)/shard_map/convert_element_type | solution.py:213
  (10 shorter events, 0.1 us)
Async XLA Ops:
  0.6 1.9 %copy-start = (s32[8,32,2048]{2,1,0:T(8,128)S(1)}, s32[8,32,2048]{2,1,0:T(8,128)}, u32[]{:S(2)}) copy-start(s32[8,32,2048]{2,1,0:T(8,128)} %wt_ref.1) | copy-start | bytes 6291460
  2.7 16.9 %collective-permute-start = (f32[2,8,8,2048]{3,2,1,0:T(8,128)S(1)}, f32[2,8,8,2048]{3,2,1,0:T(8,128)S(1)}, u32[]{:S(2)}, u32[]{:S(2)}) collective-permute-start(f32[2,8,8,2048]{3,2,1,0:T(8,128)S(1)} %pad_maximum_fusion.1), channel_id=1, source_target_pairs={{0,1},{1,2},{2,3},{4,5},{5,6},{6,7},{8,9},{9,10},{10,11},{12,13},{... | collective-permute-start | bytes 3145736 | tf_op jit(solution)/shard_map/ppermute | solution.py:199
  8.0 17.6 %collective-permute-start.1 = (f32[2,8,8,2048]{3,2,1,0:T(8,128)S(1)}, f32[2,8,8,2048]{3,2,1,0:T(8,128)S(1)}, u32[]{:S(2)}, u32[]{:S(2)}) collective-permute-start(f32[2,8,8,2048]{3,2,1,0:T(8,128)S(1)} %pad_maximum_fusion.2), channel_id=1, source_target_pairs={{1,0},{2,1},{3,2},{5,4},{6,5},{7,6},{9,8},{10,9},{11,10},{13,12},{... | collective-permute-start | bytes 3145736 | tf_op jit(solution)/shard_map/ppermute | solution.py:200
  19.7 6.0 %copy-start.2 = (f32[2,8,8,2048]{3,2,1,0:T(8,128)}, f32[2,8,8,2048]{3,2,1,0:T(8,128)S(1)}, u32[]{:S(2)}) copy-start(f32[2,8,8,2048]{3,2,1,0:T(8,128)S(1)} %collective-permute-done.top_ref) | copy-start | bytes 3145732
  25.7 1.0 %copy-start.3 = (f32[2,8,8,2048]{3,2,1,0:T(8,128)}, f32[2,8,8,2048]{3,2,1,0:T(8,128)S(1)}, u32[]{:S(2)}) copy-start(f32[2,8,8,2048]{3,2,1,0:T(8,128)S(1)} %collective-permute-done.1.bot_ref) | copy-start | bytes 3145732
  43.1 8.2 %copy-start.4 = (s32[256,2]{0,1:T(2,128)S(1)}, s32[256,2]{0,1:T(2,128)}, u32[]{:S(2)}) copy-start(s32[256,2]{0,1:T(2,128)} %param.5) | copy-start | bytes 6148
  43.1 28.2 %all-to-all-start = ((f32[32,144,128]{2,1,0:T(8,128)}), f32[32,144,128]{2,1,0:T(8,128)S(1)}, u32[]{:S(2)}, u32[]{:S(2)}) async-start(f32[32,144,128]{2,1,0:T(8,128)} %shard_map.50), calls=%async_computation | async-start | bytes 4718592 | tf_op jit(solution)/shard_map/all_to_all | solution.py:202
  71.3 1.4 %copy-start.1 = (f32[32,144,128]{2,1,0:T(8,128)}, f32[32,144,128]{2,1,0:T(8,128)S(1)}, u32[]{:S(2)}) copy-start(f32[32,144,128]{2,1,0:T(8,128)S(1)} %all-to-all-done) | copy-start | bytes 7077892
  81.4 8.3 %collective-permute-start.2 = (f32[256,36,2]{0,2,1:T(2,128)S(1)}, f32[256,36,2]{0,2,1:T(2,128)S(1)}, u32[]{:S(2)}, u32[]{:S(2)}) collective-permute-start(f32[256,36,2]{0,2,1:T(2,128)S(1)} %get-tuple-element.6), channel_id=1, source_target_pairs={{0,4},{4,8},{8,12},{12,16},{16,20},{20,24},{24,28},{28,32},{32,36}... | collective-permute-start | bytes 221192 | tf_op jit(solution)/shard_map/ppermute | solution.py:25
  84.5 6.6 %collective-permute-start.3 = (f32[256,36,2]{0,2,1:T(2,128)S(1)}, f32[256,36,2]{0,2,1:T(2,128)S(1)}, u32[]{:S(2)}, u32[]{:S(2)}) collective-permute-start(f32[256,36,2]{0,2,1:T(2,128)S(1)} %get-tuple-element.7), channel_id=1, source_target_pairs={{4,0},{8,4},{12,8},{16,12},{20,16},{24,20},{28,24},{32,28},{36,32}... | collective-permute-start | bytes 221192 | tf_op jit(solution)/shard_map/ppermute | solution.py:28

commit v16 on v11

--- a/solution.py
+++ b/solution.py
@@ -121,9 +121,14 @@
     )(phase, weights, top, bottom)
 
 
-def invert_kernel(rows, x_ref, pseudo_ref, design_ref, s_ref, r_ref):
+def invert_kernel(rows, x_ref, pseudo_in, design_in, s_ref, r_ref, pseudo_ref, design_ref):
     ifg = pseudo_ref.shape[1]
     own = rows - FILTER_HALO
+    epochs = pseudo_in.shape[0]
+    pseudo_ref[...] = jnp.zeros(pseudo_ref.shape, jnp.float32)
+    design_ref[...] = jnp.zeros(design_ref.shape, jnp.float32)
+    pseudo_ref[pl.ds(0, epochs), :] = pseudo_in[...]
+    design_ref[:, pl.ds(0, epochs)] = design_in[...]
     pseudo = pseudo_ref[...]
     design = design_ref[...]
     for k in range(rows):
@@ -144,13 +149,12 @@
     ifg = pseudo.shape[1]
     epochs = pseudo.shape[0]
     wide = epochs + (-epochs) % 8
-    pseudo = jnp.pad(pseudo, ((0, wide - epochs), (0, 0)))
-    design = jnp.pad(design, ((0, 0), (0, wide - epochs)))
     whole = pl.BlockSpec(memory_space=pltpu.VMEM)
     series_t, residual_t = pl.pallas_call(
         functools.partial(invert_kernel, rows),
         in_specs=[whole, whole, whole],
         out_specs=(whole, whole),
+        scratch_shapes=[pltpu.VMEM((wide, ifg), jnp.float32), pltpu.VMEM((ifg, wide), jnp.float32)],
         out_shape=(
             jax.ShapeDtypeStruct((2 * (rows - FILTER_HALO) * 64, wide), jnp.float32),
             jax.ShapeDtypeStruct((2 * rows * 64, ifg), jnp.float32),

time: 96.4 us -> 96.4 us (level)
  local copies, waits for them, and re-layouts: 9.03 us -> 7.72 us
    pad x2 -> x0, local copies, waits for them, and re-layouts: 1.31 us -> none  [the longest x1 0.67 us: invert(): design = jnp.pad(design, ((0, 0), (0, wide - epochs)))]
where the time goes in v16:
time: 96.4 us; the launch traced here: 95.5 us
  starting transfers between devices  23.6 us (24%)
  Pallas kernels  23.5 us (24%)
  other arithmetic  23.3 us (24%)
  waiting for transfers between devices  14.9 us (15%)
  local copies, waits for them, and re-layouts  7.72 us (8%)
  matrix products  1.78 us (2%)
    pallas_call x1, Pallas kernels, unwrap(): pl.pallas_call(functools.partial(unwrap_kernel, rows_out), grid=(n // per...  17 us
    another operation x3, other arithmetic, network_maps(): factor = jnp.linalg.cholesky(normal_matrix)  9.36 us
    all_to_all x1, starting transfers between devices, on_device(): lax.all_to_all(current, 'ifg', split_axis=0, concat_axis=0, tiled=True)  8.16 us
    another operation x2, other arithmetic, network_maps(): pseudo = jax.scipy.linalg.cho_solve((factor, True), design.T)  7.94 us
    pallas_call x1, Pallas kernels, invert(): pl.pallas_call(functools.partial(invert_kernel, rows), in_specs=[whole, w...  6.47 us
    ppermute x1, waiting for transfers between devices, on_device(): top = lax.ppermute(edge_low, 'rows', forward)  6.44 us
    ppermute x1, starting transfers between devices, extended_2(): lax.ppermute(lax.slice_in_dim(block, 0, width, axis=dim), axis, backward)  6.31 us
    ppermute x1, starting transfers between devices, on_device(): top = lax.ppermute(edge_low, 'rows', forward)  5.21 us
  transfers between devices with their start and end apart: 5, of which 4 were waited for; matrix products, arithmetic and copies ran while one was open for 23% of the time, Pallas kernels for 0%

profile of v16, /device:TPU:9, one launch (start us, length us, event | category | flops | bytes accessed | tf_op | source)
XLA Modules:
  0.0 95.5 jit_solution(3383562473019861679)
XLA Ops:
  0.6 1.4 %fusion.23 = (f32[8,6,2048]{2,1,0:T(8,128)S(1)}, f32[8,6,2048]{2,1,0:T(8,128)S(1)}) fusion(f32[8,32,2048]{2,1,0:T(8,128)} %ph_ref.1), kind=kLoop, calls=%fused_computation.46 | loop fusion | bytes 1572864 | tf_op jit(solution)/shard_map/slice | solution.py:201
  2.1 0.2 copy.26
  2.3 0.2 copy-done
  2.6 0.2 fusion.10
  2.9 5.2 %collective-permute-start = (f32[2,8,6,2048]{3,1,2,0:T(8,128)S(1)}, f32[2,8,6,2048]{3,1,2,0:T(8,128)S(1)}, u32[]{:S(2)}, u32[]{:S(2)}) collective-permute-start(f32[2,8,6,2048]{3,1,2,0:T(8,128)S(1)} %pad_maximum_fusion.1), channel_id=1, source_target_pairs={{0,1},{1,2},{2,3},{4,5},{5,6},{6,7},{8,9},{9,10},{10,11},{12,13},{... | collective-permute-start | bytes 2359304 | tf_op jit(solution)/shard_map/ppermute | solution.py:202
  8.2 0.2 copy.25
  8.4 0.2 fusion.9
  8.7 1.9 %collective-permute-start.1 = (f32[2,8,6,2048]{3,1,2,0:T(8,128)S(1)}, f32[2,8,6,2048]{3,1,2,0:T(8,128)S(1)}, u32[]{:S(2)}, u32[]{:S(2)}) collective-permute-start(f32[2,8,6,2048]{3,1,2,0:T(8,128)S(1)} %pad_maximum_fusion.2), channel_id=1, source_target_pairs={{1,0},{2,1},{3,2},{5,4},{6,5},{7,6},{9,8},{10,9},{11,10},{13,12},{... | collective-permute-start | bytes 2359304 | tf_op jit(solution)/shard_map/ppermute | solution.py:203
  10.6 6.4 %collective-permute-done = f32[2,8,6,2048]{3,1,2,0:T(8,128)S(1)} collective-permute-done((f32[2,8,6,2048]{3,1,2,0:T(8,128)S(1)}, f32[2,8,6,2048]{3,1,2,0:T(8,128)S(1)}, u32[]{:S(2)}, u32[]{:S(2)}) %collective-permute-start) | collective-permute-done | bytes 786464 | tf_op jit(solution)/shard_map/ppermute | solution.py:202
  17.1 1.4 %copy.10.top_ref = f32[2,8,6,2048]{3,2,1,0:T(8,128)} copy(f32[2,8,6,2048]{3,1,2,0:T(8,128)S(1)} %collective-permute-done) | data formatting | bytes 1572864 | tf_op jit(solution)/shard_map/ppermute | solution.py:202
  18.5 5.0 %collective-permute-done.1 = f32[2,8,6,2048]{3,1,2,0:T(8,128)S(1)} collective-permute-done((f32[2,8,6,2048]{3,1,2,0:T(8,128)S(1)}, f32[2,8,6,2048]{3,1,2,0:T(8,128)S(1)}, u32[]{:S(2)}, u32[]{:S(2)}) %collective-permute-start.1) | collective-permute-done | bytes 786464 | tf_op jit(solution)/shard_map/ppermute | solution.py:203
  23.5 1.4 %copy.11.bot_ref = f32[2,8,6,2048]{3,2,1,0:T(8,128)} copy(f32[2,8,6,2048]{3,1,2,0:T(8,128)S(1)} %collective-permute-done.1) | data formatting | bytes 1572864 | tf_op jit(solution)/shard_map/ppermute | solution.py:203
  25.0 17.0 %shard_map.50 = f32[32,144,128]{2,1,0:T(8,128)} custom-call(f32[8,32,2048]{2,1,0:T(8,128)} %ph_ref.1, s32[8,32,2048]{2,1,0:T(8,128)} %wt_ref.1, f32[2,8,6,2048]{3,2,1,0:T(8,128)} %copy.10.top_ref, f32[2,8,6,2048]{3,2,1,0:T(8,128)} %copy.11.bot_ref), custom_call_target="tpu_custom_call" | custom-call | flops 94371840 | bytes 8388608 | tf_op jit(solution)/shard_map/pallas_call | solution.py:106
  42.0 8.2 %all-to-all-start = ((f32[32,144,128]{2,1,0:T(8,128)}), f32[32,144,128]{2,1,0:T(8,128)S(1)}, u32[]{:S(2)}, u32[]{:S(2)}) async-start(f32[32,144,128]{2,1,0:T(8,128)} %shard_map.50), calls=%async_computation | async-start | bytes 4718592 | tf_op jit(solution)/shard_map/all_to_all | solution.py:205
  50.2 0.5 fusion.14
  50.8 8.7 %cholesky.16 = f32[95,95]{1,0:T(8,128)S(1)} custom-call(f32[95,95]{1,0:T(8,128)S(1)} %fusion.19), custom_call_target="Cholesky" | custom-call | tf_op jit(solution)/shard_map/jit(cholesky)/cholesky | solution.py:189
  59.6 0.6 compare_reduce_fusion
  60.2 0.7 fusion.15
  60.9 7.3 %custom-call.10 = f32[1,95,95]{1,2,0:T(8,128)S(1)} custom-call(f32[1,95,95]{2,1,0:T(8,128)S(1)} %fusion.15), custom_call_target="InvertDiagBlocksLowerTriangular" | custom-call | tf_op jit(solution)/shard_map/jit(_cho_solve)/triangular_solve | solution.py:190
  68.2 0.8 convert_subtract_fusion.design_in
  69.0 0.4 fusion.13
  69.3 0.9 fusion.16.pseudo_in
  70.2 2.1 %all-to-all-done = f32[32,144,128]{2,1,0:T(8,128)S(1)} async-done(((f32[32,144,128]{2,1,0:T(8,128)}), f32[32,144,128]{2,1,0:T(8,128)S(1)}, u32[]{:S(2)}, u32[]{:S(2)}) %all-to-all-start) | async-done | bytes 2359328 | tf_op jit(solution)/shard_map/all_to_all | solution.py:205
  72.3 1.4 %copy-done.1 = f32[32,144,128]{2,1,0:T(8,128)} copy-done((f32[32,144,128]{2,1,0:T(8,128)}, f32[32,144,128]{2,1,0:T(8,128)S(1)}, u32[]{:S(2)}) %copy-start.1) | copy-done | bytes 2359320
  73.7 6.5 %shard_map.51 = (f32[2048,96]{1,0:T(8,128)}, f32[2304,256]{1,0:T(8,128)}) custom-call(f32[4608,128]{1,0:T(8,128)} %bitcast.34, f32[95,256]{1,0:T(8,128)} %fusion.16.pseudo_in, f32[256,95]{1,0:T(8,128)} %convert_subtract_fusion.design_in), custom_call_target="tpu_custom_call" | custom-call | flops 1358954496 | bytes 5603328 | tf_op jit(solution)/shard_map/pallas_call | solution.py:153
  80.2 1.1 %fusion.22 = (f32[256,36,2]{0,2,1:T(2,128)S(1)}, f32[256,36,2]{0,2,1:T(2,128)S(1)}) fusion(f32[256,36,64]{0,2,1:T(8,128)} %bitcast.32), kind=kLoop, calls=%fused_computation.45 | loop fusion | bytes 294912 | tf_op jit(solution)/shard_map/slice | solution.py:27
  81.3 2.0 %collective-permute-start.2 = (f32[256,36,2]{0,2,1:T(2,128)S(1)}, f32[256,36,2]{0,2,1:T(2,128)S(1)}, u32[]{:S(2)}, u32[]{:S(2)}) collective-permute-start(f32[256,36,2]{0,2,1:T(2,128)S(1)} %get-tuple-element.6), channel_id=1, source_target_pairs={{0,4},{4,8},{8,12},{12,16},{16,20},{20,24},{24,28},{28,32},{32,36}... | collective-permute-start | bytes 221192 | tf_op jit(solution)/shard_map/ppermute | solution.py:26
  83.2 6.3 %collective-permute-start.3 = (f32[256,36,2]{0,2,1:T(2,128)S(1)}, f32[256,36,2]{0,2,1:T(2,128)S(1)}, u32[]{:S(2)}, u32[]{:S(2)}) collective-permute-start(f32[256,36,2]{0,2,1:T(2,128)S(1)} %get-tuple-element.7), channel_id=1, source_target_pairs={{4,0},{8,4},{12,8},{16,12},{20,16},{24,20},{28,24},{32,28},{36,32}... | collective-permute-start | bytes 221192 | tf_op jit(solution)/shard_map/ppermute | solution.py:29
  89.6 1.4 %collective-permute-done.3 = f32[256,36,2]{0,2,1:T(2,128)S(1)} collective-permute-done((f32[256,36,2]{0,2,1:T(2,128)S(1)}, f32[256,36,2]{0,2,1:T(2,128)S(1)}, u32[]{:S(2)}, u32[]{:S(2)}) %collective-permute-start.3) | collective-permute-done | bytes 73760 | tf_op jit(solution)/shard_map/ppermute | solution.py:29
  91.0 1.9 %pad_maximum_fusion = f32[256,36,68]{0,2,1:T(8,128)S(1)} fusion(f32[256,36,2]{0,2,1:T(2,128)S(1)} %collective-permute-done.3, f32[256,36,64]{0,2,1:T(8,128)} %bitcast.33, f32[256,36,2]{0,2,1:T(2,128)S(1)} %collective-permute-done.2), kind=kLoop, calls=%fused_computation | loop fusion | flops 1253376 | bytes 5013504 | tf_op jit(solution)/shard_map/concatenate | solution.py:30
  92.9 0.5 fusion
  93.4 2.1 %fusion.5 = bf16[256,32,64]{0,2,1:T(8,128)(2,1)} fusion(f32[256,32,68]{0,2,1:T(8,128)S(1)} %fusion), kind=kLoop, calls=%fused_computation.11 | loop fusion | flops 4718592 | bytes 11534336 | tf_op jit(solution)/shard_map/convert_element_type | solution.py:216
  (12 shorter events, 0.4 us)
Async XLA Ops:
  0.6 1.9 %copy-start = (s32[8,32,2048]{2,1,0:T(8,128)S(1)}, s32[8,32,2048]{2,1,0:T(8,128)}, u32[]{:S(2)}) copy-start(s32[8,32,2048]{2,1,0:T(8,128)} %wt_ref.1) | copy-start | bytes 6291460
  2.9 14.1 %collective-permute-start = (f32[2,8,6,2048]{3,1,2,0:T(8,128)S(1)}, f32[2,8,6,2048]{3,1,2,0:T(8,128)S(1)}, u32[]{:S(2)}, u32[]{:S(2)}) collective-permute-start(f32[2,8,6,2048]{3,1,2,0:T(8,128)S(1)} %pad_maximum_fusion.1), channel_id=1, source_target_pairs={{0,1},{1,2},{2,3},{4,5},{5,6},{6,7},{8,9},{9,10},{10,11},{12,13},{... | collective-permute-start | bytes 2359304 | tf_op jit(solution)/shard_map/ppermute | solution.py:202
  8.7 14.8 %collective-permute-start.1 = (f32[2,8,6,2048]{3,1,2,0:T(8,128)S(1)}, f32[2,8,6,2048]{3,1,2,0:T(8,128)S(1)}, u32[]{:S(2)}, u32[]{:S(2)}) collective-permute-start(f32[2,8,6,2048]{3,1,2,0:T(8,128)S(1)} %pad_maximum_fusion.2), channel_id=1, source_target_pairs={{1,0},{2,1},{3,2},{5,4},{6,5},{7,6},{9,8},{10,9},{11,10},{13,12},{... | collective-permute-start | bytes 2359304 | tf_op jit(solution)/shard_map/ppermute | solution.py:203
  42.0 8.2 %copy-start.2 = (s32[256,2]{0,1:T(2,128)S(1)}, s32[256,2]{0,1:T(2,128)}, u32[]{:S(2)}) copy-start(s32[256,2]{0,1:T(2,128)} %param.5) | copy-start | bytes 6148
  42.0 30.3 %all-to-all-start = ((f32[32,144,128]{2,1,0:T(8,128)}), f32[32,144,128]{2,1,0:T(8,128)S(1)}, u32[]{:S(2)}, u32[]{:S(2)}) async-start(f32[32,144,128]{2,1,0:T(8,128)} %shard_map.50), calls=%async_computation | async-start | bytes 4718592 | tf_op jit(solution)/shard_map/all_to_all | solution.py:205
  72.3 1.4 %copy-start.1 = (f32[32,144,128]{2,1,0:T(8,128)}, f32[32,144,128]{2,1,0:T(8,128)S(1)}, u32[]{:S(2)}) copy-start(f32[32,144,128]{2,1,0:T(8,128)S(1)} %all-to-all-done) | copy-start | bytes 7077892
  81.3 8.3 %collective-permute-start.2 = (f32[256,36,2]{0,2,1:T(2,128)S(1)}, f32[256,36,2]{0,2,1:T(2,128)S(1)}, u32[]{:S(2)}, u32[]{:S(2)}) collective-permute-start(f32[256,36,2]{0,2,1:T(2,128)S(1)} %get-tuple-element.6), channel_id=1, source_target_pairs={{0,4},{4,8},{8,12},{12,16},{16,20},{20,24},{24,28},{28,32},{32,36}... | collective-permute-start | bytes 221192 | tf_op jit(solution)/shard_map/ppermute | solution.py:26
  83.2 7.7 %collective-permute-start.3 = (f32[256,36,2]{0,2,1:T(2,128)S(1)}, f32[256,36,2]{0,2,1:T(2,128)S(1)}, u32[]{:S(2)}, u32[]{:S(2)}) collective-permute-start(f32[256,36,2]{0,2,1:T(2,128)S(1)} %get-tuple-element.7), channel_id=1, source_target_pairs={{4,0},{8,4},{12,8},{16,12},{20,16},{24,20},{28,24},{32,28},{36,32}... | collective-permute-start | bytes 221192 | tf_op jit(solution)/shard_map/ppermute | solution.py:29
